TPU v7x, 768 devices: a whole 4x8x12 slice. The times are simulated.
768 devices in a mesh: sec: 128 (over x, z_lo, y), blk: 6 (over z_hi, core).
Axes of the slice: x: 4, y: 8, z: 12 (z_hi: 3, z_lo: 4; z = z_hi * 4 + z_lo), core: 2. Of those that a mesh axis runs over, the one named last changes fastest.
Arguments:
- slab_state: float32 [9, 8, 2048, 768], P(None, None, 'sec', 'blk'), may hold values from -6 to 6
- buoyancy: float32 [8, 2048, 768], P(None, 'sec', 'blk'), may hold values from 0.5 to 1
- lame_lambda: float32 [8, 2048, 768], P(None, 'sec', 'blk'), may hold values from 0.5 to 2
- lame_mu: float32 [8, 2048, 768], P(None, 'sec', 'blk'), may hold values from 0.3 to 1.2
- face_map: int32 [768], replicated, may hold values from 0 to 3071
- band_widths: int32 [128, 6], P('sec'), may hold values from 2 to 9
- ocean_state: float32 [3, 2048, 3072], P(None, 'sec', 'blk'), may hold values from -6 to 6
- water_depth: float32 [2048, 3072], P('sec', 'blk'), may hold values from 0.25 to 1
Outputs:
- slab_out: float32 [9, 8, 2048, 768], P(None, None, 'sec', 'blk')
- ocean_out: float32 [3, 2048, 3072], P(None, 'sec', 'blk')
Inputs may be any that keep to these rules, and one draw needn't show every extreme that they name: `face_map`: each entry is the ocean column over which that seafloor face column lies. `band_widths`: the Kajiura band width of each ocean tile in ocean cells.
All inputs are finite; a program needn't handle non-finite values.
Results may differ from a plain program's by a relative error of at most 0.00014.
Values sent between devices are 32-bit elements; how exact they have to be, the bound alone decides.
No kernel may reach another device: no remote copies, remote signals or barrier semaphores. Data moves between devices by JAX's collectives and lax.ppermute only.
A program may use at most 64 MiB of HBM per device.

v0:
```python
import math

import jax
import jax.numpy as jnp
from jax import lax
from jax.sharding import PartitionSpec as P

SLAB_STEPS = 2
WAVE_STEPS = 4


time_step = 0.25
wave_step = 0.5


def padded(x, sides, width):
    for axis, dim in sides:
        devices, length = (lax.axis_size(axis), x.shape[dim])
        up = [(i, (i + 1) % devices) for i in range(devices - 1)]
        down = [(j, i) for i, j in up]
        last = lax.slice_in_dim(x, length - width, length, axis=dim)
        leading = lax.slice_in_dim(x, 0, width, axis=dim)
        before = lax.ppermute(last, axis, up)
        after = lax.ppermute(leading, axis, down)
        x = jnp.concatenate([before, x, after], axis=dim)
    return x


def sech_kernel(distance, band_width):
    scaled = jnp.abs(distance) * (math.pi / 2.0) / band_width
    decay = jnp.exp(-scaled)
    return 2.0 * decay / (1.0 + decay * decay) / (2.0 * band_width)


def offset_slice(values, dimension, offset):
    slicer = [slice(1, -1)] * 3
    extent = values.shape[dimension]
    slicer[dimension] = slice(1 + offset, extent - 1 + offset)
    return values[tuple(slicer)]


def forward(values, dimension):
    return offset_slice(values, dimension, 1) - offset_slice(values, dimension, 0)


def backward(values, dimension):
    return offset_slice(values, dimension, 0) - offset_slice(values, dimension, -1)


def new_velocity(velocity, stress_padded, buoyancy):
    results = []
    for dimension in range(3):
        summed = forward(stress_padded[dimension], dimension)
        for across in range(3):
            if across != dimension:
                summed = summed + backward(stress_padded[6 - dimension - across], across)
        results.append(velocity[dimension] + time_step * buoyancy * summed)
    return jnp.stack(results)


def new_stress(stress, velocity_padded, lame_lambda, lame_mu):
    strain_rates = [backward(velocity_padded[dimension], dimension) for dimension in range(3)]
    dilatation = strain_rates[0] + strain_rates[1] + strain_rates[2]
    results = []
    for dimension in range(3):
        results.append(
            stress[dimension]
            + time_step * (lame_lambda * dilatation + 2.0 * lame_mu * strain_rates[dimension])
        )
    results.append(
        stress[3]
        + time_step * lame_mu * (forward(velocity_padded[1], 2) + forward(velocity_padded[2], 1))
    )
    results.append(
        stress[4]
        + time_step * lame_mu * (forward(velocity_padded[0], 2) + forward(velocity_padded[2], 0))
    )
    results.append(
        stress[5]
        + time_step * lame_mu * (forward(velocity_padded[0], 1) + forward(velocity_padded[1], 0))
    )
    return jnp.stack(results)


def pad_thickness(values):
    return jnp.pad(values, ((0, 0), (1, 1), (0, 0), (0, 0)))


def domain_mask(row_index, row_count, row_extent, col_index, col_count, col_extent, margin):
    row_cells = (
        row_index * row_extent - margin + jnp.arange(row_extent + 2 * margin, dtype=jnp.int32)
    )
    col_cells = (
        col_index * col_extent - margin + jnp.arange(col_extent + 2 * margin, dtype=jnp.int32)
    )
    row_valid = (row_cells >= 0) & (row_cells < row_count * row_extent)
    col_valid = (col_cells >= 0) & (col_cells < col_count * col_extent)
    return (row_valid[:, None] & col_valid[None, :]).astype(jnp.float32)


def on_device(
    slab_state, buoyancy, lame_lambda, lame_mu, face_map, band_widths, ocean_state, water_depth
):
    strike_dev = slab_state.shape[2]
    dip_dev = slab_state.shape[3]
    ocean_dev = ocean_state.shape[2]
    sec_index = lax.axis_index("sec")
    blk_index = lax.axis_index("blk")
    sec_count = lax.axis_size("sec")
    blk_count = lax.axis_size("blk")
    surface_rate = jnp.zeros((strike_dev, dip_dev), jnp.float32)
    velocity = slab_state[:3]
    stress = slab_state[3:]
    for stepping in range(SLAB_STEPS):
        stress_wide = padded(stress, (("sec", 2), ("blk", 3)), 1)
        velocity = new_velocity(velocity, pad_thickness(stress_wide), buoyancy)
        surface_rate = surface_rate + velocity[0, 0]
        velocity_wide = padded(velocity, (("sec", 2), ("blk", 3)), 1)
        stress = new_stress(stress, pad_thickness(velocity_wide), lame_lambda, lame_mu)
    slab_out = jnp.concatenate([velocity, stress], 0)
    uplift = time_step * surface_rate
    own_map = lax.dynamic_slice_in_dim(face_map, blk_index * dip_dev, dip_dev, 0)
    widths = jnp.repeat(band_widths[0], ocean_dev).astype(jnp.float32)
    columns = jnp.arange(ocean_dev * blk_count, dtype=jnp.int32)
    distance = (columns[:, None] - own_map[None, :]).astype(jnp.float32)
    kernel = sech_kernel(distance, widths[:, None])
    partial_value = jnp.einsum("xy,cy->xc", uplift, kernel, precision=lax.Precision.HIGHEST)
    source = lax.psum_scatter(partial_value, "blk", scatter_dimension=1, tiled=True)
    fields = jnp.stack([ocean_state[0] + source, ocean_state[1], ocean_state[2]])
    wet_mask = domain_mask(sec_index, sec_count, strike_dev, blk_index, blk_count, ocean_dev, 1)
    for stepping in range(WAVE_STEPS):
        extended_ocean = padded(fields, (("sec", 1), ("blk", 2)), 2)
        level = extended_ocean[0]
        flux_strike = extended_ocean[1]
        flux_dip = extended_ocean[2]
        surface = (
            level[1:-1, 1:-1]
            - wave_step
            * 0.5
            * (
                flux_strike[2:, 1:-1]
                - flux_strike[:-2, 1:-1]
                + (flux_dip[1:-1, 2:] - flux_dip[1:-1, :-2])
            )
        ) * wet_mask
        new_strike = flux_strike[2:-2, 2:-2] - wave_step * 0.5 * water_depth * (
            surface[2:, 1:-1] - surface[:-2, 1:-1]
        )
        new_dip = flux_dip[2:-2, 2:-2] - wave_step * 0.5 * water_depth * (
            surface[1:-1, 2:] - surface[1:-1, :-2]
        )
        fields = jnp.stack([surface[1:-1, 1:-1], new_strike, new_dip])
    return (slab_out, fields)


def solution(mesh):
    in_specs = (
        P(None, None, "sec", "blk"),
        P(None, "sec", "blk"),
        P(None, "sec", "blk"),
        P(None, "sec", "blk"),
        P(),
        P("sec", None),
        P(None, "sec", "blk"),
        P("sec", "blk"),
    )
    out_specs = (P(None, None, "sec", "blk"), P(None, "sec", "blk"))
    return jax.shard_map(
        on_device, mesh=mesh, in_specs=in_specs, out_specs=out_specs, check_vma=False
    )
```

profile of v0, /device:TPU:7, one launch (start us, length us, event | category | flops | bytes accessed | tf_op | source)
XLA Modules:
  0.0 251.0 jit_solution(13928589291523046032)
XLA Ops:
  7.2 1.1 fusion.111
  8.3 3.2 %collective-permute-start = (f32[6,8,1,128]{3,1,2,0:T(8,128)S(1)}, f32[6,8,1,128]{3,1,2,0:T(8,128)S(1)}, u32[]{:S(2)}, u32[]{:S(2)}) collective-permute-start(f32[6,8,1,128]{3,1,2,0:T(8,128)S(1)} %bitcast.182), channel_id=1, source_target_pairs={{0,6},{6,12},{12,18},{18,24},{24,30},{30,36},{36,42},{42,48},{48,5... | collective-permute-start | bytes 73736 | tf_op jit(solution)/shard_map/ppermute | solution.py:23
  11.5 9.5 %collective-permute-start.1 = (f32[6,8,1,128]{3,1,2,0:T(8,128)S(1)}, f32[6,8,1,128]{3,1,2,0:T(8,128)S(1)}, u32[]{:S(2)}, u32[]{:S(2)}) collective-permute-start(f32[6,8,1,128]{3,1,2,0:T(8,128)S(1)} %bitcast.181), channel_id=1, source_target_pairs={{6,0},{12,6},{18,12},{24,18},{30,24},{36,30},{42,36},{48,42},{54,4... | collective-permute-start | bytes 73736 | tf_op jit(solution)/shard_map/ppermute | solution.py:24
  21.0 1.0 slice.586
  22.8 11.5 %collective-permute-start.2 = (f32[6,8,18,1]{2,1,3,0:T(8,128)S(1)}, f32[6,8,18,1]{2,1,3,0:T(8,128)S(1)}, u32[]{:S(2)}, u32[]{:S(2)}) collective-permute-start(f32[6,8,18,1]{2,1,3,0:T(8,128)S(1)} %copy.121), channel_id=1, source_target_pairs={{0,1},{1,2},{2,3},{3,4},{4,5},{6,7},{7,8},{8,9},{9,10},{10,11},{12... | collective-permute-start | bytes 10376 | tf_op jit(solution)/shard_map/ppermute | solution.py:23
  34.7 1.9 collective-permute-start.3
  37.1 6.7 %collective-permute-done.3 = f32[6,8,18,1]{2,1,3,0:T(8,128)S(1)} collective-permute-done((f32[6,8,18,1]{2,1,3,0:T(8,128)S(1)}, f32[6,8,18,1]{2,1,3,0:T(8,128)S(1)}, u32[]{:S(2)}, u32[]{:S(2)}) %collective-permute-start.3) | collective-permute-done | bytes 3488 | tf_op jit(solution)/shard_map/ppermute | solution.py:24
  46.2 1.9 collective-permute-start.4
  48.1 8.8 %collective-permute-start.5 = (f32[3,8,1,128]{3,1,2,0:T(8,128)S(1)}, f32[3,8,1,128]{3,1,2,0:T(8,128)S(1)}, u32[]{:S(2)}, u32[]{:S(2)}) collective-permute-start(f32[3,8,1,128]{3,1,2,0:T(8,128)S(1)} %get-tuple-element.69), channel_id=1, source_target_pairs={{6,0},{12,6},{18,12},{24,18},{30,24},{36,30},{42,36},{48,42},{54,4... | collective-permute-start | bytes 36872 | tf_op jit(solution)/shard_map/ppermute | solution.py:24
  57.9 2.9 %collective-permute-start.6 = (f32[3,8,18,1]{3,1,2,0:T(8,128)S(1)}, f32[3,8,18,1]{3,1,2,0:T(8,128)S(1)}, u32[]{:S(2)}, u32[]{:S(2)}) collective-permute-start(f32[3,8,18,1]{3,1,2,0:T(8,128)S(1)} %get-tuple-element.64), channel_id=1, source_target_pairs={{0,1},{1,2},{2,3},{3,4},{4,5},{6,7},{7,8},{8,9},{9,10},{10,11},{12... | collective-permute-start | bytes 5192 | tf_op jit(solution)/shard_map/ppermute | solution.py:23
  60.8 1.9 collective-permute-start.7
  62.7 0.9 collective-permute-done.6
  63.6 9.8 %collective-permute-done.7 = f32[3,8,18,1]{3,1,2,0:T(8,128)S(1)} collective-permute-done((f32[3,8,18,1]{3,1,2,0:T(8,128)S(1)}, f32[3,8,18,1]{3,1,2,0:T(8,128)S(1)}, u32[]{:S(2)}, u32[]{:S(2)}) %collective-permute-start.7) | collective-permute-done | bytes 1760 | tf_op jit(solution)/shard_map/ppermute | solution.py:24
  74.8 1.9 collective-permute-start.8
  76.8 10.5 %collective-permute-start.9 = (f32[6,8,1,128]{3,1,2,0:T(8,128)S(1)}, f32[6,8,1,128]{3,1,2,0:T(8,128)S(1)}, u32[]{:S(2)}, u32[]{:S(2)}) collective-permute-start(f32[6,8,1,128]{3,1,2,0:T(8,128)S(1)} %get-tuple-element.55), channel_id=1, source_target_pairs={{6,0},{12,6},{18,12},{24,18},{30,24},{36,30},{42,36},{48,42},{54,4... | collective-permute-start | bytes 73736 | tf_op jit(solution)/shard_map/ppermute | solution.py:24
  87.3 0.9 collective-permute-done.9
  88.8 2.6 %collective-permute-start.10 = (f32[6,8,18,1]{2,1,3,0:T(8,128)S(1)}, f32[6,8,18,1]{2,1,3,0:T(8,128)S(1)}, u32[]{:S(2)}, u32[]{:S(2)}) collective-permute-start(f32[6,8,18,1]{2,1,3,0:T(8,128)S(1)} %copy.103), channel_id=1, source_target_pairs={{0,1},{1,2},{2,3},{3,4},{4,5},{6,7},{7,8},{8,9},{9,10},{10,11},{12... | collective-permute-start | bytes 10376 | tf_op jit(solution)/shard_map/ppermute | solution.py:23
  91.8 1.9 collective-permute-start.11
  95.0 5.9 %collective-permute-done.11 = f32[6,8,18,1]{2,1,3,0:T(8,128)S(1)} collective-permute-done((f32[6,8,18,1]{2,1,3,0:T(8,128)S(1)}, f32[6,8,18,1]{2,1,3,0:T(8,128)S(1)}, u32[]{:S(2)}, u32[]{:S(2)}) %collective-permute-start.11) | collective-permute-done | bytes 3488 | tf_op jit(solution)/shard_map/ppermute | solution.py:24
  101.3 0.9 select_maximum_fusion
  102.7 3.1 %fusion.1 = f32[16,3072]{1,0:T(8,128)} fusion(f32[16,128]{1,0:T(8,128)S(1)} %bitcast.183, f32[3072]{0:T(1024)S(1)} %broadcast_multiply_fusion, f32[3072]{0:T(1024)S(1)} %convert_element_type.30, s32[128]{0:T(128)S(1)} %dynamic_slice.3), kind=kOutput, calls=%fused_computation.10 | convolution fusion | flops 79822848 | bytes 229888 | tf_op jit(solution)/shard_map/xy,cy->xc/dot_general | solution.py:127
  106.0 1.9 collective-permute-start.12
  108.0 8.8 %collective-permute-start.13 = (f32[3,8,1,128]{3,1,2,0:T(8,128)S(1)}, f32[3,8,1,128]{3,1,2,0:T(8,128)S(1)}, u32[]{:S(2)}, u32[]{:S(2)}) collective-permute-start(f32[3,8,1,128]{3,1,2,0:T(8,128)S(1)} %get-tuple-element.67), channel_id=1, source_target_pairs={{6,0},{12,6},{18,12},{24,18},{30,24},{36,30},{42,36},{48,42},{54,4... | collective-permute-start | bytes 36872 | tf_op jit(solution)/shard_map/ppermute | solution.py:24
  117.7 2.8 %collective-permute-start.14 = (f32[3,8,18,1]{3,1,2,0:T(8,128)S(1)}, f32[3,8,18,1]{3,1,2,0:T(8,128)S(1)}, u32[]{:S(2)}, u32[]{:S(2)}) collective-permute-start(f32[3,8,18,1]{3,1,2,0:T(8,128)S(1)} %get-tuple-element.62), channel_id=1, source_target_pairs={{0,1},{1,2},{2,3},{3,4},{4,5},{6,7},{7,8},{8,9},{9,10},{10,11},{12... | collective-permute-start | bytes 5192 | tf_op jit(solution)/shard_map/ppermute | solution.py:23
  120.5 1.9 collective-permute-start.15
  122.4 1.0 collective-permute-done.14
  123.4 8.9 %collective-permute-done.15 = f32[3,8,18,1]{3,1,2,0:T(8,128)S(1)} collective-permute-done((f32[3,8,18,1]{3,1,2,0:T(8,128)S(1)}, f32[3,8,18,1]{3,1,2,0:T(8,128)S(1)}, u32[]{:S(2)}, u32[]{:S(2)}) %collective-permute-start.15) | collective-permute-done | bytes 1760 | tf_op jit(solution)/shard_map/ppermute | solution.py:24
  132.8 13.7 %reduce-scatter.2.cloned.1.call-done = f32[16,512]{1,0:T(8,128)} async-done(((f32[16,3072]{1,0:T(8,128)}), f32[16,512]{1,0:T(8,128)}) %reduce-scatter.2.cloned.1.call-update) | async-done | bytes 32784 | tf_op jit(solution)/shard_map/reduce_scatter | solution.py:128
  147.3 3.0 %collective-permute-start.16 = (f32[3,2,512]{2,1,0:T(2,128)S(1)}, f32[3,2,512]{2,1,0:T(2,128)S(1)}, u32[]{:S(2)}, u32[]{:S(2)}) collective-permute-start(f32[3,2,512]{2,1,0:T(2,128)S(1)} %get-tuple-element.97), channel_id=1, source_target_pairs={{0,6},{6,12},{12,18},{18,24},{24,30},{30,36},{36,42},{42,48},{48,5... | collective-permute-start | bytes 36872 | tf_op jit(solution)/shard_map/ppermute | solution.py:23
  150.3 7.5 %collective-permute-start.17 = (f32[3,2,512]{2,1,0:T(2,128)S(1)}, f32[3,2,512]{2,1,0:T(2,128)S(1)}, u32[]{:S(2)}, u32[]{:S(2)}) collective-permute-start(f32[3,2,512]{2,1,0:T(2,128)S(1)} %get-tuple-element.98), channel_id=1, source_target_pairs={{6,0},{12,6},{18,12},{24,18},{30,24},{36,30},{42,36},{48,42},{54,4... | collective-permute-start | bytes 36872 | tf_op jit(solution)/shard_map/ppermute | solution.py:24
  158.7 2.9 %collective-permute-start.18 = (f32[3,20,2]{2,1,0:T(8,128)S(1)}, f32[3,20,2]{2,1,0:T(8,128)S(1)}, u32[]{:S(2)}, u32[]{:S(2)}) collective-permute-start(f32[3,20,2]{2,1,0:T(8,128)S(1)} %get-tuple-element.89), channel_id=1, source_target_pairs={{0,1},{1,2},{2,3},{3,4},{4,5},{6,7},{7,8},{8,9},{9,10},{10,11},{12... | collective-permute-start | bytes 1448 | tf_op jit(solution)/shard_map/ppermute | solution.py:23
  161.6 1.9 collective-permute-start.19
  163.8 7.0 %collective-permute-done.19 = f32[3,20,2]{2,1,0:T(8,128)S(1)} collective-permute-done((f32[3,20,2]{2,1,0:T(8,128)S(1)}, f32[3,20,2]{2,1,0:T(8,128)S(1)}, u32[]{:S(2)}, u32[]{:S(2)}) %collective-permute-start.19) | collective-permute-done | bytes 512 | tf_op jit(solution)/shard_map/ppermute | solution.py:24
  171.3 1.9 collective-permute-start.20
  173.2 8.7 %collective-permute-start.21 = (f32[3,2,512]{2,1,0:T(2,128)S(1)}, f32[3,2,512]{2,1,0:T(2,128)S(1)}, u32[]{:S(2)}, u32[]{:S(2)}) collective-permute-start(f32[3,2,512]{2,1,0:T(2,128)S(1)} %get-tuple-element.96), channel_id=1, source_target_pairs={{6,0},{12,6},{18,12},{24,18},{30,24},{36,30},{42,36},{48,42},{54,4... | collective-permute-start | bytes 36872 | tf_op jit(solution)/shard_map/ppermute | solution.py:24
  182.8 2.8 %collective-permute-start.22 = (f32[3,20,2]{2,1,0:T(8,128)S(1)}, f32[3,20,2]{2,1,0:T(8,128)S(1)}, u32[]{:S(2)}, u32[]{:S(2)}) collective-permute-start(f32[3,20,2]{2,1,0:T(8,128)S(1)} %get-tuple-element.87), channel_id=1, source_target_pairs={{0,1},{1,2},{2,3},{3,4},{4,5},{6,7},{7,8},{8,9},{9,10},{10,11},{12... | collective-permute-start | bytes 1448 | tf_op jit(solution)/shard_map/ppermute | solution.py:23
  185.6 1.9 collective-permute-start.23
  187.6 7.2 %collective-permute-done.23 = f32[3,20,2]{2,1,0:T(8,128)S(1)} collective-permute-done((f32[3,20,2]{2,1,0:T(8,128)S(1)}, f32[3,20,2]{2,1,0:T(8,128)S(1)}, u32[]{:S(2)}, u32[]{:S(2)}) %collective-permute-start.23) | collective-permute-done | bytes 512 | tf_op jit(solution)/shard_map/ppermute | solution.py:24
  195.3 1.9 collective-permute-start.24
  197.2 9.1 %collective-permute-start.25 = (f32[3,2,512]{2,1,0:T(2,128)S(1)}, f32[3,2,512]{2,1,0:T(2,128)S(1)}, u32[]{:S(2)}, u32[]{:S(2)}) collective-permute-start(f32[3,2,512]{2,1,0:T(2,128)S(1)} %get-tuple-element.94), channel_id=1, source_target_pairs={{6,0},{12,6},{18,12},{24,18},{30,24},{36,30},{42,36},{48,42},{54,4... | collective-permute-start | bytes 36872 | tf_op jit(solution)/shard_map/ppermute | solution.py:24
  207.2 2.6 %collective-permute-start.26 = (f32[3,20,2]{2,1,0:T(8,128)S(1)}, f32[3,20,2]{2,1,0:T(8,128)S(1)}, u32[]{:S(2)}, u32[]{:S(2)}) collective-permute-start(f32[3,20,2]{2,1,0:T(8,128)S(1)} %get-tuple-element.85), channel_id=1, source_target_pairs={{0,1},{1,2},{2,3},{3,4},{4,5},{6,7},{7,8},{8,9},{9,10},{10,11},{12... | collective-permute-start | bytes 1448 | tf_op jit(solution)/shard_map/ppermute | solution.py:23
  209.9 1.9 collective-permute-start.27
  211.8 7.3 %collective-permute-done.27 = f32[3,20,2]{2,1,0:T(8,128)S(1)} collective-permute-done((f32[3,20,2]{2,1,0:T(8,128)S(1)}, f32[3,20,2]{2,1,0:T(8,128)S(1)}, u32[]{:S(2)}, u32[]{:S(2)}) %collective-permute-start.27) | collective-permute-done | bytes 512 | tf_op jit(solution)/shard_map/ppermute | solution.py:24
  219.6 1.9 collective-permute-start.28
  221.5 8.7 %collective-permute-start.29 = (f32[3,2,512]{2,1,0:T(2,128)S(1)}, f32[3,2,512]{2,1,0:T(2,128)S(1)}, u32[]{:S(2)}, u32[]{:S(2)}) collective-permute-start(f32[3,2,512]{2,1,0:T(2,128)S(1)} %get-tuple-element.92), channel_id=1, source_target_pairs={{6,0},{12,6},{18,12},{24,18},{30,24},{36,30},{42,36},{48,42},{54,4... | collective-permute-start | bytes 36872 | tf_op jit(solution)/shard_map/ppermute | solution.py:24
  231.1 2.8 %collective-permute-start.30 = (f32[3,20,2]{2,1,0:T(8,128)S(1)}, f32[3,20,2]{2,1,0:T(8,128)S(1)}, u32[]{:S(2)}, u32[]{:S(2)}) collective-permute-start(f32[3,20,2]{2,1,0:T(8,128)S(1)} %get-tuple-element.83), channel_id=1, source_target_pairs={{0,1},{1,2},{2,3},{3,4},{4,5},{6,7},{7,8},{8,9},{9,10},{10,11},{12... | collective-permute-start | bytes 1448 | tf_op jit(solution)/shard_map/ppermute | solution.py:23
  233.8 1.9 collective-permute-start.31
  235.8 7.2 %collective-permute-done.31 = f32[3,20,2]{2,1,0:T(8,128)S(1)} collective-permute-done((f32[3,20,2]{2,1,0:T(8,128)S(1)}, f32[3,20,2]{2,1,0:T(8,128)S(1)}, u32[]{:S(2)}, u32[]{:S(2)}) %collective-permute-start.31) | collective-permute-done | bytes 512 | tf_op jit(solution)/shard_map/ppermute | solution.py:24
  (124 shorter events, 18.0 us)
Async XLA Ops:
  7.2 139.4 %reduce-scatter.2.cloned.1.call-start = ((), (), s32[]{:S(2)}) async-start(), calls=%async_computation.1 | async-start | bytes 229376 | tf_op jit(solution)/shard_map/reduce_scatter | solution.py:128
  8.3 13.8 %collective-permute-start = (f32[6,8,1,128]{3,1,2,0:T(8,128)S(1)}, f32[6,8,1,128]{3,1,2,0:T(8,128)S(1)}, u32[]{:S(2)}, u32[]{:S(2)}) collective-permute-start(f32[6,8,1,128]{3,1,2,0:T(8,128)S(1)} %bitcast.182), channel_id=1, source_target_pairs={{0,6},{6,12},{12,18},{18,24},{24,30},{30,36},{36,42},{42,48},{48,5... | collective-permute-start | bytes 73736 | tf_op jit(solution)/shard_map/ppermute | solution.py:23
  11.5 10.7 %collective-permute-start.1 = (f32[6,8,1,128]{3,1,2,0:T(8,128)S(1)}, f32[6,8,1,128]{3,1,2,0:T(8,128)S(1)}, u32[]{:S(2)}, u32[]{:S(2)}) collective-permute-start(f32[6,8,1,128]{3,1,2,0:T(8,128)S(1)} %bitcast.181), channel_id=1, source_target_pairs={{6,0},{12,6},{18,12},{24,18},{30,24},{36,30},{42,36},{48,42},{54,4... | collective-permute-start | bytes 73736 | tf_op jit(solution)/shard_map/ppermute | solution.py:24
  22.0 14.5 %copy-start.1 = (f32[9,8,16,128]{3,2,1,0:T(8,128)S(1)}, f32[9,8,16,128]{3,2,1,0:T(8,128)}, u32[]{:S(2)}) copy-start(f32[9,8,16,128]{3,2,1,0:T(8,128)} %param.8) | copy-start | bytes 1769476
  22.8 13.8 %collective-permute-start.2 = (f32[6,8,18,1]{2,1,3,0:T(8,128)S(1)}, f32[6,8,18,1]{2,1,3,0:T(8,128)S(1)}, u32[]{:S(2)}, u32[]{:S(2)}) collective-permute-start(f32[6,8,18,1]{2,1,3,0:T(8,128)S(1)} %copy.121), channel_id=1, source_target_pairs={{0,1},{1,2},{2,3},{3,4},{4,5},{6,7},{7,8},{8,9},{9,10},{10,11},{12... | collective-permute-start | bytes 10376 | tf_op jit(solution)/shard_map/ppermute | solution.py:23
  34.7 9.0 %collective-permute-start.3 = (f32[6,8,18,1]{2,1,3,0:T(8,128)S(1)}, f32[6,8,18,1]{2,1,3,0:T(8,128)S(1)}, u32[]{:S(2)}, u32[]{:S(2)}) collective-permute-start(f32[6,8,18,1]{2,1,3,0:T(8,128)S(1)} %copy.122), channel_id=1, source_target_pairs={{1,0},{2,1},{3,2},{4,3},{5,4},{7,6},{8,7},{9,8},{10,9},{11,10},{13... | collective-permute-start | bytes 10376 | tf_op jit(solution)/shard_map/ppermute | solution.py:24
  44.9 0.8 copy-start.2
  45.2 11.8 %copy-start.7 = (s32[1,6]{1,0:T(1,128)S(1)}, s32[1,6]{1,0:T(1,128)}, u32[]{:S(2)}) copy-start(s32[1,6]{1,0:T(1,128)} %param.13) | copy-start | bytes 76
  46.2 10.8 %collective-permute-start.4 = (f32[3,8,1,128]{3,1,2,0:T(8,128)S(1)}, f32[3,8,1,128]{3,1,2,0:T(8,128)S(1)}, u32[]{:S(2)}, u32[]{:S(2)}) collective-permute-start(f32[3,8,1,128]{3,1,2,0:T(8,128)S(1)} %get-tuple-element.68), channel_id=1, source_target_pairs={{0,6},{6,12},{12,18},{18,24},{24,30},{30,36},{36,42},{42,48},{48,5... | collective-permute-start | bytes 36872 | tf_op jit(solution)/shard_map/ppermute | solution.py:23
  48.1 9.6 %collective-permute-start.5 = (f32[3,8,1,128]{3,1,2,0:T(8,128)S(1)}, f32[3,8,1,128]{3,1,2,0:T(8,128)S(1)}, u32[]{:S(2)}, u32[]{:S(2)}) collective-permute-start(f32[3,8,1,128]{3,1,2,0:T(8,128)S(1)} %get-tuple-element.69), channel_id=1, source_target_pairs={{6,0},{12,6},{18,12},{24,18},{30,24},{36,30},{42,36},{48,42},{54,4... | collective-permute-start | bytes 36872 | tf_op jit(solution)/shard_map/ppermute | solution.py:24
  57.9 16.1 %copy-start = (f32[8,16,128]{2,1,0:T(8,128)S(1)}, f32[8,16,128]{2,1,0:T(8,128)}, u32[]{:S(2)}) copy-start(f32[8,16,128]{2,1,0:T(8,128)} %param.11) | copy-start | bytes 196612
  57.9 16.1 %copy-start.4 = (f32[8,16,128]{2,1,0:T(8,128)S(1)}, f32[8,16,128]{2,1,0:T(8,128)}, u32[]{:S(2)}) copy-start(f32[8,16,128]{2,1,0:T(8,128)} %param.10) | copy-start | bytes 196612
  57.9 5.7 %collective-permute-start.6 = (f32[3,8,18,1]{3,1,2,0:T(8,128)S(1)}, f32[3,8,18,1]{3,1,2,0:T(8,128)S(1)}, u32[]{:S(2)}, u32[]{:S(2)}) collective-permute-start(f32[3,8,18,1]{3,1,2,0:T(8,128)S(1)} %get-tuple-element.64), channel_id=1, source_target_pairs={{0,1},{1,2},{2,3},{3,4},{4,5},{6,7},{7,8},{8,9},{9,10},{10,11},{12... | collective-permute-start | bytes 5192 | tf_op jit(solution)/shard_map/ppermute | solution.py:23
  60.8 12.7 %collective-permute-start.7 = (f32[3,8,18,1]{3,1,2,0:T(8,128)S(1)}, f32[3,8,18,1]{3,1,2,0:T(8,128)S(1)}, u32[]{:S(2)}, u32[]{:S(2)}) collective-permute-start(f32[3,8,18,1]{3,1,2,0:T(8,128)S(1)} %get-tuple-element.65), channel_id=1, source_target_pairs={{1,0},{2,1},{3,2},{4,3},{5,4},{7,6},{8,7},{9,8},{10,9},{11,10},{13... | collective-permute-start | bytes 5192 | tf_op jit(solution)/shard_map/ppermute | solution.py:24
  74.8 12.5 %collective-permute-start.8 = (f32[6,8,1,128]{3,1,2,0:T(8,128)S(1)}, f32[6,8,1,128]{3,1,2,0:T(8,128)S(1)}, u32[]{:S(2)}, u32[]{:S(2)}) collective-permute-start(f32[6,8,1,128]{3,1,2,0:T(8,128)S(1)} %get-tuple-element.54), channel_id=1, source_target_pairs={{0,6},{6,12},{12,18},{18,24},{24,30},{30,36},{36,42},{42,48},{48,5... | collective-permute-start | bytes 73736 | tf_op jit(solution)/shard_map/ppermute | solution.py:23
  76.8 11.5 %collective-permute-start.9 = (f32[6,8,1,128]{3,1,2,0:T(8,128)S(1)}, f32[6,8,1,128]{3,1,2,0:T(8,128)S(1)}, u32[]{:S(2)}, u32[]{:S(2)}) collective-permute-start(f32[6,8,1,128]{3,1,2,0:T(8,128)S(1)} %get-tuple-element.55), channel_id=1, source_target_pairs={{6,0},{12,6},{18,12},{24,18},{30,24},{36,30},{42,36},{48,42},{54,4... | collective-permute-start | bytes 73736 | tf_op jit(solution)/shard_map/ppermute | solution.py:24
  87.3 6.5 %copy-start.5 = (f32[3,16,512]{2,1,0:T(8,128)S(1)}, f32[3,16,512]{2,1,0:T(8,128)}, u32[]{:S(2)}) copy-start(f32[3,16,512]{2,1,0:T(8,128)} %param.14) | copy-start | bytes 294916
  88.8 5.7 %collective-permute-start.10 = (f32[6,8,18,1]{2,1,3,0:T(8,128)S(1)}, f32[6,8,18,1]{2,1,3,0:T(8,128)S(1)}, u32[]{:S(2)}, u32[]{:S(2)}) collective-permute-start(f32[6,8,18,1]{2,1,3,0:T(8,128)S(1)} %copy.103), channel_id=1, source_target_pairs={{0,1},{1,2},{2,3},{3,4},{4,5},{6,7},{7,8},{8,9},{9,10},{10,11},{12... | collective-permute-start | bytes 10376 | tf_op jit(solution)/shard_map/ppermute | solution.py:23
  91.8 9.0 %collective-permute-start.11 = (f32[6,8,18,1]{2,1,3,0:T(8,128)S(1)}, f32[6,8,18,1]{2,1,3,0:T(8,128)S(1)}, u32[]{:S(2)}, u32[]{:S(2)}) collective-permute-start(f32[6,8,18,1]{2,1,3,0:T(8,128)S(1)} %copy.104), channel_id=1, source_target_pairs={{1,0},{2,1},{3,2},{4,3},{5,4},{7,6},{8,7},{9,8},{10,9},{11,10},{13... | collective-permute-start | bytes 10376 | tf_op jit(solution)/shard_map/ppermute | solution.py:24
  106.0 10.7 %collective-permute-start.12 = (f32[3,8,1,128]{3,1,2,0:T(8,128)S(1)}, f32[3,8,1,128]{3,1,2,0:T(8,128)S(1)}, u32[]{:S(2)}, u32[]{:S(2)}) collective-permute-start(f32[3,8,1,128]{3,1,2,0:T(8,128)S(1)} %get-tuple-element.66), channel_id=1, source_target_pairs={{0,6},{6,12},{12,18},{18,24},{24,30},{30,36},{36,42},{42,48},{48,5... | collective-permute-start | bytes 36872 | tf_op jit(solution)/shard_map/ppermute | solution.py:23
  108.0 9.6 %collective-permute-start.13 = (f32[3,8,1,128]{3,1,2,0:T(8,128)S(1)}, f32[3,8,1,128]{3,1,2,0:T(8,128)S(1)}, u32[]{:S(2)}, u32[]{:S(2)}) collective-permute-start(f32[3,8,1,128]{3,1,2,0:T(8,128)S(1)} %get-tuple-element.67), channel_id=1, source_target_pairs={{6,0},{12,6},{18,12},{24,18},{30,24},{36,30},{42,36},{48,42},{54,4... | collective-permute-start | bytes 36872 | tf_op jit(solution)/shard_map/ppermute | solution.py:24
  117.7 5.7 %collective-permute-start.14 = (f32[3,8,18,1]{3,1,2,0:T(8,128)S(1)}, f32[3,8,18,1]{3,1,2,0:T(8,128)S(1)}, u32[]{:S(2)}, u32[]{:S(2)}) collective-permute-start(f32[3,8,18,1]{3,1,2,0:T(8,128)S(1)} %get-tuple-element.62), channel_id=1, source_target_pairs={{0,1},{1,2},{2,3},{3,4},{4,5},{6,7},{7,8},{8,9},{9,10},{10,11},{12... | collective-permute-start | bytes 5192 | tf_op jit(solution)/shard_map/ppermute | solution.py:23
  120.5 11.8 %collective-permute-start.15 = (f32[3,8,18,1]{3,1,2,0:T(8,128)S(1)}, f32[3,8,18,1]{3,1,2,0:T(8,128)S(1)}, u32[]{:S(2)}, u32[]{:S(2)}) collective-permute-start(f32[3,8,18,1]{3,1,2,0:T(8,128)S(1)} %get-tuple-element.63), channel_id=1, source_target_pairs={{1,0},{2,1},{3,2},{4,3},{5,4},{7,6},{8,7},{9,8},{10,9},{11,10},{13... | collective-permute-start | bytes 5192 | tf_op jit(solution)/shard_map/ppermute | solution.py:24
  147.3 10.8 %collective-permute-start.16 = (f32[3,2,512]{2,1,0:T(2,128)S(1)}, f32[3,2,512]{2,1,0:T(2,128)S(1)}, u32[]{:S(2)}, u32[]{:S(2)}) collective-permute-start(f32[3,2,512]{2,1,0:T(2,128)S(1)} %get-tuple-element.97), channel_id=1, source_target_pairs={{0,6},{6,12},{12,18},{18,24},{24,30},{30,36},{36,42},{42,48},{48,5... | collective-permute-start | bytes 36872 | tf_op jit(solution)/shard_map/ppermute | solution.py:23
  150.3 8.3 %collective-permute-start.17 = (f32[3,2,512]{2,1,0:T(2,128)S(1)}, f32[3,2,512]{2,1,0:T(2,128)S(1)}, u32[]{:S(2)}, u32[]{:S(2)}) collective-permute-start(f32[3,2,512]{2,1,0:T(2,128)S(1)} %get-tuple-element.98), channel_id=1, source_target_pairs={{6,0},{12,6},{18,12},{24,18},{30,24},{36,30},{42,36},{48,42},{54,4... | collective-permute-start | bytes 36872 | tf_op jit(solution)/shard_map/ppermute | solution.py:24
  157.8 13.3 %copy-start.3 = (f32[16,512]{1,0:T(8,128)S(1)}, f32[16,512]{1,0:T(8,128)}, u32[]{:S(2)}) copy-start(f32[16,512]{1,0:T(8,128)} %param.15) | copy-start | bytes 98308
  158.7 5.0 %collective-permute-start.18 = (f32[3,20,2]{2,1,0:T(8,128)S(1)}, f32[3,20,2]{2,1,0:T(8,128)S(1)}, u32[]{:S(2)}, u32[]{:S(2)}) collective-permute-start(f32[3,20,2]{2,1,0:T(8,128)S(1)} %get-tuple-element.89), channel_id=1, source_target_pairs={{0,1},{1,2},{2,3},{3,4},{4,5},{6,7},{7,8},{8,9},{9,10},{10,11},{12... | collective-permute-start | bytes 1448 | tf_op jit(solution)/shard_map/ppermute | solution.py:23
  161.6 9.2 %collective-permute-start.19 = (f32[3,20,2]{2,1,0:T(8,128)S(1)}, f32[3,20,2]{2,1,0:T(8,128)S(1)}, u32[]{:S(2)}, u32[]{:S(2)}) collective-permute-start(f32[3,20,2]{2,1,0:T(8,128)S(1)} %get-tuple-element.90), channel_id=1, source_target_pairs={{1,0},{2,1},{3,2},{4,3},{5,4},{7,6},{8,7},{9,8},{10,9},{11,10},{13... | collective-permute-start | bytes 1448 | tf_op jit(solution)/shard_map/ppermute | solution.py:24
  171.3 10.7 %collective-permute-start.20 = (f32[3,2,512]{2,1,0:T(2,128)S(1)}, f32[3,2,512]{2,1,0:T(2,128)S(1)}, u32[]{:S(2)}, u32[]{:S(2)}) collective-permute-start(f32[3,2,512]{2,1,0:T(2,128)S(1)} %get-tuple-element.95), channel_id=1, source_target_pairs={{0,6},{6,12},{12,18},{18,24},{24,30},{30,36},{36,42},{42,48},{48,5... | collective-permute-start | bytes 36872 | tf_op jit(solution)/shard_map/ppermute | solution.py:23
  173.2 9.5 %collective-permute-start.21 = (f32[3,2,512]{2,1,0:T(2,128)S(1)}, f32[3,2,512]{2,1,0:T(2,128)S(1)}, u32[]{:S(2)}, u32[]{:S(2)}) collective-permute-start(f32[3,2,512]{2,1,0:T(2,128)S(1)} %get-tuple-element.96), channel_id=1, source_target_pairs={{6,0},{12,6},{18,12},{24,18},{30,24},{36,30},{42,36},{48,42},{54,4... | collective-permute-start | bytes 36872 | tf_op jit(solution)/shard_map/ppermute | solution.py:24
  182.8 4.7 %collective-permute-start.22 = (f32[3,20,2]{2,1,0:T(8,128)S(1)}, f32[3,20,2]{2,1,0:T(8,128)S(1)}, u32[]{:S(2)}, u32[]{:S(2)}) collective-permute-start(f32[3,20,2]{2,1,0:T(8,128)S(1)} %get-tuple-element.87), channel_id=1, source_target_pairs={{0,1},{1,2},{2,3},{3,4},{4,5},{6,7},{7,8},{8,9},{9,10},{10,11},{12... | collective-permute-start | bytes 1448 | tf_op jit(solution)/shard_map/ppermute | solution.py:23
  185.6 9.2 %collective-permute-start.23 = (f32[3,20,2]{2,1,0:T(8,128)S(1)}, f32[3,20,2]{2,1,0:T(8,128)S(1)}, u32[]{:S(2)}, u32[]{:S(2)}) collective-permute-start(f32[3,20,2]{2,1,0:T(8,128)S(1)} %get-tuple-element.88), channel_id=1, source_target_pairs={{1,0},{2,1},{3,2},{4,3},{5,4},{7,6},{8,7},{9,8},{10,9},{11,10},{13... | collective-permute-start | bytes 1448 | tf_op jit(solution)/shard_map/ppermute | solution.py:24
  195.3 11.1 %collective-permute-start.24 = (f32[3,2,512]{2,1,0:T(2,128)S(1)}, f32[3,2,512]{2,1,0:T(2,128)S(1)}, u32[]{:S(2)}, u32[]{:S(2)}) collective-permute-start(f32[3,2,512]{2,1,0:T(2,128)S(1)} %get-tuple-element.93), channel_id=1, source_target_pairs={{0,6},{6,12},{12,18},{18,24},{24,30},{30,36},{36,42},{42,48},{48,5... | collective-permute-start | bytes 36872 | tf_op jit(solution)/shard_map/ppermute | solution.py:23
  197.2 9.9 %collective-permute-start.25 = (f32[3,2,512]{2,1,0:T(2,128)S(1)}, f32[3,2,512]{2,1,0:T(2,128)S(1)}, u32[]{:S(2)}, u32[]{:S(2)}) collective-permute-start(f32[3,2,512]{2,1,0:T(2,128)S(1)} %get-tuple-element.94), channel_id=1, source_target_pairs={{6,0},{12,6},{18,12},{24,18},{30,24},{36,30},{42,36},{48,42},{54,4... | collective-permute-start | bytes 36872 | tf_op jit(solution)/shard_map/ppermute | solution.py:24
  207.2 4.6 %collective-permute-start.26 = (f32[3,20,2]{2,1,0:T(8,128)S(1)}, f32[3,20,2]{2,1,0:T(8,128)S(1)}, u32[]{:S(2)}, u32[]{:S(2)}) collective-permute-start(f32[3,20,2]{2,1,0:T(8,128)S(1)} %get-tuple-element.85), channel_id=1, source_target_pairs={{0,1},{1,2},{2,3},{3,4},{4,5},{6,7},{7,8},{8,9},{9,10},{10,11},{12... | collective-permute-start | bytes 1448 | tf_op jit(solution)/shard_map/ppermute | solution.py:23
  209.9 9.2 %collective-permute-start.27 = (f32[3,20,2]{2,1,0:T(8,128)S(1)}, f32[3,20,2]{2,1,0:T(8,128)S(1)}, u32[]{:S(2)}, u32[]{:S(2)}) collective-permute-start(f32[3,20,2]{2,1,0:T(8,128)S(1)} %get-tuple-element.86), channel_id=1, source_target_pairs={{1,0},{2,1},{3,2},{4,3},{5,4},{7,6},{8,7},{9,8},{10,9},{11,10},{13... | collective-permute-start | bytes 1448 | tf_op jit(solution)/shard_map/ppermute | solution.py:24
  219.6 10.6 %collective-permute-start.28 = (f32[3,2,512]{2,1,0:T(2,128)S(1)}, f32[3,2,512]{2,1,0:T(2,128)S(1)}, u32[]{:S(2)}, u32[]{:S(2)}) collective-permute-start(f32[3,2,512]{2,1,0:T(2,128)S(1)} %get-tuple-element.91), channel_id=1, source_target_pairs={{0,6},{6,12},{12,18},{18,24},{24,30},{30,36},{36,42},{42,48},{48,5... | collective-permute-start | bytes 36872 | tf_op jit(solution)/shard_map/ppermute | solution.py:23
  221.5 9.5 %collective-permute-start.29 = (f32[3,2,512]{2,1,0:T(2,128)S(1)}, f32[3,2,512]{2,1,0:T(2,128)S(1)}, u32[]{:S(2)}, u32[]{:S(2)}) collective-permute-start(f32[3,2,512]{2,1,0:T(2,128)S(1)} %get-tuple-element.92), channel_id=1, source_target_pairs={{6,0},{12,6},{18,12},{24,18},{30,24},{36,30},{42,36},{48,42},{54,4... | collective-permute-start | bytes 36872 | tf_op jit(solution)/shard_map/ppermute | solution.py:24
  231.1 4.7 %collective-permute-start.30 = (f32[3,20,2]{2,1,0:T(8,128)S(1)}, f32[3,20,2]{2,1,0:T(8,128)S(1)}, u32[]{:S(2)}, u32[]{:S(2)}) collective-permute-start(f32[3,20,2]{2,1,0:T(8,128)S(1)} %get-tuple-element.83), channel_id=1, source_target_pairs={{0,1},{1,2},{2,3},{3,4},{4,5},{6,7},{7,8},{8,9},{9,10},{10,11},{12... | collective-permute-start | bytes 1448 | tf_op jit(solution)/shard_map/ppermute | solution.py:23
  233.8 9.2 %collective-permute-start.31 = (f32[3,20,2]{2,1,0:T(8,128)S(1)}, f32[3,20,2]{2,1,0:T(8,128)S(1)}, u32[]{:S(2)}, u32[]{:S(2)}) collective-permute-start(f32[3,20,2]{2,1,0:T(8,128)S(1)} %get-tuple-element.84), channel_id=1, source_target_pairs={{1,0},{2,1},{3,2},{4,3},{5,4},{7,6},{8,7},{9,8},{10,9},{11,10},{13... | collective-permute-start | bytes 1448 | tf_op jit(solution)/shard_map/ppermute | solution.py:24
  235.8 8.3 %copy-start.6 = (f32[9,8,16,128]{3,2,1,0:T(8,128)}, f32[9,8,16,128]{3,2,1,0:T(8,128)S(1)}, u32[]{:S(2)}) copy-start(f32[9,8,16,128]{3,2,1,0:T(8,128)S(1)} %copy_dynamic-update-slice_fusion.1) | copy-start | bytes 1769476
Sparse Core Ops, SparseCore 0:
  106.0 40.4 reduce-scatter.1
where the time goes:
time: 252 us; the launch traced here: 251 us
  starting transfers between devices  135 us (54%)
  waiting for transfers between devices  80.9 us (32%)
  between operations  15 us (6%)
  local copies, waits for them, and re-layouts  8.32 us (3%)
  other arithmetic  8.17 us (3%)
  matrix products  3.13 us (1%)
    ppermute x16, starting transfers between devices, padded(): after = lax.ppermute(leading, axis, down)  86.9 us
    ppermute x16, waiting for transfers between devices, padded(): after = lax.ppermute(leading, axis, down)  65.3 us
    ppermute x16, starting transfers between devices, padded(): before = lax.ppermute(last, axis, up)  48.5 us
    reduce_scatter x1, waiting for transfers between devices, on_device(): lax.psum_scatter(partial_value, 'blk', scatter_dimension=1, tiled=True)  13.7 us
  transfers between devices with their start and end apart: 33, of which 18 were waited for; matrix products, arithmetic and copies ran while one was open for 2% of the time, Pallas kernels for 0%

commit v1 on v0

v1 whole, which is shorter than its diff:
```python
import math

import jax
import jax.numpy as jnp
from jax import lax
from jax.experimental import pallas as pl
from jax.experimental.pallas import tpu as pltpu
from jax.sharding import PartitionSpec as P

Q = 0.25
R = 16
LANES = 128
DEPTH = 8
COLS = 512
S11, S22, S33, S23, S13, S12, BUO, LAM, MU = 3, 4, 5, 6, 7, 8, 9, 10, 11
UP_PLANES = [(S11, 0), (S11, 1), (S11, 2)] + [
    (f, t) for f in (S12, S13, S23, S22, S33, 0, 1, 2, BUO, LAM, MU) for t in (0, 1)
]
N_UP = len(UP_PLANES)
UP_INDEX = {ft: i for i, ft in enumerate(UP_PLANES)}
STRIP = N_UP
N_STRIP = 24
MISC = STRIP + N_STRIP
OCEAN = MISC + 1
SEC_TILES = OCEAN + 16
B_UP, B_FACTOR, B_SLAB, B_OCEAN, BLK_TILES = 0, 4, 6, 12, 13
F32 = jnp.float32
BF16 = jnp.bfloat16
VMEM = pl.BlockSpec(memory_space=pltpu.VMEM)


def lane_iota(shape):
    return lax.broadcasted_iota(jnp.int32, shape, len(shape) - 1)


def row_iota(shape):
    return lax.broadcasted_iota(jnp.int32, shape, 0)


def reader(slab, mats):
    def read(f, t, rows):
        return slab[f, t, rows, :] if f < 9 else mats[f - 9][t, rows, :]

    return read


def pack_kernel(slab, buo, lam, mu, ocean, depth, widths, first, second):
    odd = lax.rem(lax.axis_index("sec"), 2)
    read = reader(slab, (buo, lam, mu))
    for out, lower in ((first, odd), (second, 1 - odd)):
        start = pl.multiple_of(lower * 8, 8)
        rows = pl.ds(start, 8)
        for i, (f, t) in enumerate(UP_PLANES):
            out[i] = read(f, t, rows)
        for p in range(96):
            f, t = p // 8, p % 8
            strip = jnp.where(lower == 1, read(f, t, slice(14, 16)), read(f, t, slice(0, 2)))
            out[STRIP + p // 4, 2 * (p % 4) : 2 * (p % 4) + 2, :] = strip
        out[MISC] = jnp.zeros((8, LANES), F32)
        for t in (0, 1):
            out[MISC, t : t + 1, :] = read(S12, t, slice(7, 8))
        out[MISC, 2:3, 0 : widths.shape[1]] = widths[...].astype(F32)
        for f in range(4):
            for k in range(4):
                cols = slice(k * LANES, (k + 1) * LANES)
                out[OCEAN + 4 * f + k] = ocean[f, rows, cols] if f < 3 else depth[rows, cols]


def sides(first, second):
    odd = lax.rem(lax.axis_index("sec"), 2)

    def top(i):
        return jnp.where(odd == 0, first[i], second[i])

    def bottom(i):
        return jnp.where(odd == 0, second[i], first[i])

    return top, bottom


def uplift_kernel(slab, buo, lam, mu, ocean, depth, first, second, send, strips):
    me = lax.axis_index("blk")
    read = reader(slab, (buo, lam, mu))
    top, bottom = sides(first, second)
    shape = (32, LANES)
    lane, row = lane_iota(shape), row_iota(shape)

    def plane(f, t):
        i = UP_INDEX[(f, t)]
        return jnp.concatenate([top(i), read(f, t, slice(0, 16)), bottom(i)], axis=0)

    def north(x):
        return pltpu.roll(x, 1, 0)

    def south(x):
        return pltpu.roll(x, 31, 0)

    def west(x):
        return jnp.where(lane == 0, 0.0, pltpu.roll(x, 1, 1))

    def east(x):
        return jnp.where(lane == LANES - 1, 0.0, pltpu.roll(x, LANES - 1, 1))

    s11 = [plane(S11, t) for t in range(3)]
    s22, s33, s23, s13, s12 = ([plane(f, t) for t in (0, 1)] for f in (S22, S33, S23, S13, S12))
    b, la, m = ([plane(f, t) for t in (0, 1)] for f in (BUO, LAM, MU))
    misc = top(MISC)
    v1, v2, v3 = [], [], []
    for t in (0, 1):
        above = lambda s: s[t] - s[t - 1] if t else s[t]
        s12n = jnp.where(row == 0, misc[t : t + 1, :], north(s12[t]))
        v1.append(plane(0, t) + Q * b[t] * (s11[t + 1] - s11[t] + (s12[t] - s12n) + (s13[t] - west(s13[t]))))
        v2.append(plane(1, t) + Q * b[t] * (south(s22[t]) - s22[t] + above(s12) + (s23[t] - west(s23[t]))))
        v3.append(plane(2, t) + Q * b[t] * (east(s33[t]) - s33[t] + above(s13) + (s23[t] - north(s23[t]))))
    n11 = []
    for t in (0, 1):
        d1 = v1[t] - v1[t - 1] if t else v1[t]
        dil = d1 + (v2[t] - north(v2[t])) + (v3[t] - west(v3[t]))
        n11.append(s11[t] + Q * (la[t] * dil + 2.0 * m[t] * d1))
    n12 = s12[0] + Q * m[0] * (south(v1[0]) - v1[0] + v2[1] - v2[0])
    n13 = s13[0] + Q * m[0] * (east(v1[0]) - v1[0] + v3[1] - v3[0])
    g = Q * Q * b[0]
    rise = 2.0 * Q * v1[0] + g * (n11[1] - n11[0] + n12 - north(n12) + n13 - west(n13))

    la0, la1 = Q * la[0], Q * la[1]
    m0, m1 = la0 + 2.0 * Q * m[0], la1 + 2.0 * Q * m[1]
    q0 = Q * m[0]
    q0n = north(q0)
    b0, b1 = Q * b[0], Q * b[1]
    left = [
        g * (la1 + q0) * b1,
        -g * (la0 + q0) * b0,
        g * q0,
        g * q0 * s13[0],
        s13[0],
        south(s13[0]),
        north(s13[0]),
        s13[1],
        s23[0],
        north(s23[0]),
        s23[1],
        north(s23[1]),
        v3[1],
        b1,
        v3[0],
        b0,
        n13,
        q0,
        q0 * s13[0],
        q0 * b1,
        q0 * b0,
        s13[0],
    ]
    right = [
        s33[1],
        s33[0],
        v1[0],
        -b0,
        -(2.0 * Q - g * (m1 + m0 + 2.0 * q0 + q0n)) * b0,
        -g * q0 * south(b0),
        -g * q0n * north(b0),
        -g * m1 * b1,
        g * (la0 + q0) * b0,
        -g * (la0 + q0n) * north(b0),
        -g * (la1 + q0) * b1,
        g * (la1 + q0n) * north(b1),
        -g * la1,
        -g * la1 * s33[1],
        g * la0,
        g * la0 * s33[0],
        -g,
        -g * v1[0],
        g * b0,
        -g * s33[1],
        g * s33[0],
        -pltpu.roll(g, LANES - 1, 1) * q0 * b0,
    ]
    factors = jnp.zeros(shape, F32)
    for i, (x, y) in enumerate(zip(left, right)):
        factors = jnp.where(lane == i, pltpu.roll(x, (i + 1) % LANES, 1), factors)
        factors = jnp.where(lane == 32 + i, pltpu.roll(y, 32 + i, 1), factors)
    packed = jnp.where(lane[:16] < 64, factors[:16], pltpu.roll(factors[16:], 64, 1))

    tile = (8, LANES)
    tlane = lane_iota(tile)
    strips[...] = jnp.zeros((96, 8, LANES), F32)
    odd = lax.rem(lax.axis_index("sec"), 2)
    for p in range(96):
        i, at = STRIP + p // 4, slice(2 * (p % 4), 2 * (p % 4) + 2)
        a, c = first[i, at, :], second[i, at, :]
        strips[p, 0:2, :] = jnp.where(odd == 0, c, a)
        strips[p, 6:8, :] = jnp.where(odd == 0, a, c)
    heads, tails = [], []
    for r in range(3):
        for half in range(2):
            head, tail = jnp.zeros(tile, F32), jnp.zeros(tile, F32)
            for t in range(4 * half, 4 * half + 4):
                for f in range(12):
                    at = 24 * (t % 4) + 2 * f
                    x = read(f, t, slice(8 * r, 8 * r + 8)) if r < 2 else strips[f * 8 + t]
                    x = pltpu.roll(x, at + 2, 1)
                    tail = jnp.where((tlane >= at) & (tlane < at + 2), x, tail)
                    head = jnp.where((tlane >= at + 2) & (tlane < at + 4), x, head)
            heads.append(head)
            tails.append(tail)
    head, tail = jnp.zeros(tile, F32), jnp.zeros(tile, F32)
    for f in range(4):
        for r in range(4):
            at = 32 * f + 8 * r
            ends = []
            for k in (0, 3):
                cols = slice(k * LANES, (k + 1) * LANES)
                rows = slice(8 * r - 8, 8 * r)
                if r == 0:
                    x = top(OCEAN + 4 * f + k)
                elif r == 3:
                    x = bottom(OCEAN + 4 * f + k)
                else:
                    x = ocean[f, rows, cols] if f < 3 else depth[rows, cols]
                ends.append(x)
            here = (tlane >= at) & (tlane < at + 8)
            head = jnp.where(here, pltpu.roll(ends[0], at, 1), head)
            tail = jnp.where(here, pltpu.roll(ends[1], (at + 8) % LANES, 1), tail)
    heads.append(head)
    tails.append(tail)
    for d in range(send.shape[0]):
        for r in range(4):
            send[d, B_UP + r] = rise[8 * r : 8 * r + 8]
        for r in range(2):
            send[d, B_FACTOR + r] = packed[8 * r : 8 * r + 8]
        for i in range(7):
            send[d, B_SLAB + i] = jnp.where(d < me, heads[i], tails[i])


def filter_kernel(face, widths, first, second, hi, lo):
    me = lax.axis_index("blk")
    top, bottom = sides(first, second)
    lane = lane_iota((1, LANES))
    face_at = (face[...] - me * COLS).astype(F32)
    width = face.shape[1]

    def scales(row):
        out = []
        for j in (me, me + 1, me - 1):
            w = jnp.sum(jnp.where(lane[:, : row.shape[1]] == j, row, 0.0), axis=1, keepdims=True)
            w = jnp.where(w > 0.0, w, 1.0)
            out.append((-(math.pi / 2.0) * math.log2(math.e) / w, 1.0 / w))
        return out

    groups = [scales(top(MISC)[2:3, :]), scales(widths[...].astype(F32)), scales(bottom(MISC)[2:3, :])]

    def put(k, rows, distance, rate, gain):
        decay = jnp.exp2(distance * rate)
        value = decay / (1.0 + decay * decay) * gain
        upper = value.astype(BF16)
        hi[k, rows, :] = upper
        lo[k, rows, :] = (value - upper.astype(F32)).astype(BF16)

    @pl.loop(0, COLS // 16)
    def _(c):
        start = pl.multiple_of(c * 16, 16)
        at = (lax.broadcasted_iota(jnp.int32, (16, width), 0) + start).astype(F32)
        distance = jnp.abs(at - face_at)
        for k in range(3):
            put(k, pl.ds(start, 16), distance, *groups[k][0])

    row = row_iota((16, width))
    at = jnp.where(row < 8, row + COLS, row - 16).astype(F32)
    distance = jnp.abs(at - face_at)
    for k in range(3):
        rate = jnp.where(row < 8, groups[k][1][0], groups[k][2][0])
        gain = jnp.where(row < 8, groups[k][1][1], groups[k][2][1])
        put(k, slice(COLS, COLS + 16), distance, rate, gain)


def final_kernel(
    slab, buo, lam, mu, ocean, depth, first, second, strips, recv, hi, lo, slab_out, ocean_out, cells, mats, flat
):
    sec, me = lax.axis_index("sec"), lax.axis_index("blk")
    n_sec, n_blk = lax.axis_size("sec"), lax.axis_size("blk")
    read = reader(slab, (buo, lam, mu))
    top, bottom = sides(first, second)
    shape = (32, LANES)
    lane = lane_iota(shape)
    before, after = jnp.maximum(me - 1, 0), jnp.minimum(me + 1, n_blk - 1)
    tile = (8, LANES)
    tlane = lane_iota(tile)

    rises = [jnp.concatenate([recv[j, B_UP + r] for r in range(4)], axis=0) for j in range(n_blk)]
    factors = []
    for j in range(n_blk):
        x = jnp.concatenate([recv[j, B_FACTOR], recv[j, B_FACTOR + 1]], axis=0)
        factors.append(jnp.concatenate([x, pltpu.roll(x, 64, 1)], axis=0))
    for j in range(n_blk - 1):
        terms = factors[j] * pltpu.roll(factors[j + 1], LANES - 32, 1)
        pick = lambda a, z: jnp.sum(jnp.where((lane >= a) & (lane < z), terms, 0.0), axis=1, keepdims=True)
        rises[j] = rises[j] + jnp.where(lane == LANES - 1, pick(0, 4), 0.0)
        rises[j + 1] = rises[j + 1] + jnp.where(lane == 0, pick(4, 21), 0.0) + jnp.where(lane == 1, pick(21, 22), 0.0)
    rise = jnp.concatenate(rises, axis=1)
    rise_hi = rise.astype(BF16)
    rise_lo = (rise - rise_hi.astype(F32)).astype(BF16)

    def dot(a, c):
        return lax.dot_general(a, c, (((1,), (1,)), ((), ())), preferred_element_type=F32)

    source = None
    col = lane_iota((COLS + 16, 32))
    for k in range(3):
        a = hi[k]
        part = dot(a, rise_hi) + dot(a, rise_lo) + dot(lo[k], rise_hi)
        source = part if k == 0 else jnp.where(col >= (0, 8, 24)[k], part, source)
    flat[...] = jnp.zeros((5 * LANES, LANES), F32)
    flat[0 : COLS + 8, 0:32] = source[0 : COLS + 8]
    flat[5 * LANES - 8 : 5 * LANES, 0:32] = source[COLS + 8 : COLS + 16]
    source = jnp.concatenate(
        [flat[k * LANES : (k + 1) * LANES, :].T[0:32] for k in range(5)], axis=1
    )

    ring = (32, 5 * LANES)
    seas = []
    for f in range(4):
        tiles = []
        for k in range(4):
            cols = slice(k * LANES, (k + 1) * LANES)
            own = ocean[f, :, cols] if f < 3 else depth[:, cols]
            i = OCEAN + 4 * f + k
            tiles.append(jnp.concatenate([top(i), own, bottom(i)], axis=0))
        halo = []
        for r in range(4):
            at = 32 * f + 8 * r
            east_in = pltpu.roll(recv[after, B_OCEAN], (LANES - at) % LANES, 1)
            west_in = pltpu.roll(recv[before, B_OCEAN], (2 * LANES - 8 - at) % LANES, 1)
            x = jnp.where((tlane < 8) & (me < n_blk - 1), east_in, 0.0)
            halo.append(jnp.where((tlane >= LANES - 8) & (me > 0), west_in, x))
        tiles.append(jnp.concatenate(halo, axis=0))
        seas.append(jnp.concatenate(tiles, axis=1))
    surface, strike, dip, water = seas
    at = lane_iota(ring)
    at = jnp.where(at >= 5 * LANES - 8, at - 5 * LANES, at)
    x, y = row_iota(ring) - 8 + sec * R, at + me * COLS
    wet = (x >= 0) & (x < n_sec * R) & (y >= 0) & (y < n_blk * COLS) & (at < COLS + 8)
    surface = surface + source
    water = 0.25 * water
    for step in range(4):
        change = pltpu.roll(strike, 31, 0) - pltpu.roll(strike, 1, 0)
        change = change + (pltpu.roll(dip, 5 * LANES - 1, 1) - pltpu.roll(dip, 1, 1))
        surface = jnp.where(wet, surface - 0.25 * change, 0.0)
        strike = strike - water * (pltpu.roll(surface, 31, 0) - pltpu.roll(surface, 1, 0))
        dip = dip - water * (pltpu.roll(surface, 5 * LANES - 1, 1) - pltpu.roll(surface, 1, 1))
    ocean_out[0] = surface[8:24, 0:COLS]
    ocean_out[1] = strike[8:24, 0:COLS]
    ocean_out[2] = dip[8:24, 0:COLS]

    for f in range(9):
        for t in (0, DEPTH + 1):
            cells[f, t] = jnp.zeros((24, 2 * LANES), F32)
    west_on, east_on = me > 0, me < n_blk - 1
    for r in range(3):
        rows = slice(8 * r, 8 * r + 8)
        for half in range(2):
            i = B_SLAB + 2 * r + half
            east_in = jnp.where(east_on, recv[after, i], 0.0)
            west_in = jnp.where(west_on, recv[before, i], 0.0)
            for t in range(4 * half, 4 * half + 4):
                for f in range(12):
                    at = 24 * (t % 4) + 2 * f
                    edge = jnp.where(tlane < at + 2, west_in, east_in)
                    edge = pltpu.roll(edge, LANES - at - 2, 1)
                    own = read(f, t, rows) if r < 2 else strips[f * 8 + t]
                    if f < 9:
                        cells[f, t + 1, rows, 0:LANES] = own
                        cells[f, t + 1, rows, LANES:] = edge
                    else:
                        mats[f - 9, t, rows, 0:LANES] = own
                        mats[f - 9, t, rows, LANES:] = edge

    north = lambda v: pltpu.roll(v, 1, 0)
    south = lambda v: pltpu.roll(v, 23, 0)
    west = lambda v: pltpu.roll(v, 1, 1)
    east = lambda v: pltpu.roll(v, 2 * LANES - 1, 1)
    for step in range(2):

        @pl.loop(1, DEPTH + 1)
        def _(t):
            qb = Q * mats[0, t - 1]
            s12, s13, s23 = cells[S12, t], cells[S13, t], cells[S23, t]
            s11, s22, s33 = cells[S11, t], cells[S22, t], cells[S33, t]
            cells[0, t] = cells[0, t] + qb * (
                cells[S11, t + 1] - s11 + (s12 - north(s12)) + (s13 - west(s13))
            )
            cells[1, t] = cells[1, t] + qb * (
                south(s22) - s22 + (s12 - cells[S12, t - 1]) + (s23 - west(s23))
            )
            cells[2, t] = cells[2, t] + qb * (
                east(s33) - s33 + (s13 - cells[S13, t - 1]) + (s23 - north(s23))
            )

        @pl.loop(1, DEPTH + 1)
        def _(t):
            la, m = Q * mats[1, t - 1], Q * mats[2, t - 1]
            v1, v2, v3 = cells[0, t], cells[1, t], cells[2, t]
            d1, d2, d3 = v1 - cells[0, t - 1], v2 - north(v2), v3 - west(v3)
            dil = la * (d1 + d2 + d3)
            m2 = 2.0 * m
            new = [
                cells[S11, t] + (dil + m2 * d1),
                cells[S22, t] + (dil + m2 * d2),
                cells[S33, t] + (dil + m2 * d3),
                cells[S23, t] + m * (east(v2) - v2 + (south(v3) - v3)),
                cells[S13, t] + m * (east(v1) - v1 + (cells[2, t + 1] - v3)),
                cells[S12, t] + m * (south(v1) - v1 + (cells[1, t + 1] - v2)),
            ]
            if step == 0:
                for f, x in enumerate(new):
                    cells[3 + f, t] = x
            else:
                for f, x in enumerate([v1, v2, v3] + new):
                    slab_out[f, t - 1] = x[0:R, 0:LANES]


def call(kernel, out_shape, flops, *args, scratch=()):
    many = isinstance(out_shape, (list, tuple))
    outs = list(out_shape) if many else [out_shape]
    n_bytes = sum(a.size * a.dtype.itemsize for a in args) + sum(math.prod(o.shape) * o.dtype.itemsize for o in outs)
    return pl.pallas_call(
        kernel,
        out_shape=out_shape,
        in_specs=[VMEM] * len(args),
        out_specs=[VMEM] * len(outs) if many else VMEM,
        scratch_shapes=scratch,
        compiler_params=pltpu.CompilerParams(vmem_limit_bytes=40 * 1024 * 1024),
        cost_estimate=pl.CostEstimate(flops=flops, bytes_accessed=n_bytes, transcendentals=0),
    )(*args)


def swap(x, axis, start):
    pairs = []
    for i in range(start, lax.axis_size(axis) - 1, 2):
        pairs += [(i, i + 1), (i + 1, i)]
    return lax.ppermute(x, axis, pairs)


def on_device(slab_state, buoyancy, lame_lambda, lame_mu, face_map, band_widths, ocean_state, water_depth):
    n_blk = lax.axis_size("blk")
    n_face = face_map.shape[0]
    arr = jax.ShapeDtypeStruct
    own = (slab_state, buoyancy, lame_lambda, lame_mu, ocean_state, water_depth)
    message = arr((SEC_TILES, 8, LANES), F32)
    first, second = call(pack_kernel, (message, message), 10**6, *own, band_widths)
    first = swap(first, "sec", 1)
    second = swap(second, "sec", 0)
    send, strips = call(
        uplift_kernel,
        (arr((n_blk, BLK_TILES, 8, LANES), F32), arr((96, 8, LANES), F32)),
        10**7,
        *own,
        first,
        second,
    )
    recv = lax.all_to_all(send, "blk", 0, 0, tiled=True)
    kernels = arr((3, COLS + 16, n_face), BF16)
    hi, lo = call(
        filter_kernel, (kernels, kernels), 10**8, face_map.reshape(1, n_face), band_widths, first, second
    )
    return call(
        final_kernel,
        (arr(slab_state.shape, F32), arr(ocean_state.shape, F32)),
        10**8,
        *own,
        first,
        second,
        strips,
        recv,
        hi,
        lo,
        scratch=[
            pltpu.VMEM((9, DEPTH + 2, 24, 2 * LANES), F32),
            pltpu.VMEM((3, DEPTH, 24, 2 * LANES), F32),
            pltpu.VMEM((5 * LANES, LANES), F32),
        ],
    )


def solution(mesh):
    in_specs = (
        P(None, None, "sec", "blk"),
        P(None, "sec", "blk"),
        P(None, "sec", "blk"),
        P(None, "sec", "blk"),
        P(),
        P("sec", None),
        P(None, "sec", "blk"),
        P("sec", "blk"),
    )
    out_specs = (P(None, None, "sec", "blk"), P(None, "sec", "blk"))
    return jax.shard_map(on_device, mesh=mesh, in_specs=in_specs, out_specs=out_specs, check_vma=False)
```

time: 252 us -> 69.8 us (0.28)
  starting transfers between devices: 135 us -> 25.9 us
  waiting for transfers between devices: 80.9 us -> 16.7 us
  between operations: 15 us -> 0.75 us
  Pallas kernels: 0 us -> 12.2 us
  other arithmetic: 8.17 us -> 0 us
  local copies, waits for them, and re-layouts: 8.32 us -> 13.4 us
  matrix products: 3.13 us -> 0 us
    ppermute x32 -> x2, starting transfers between devices: 135 us -> 12.8 us  [swap(): return lax.ppermute(x, axis, pairs)]
    ppermute x32 -> x2, waiting for transfers between devices: 67.2 us -> 7 us  [swap(): return lax.ppermute(x, axis, pairs)]
    reduce_scatter x1 -> x0, waiting for transfers between devices: 13.7 us -> none  [on_device(): lax.psum_scatter(partial_value, 'blk', scatter_dimension=1, tiled=True)]
    all_to_all x0 -> x1, starting transfers between devices: none -> 13.1 us  [on_device(): recv = lax.all_to_all(send, 'blk', 0, 0, tiled=True)]
    pallas_call x0 -> x4, Pallas kernels: none -> 12.2 us  [call(): pl.pallas_call(kernel, out_shape=out_shape, in_specs=[VMEM] * len(args),...]
    unnamed x28 -> x44, local copies, waits for them, and re-layouts: 1.65 us -> 13.4 us
    all_to_all x0 -> x1, waiting for transfers between devices: none -> 9.68 us  [on_device(): recv = lax.all_to_all(send, 'blk', 0, 0, tiled=True)]
    slice x11 -> x0, local copies, waits for them, and re-layouts: 3.54 us -> none  [the longest x2 1.46 us: padded(): leading = lax.slice_in_dim(x, 0, width, axis=dim)]
  transfers between devices with their start and end apart: 33 -> 3, of which waited for: 18 -> 3; matrix products, arithmetic and copies ran while one was open for 2% -> 0% of each run, Pallas kernels for 0% -> 4%
where the time goes in v1:
time: 69.8 us; the launch traced here: 69 us
  starting transfers between devices  25.9 us (37%)
  waiting for transfers between devices  16.7 us (24%)
  local copies, waits for them, and re-layouts  13.4 us (19%)
  Pallas kernels  12.2 us (17%)
  between operations  0.75 us (1%)
    unnamed x44, local copies, waits for them, and re-layouts  13.4 us
    all_to_all x1, starting transfers between devices, on_device(): recv = lax.all_to_all(send, 'blk', 0, 0, tiled=True)  13.1 us
    ppermute x2, starting transfers between devices, swap(): return lax.ppermute(x, axis, pairs)  12.8 us
    pallas_call x4, Pallas kernels, call(): pl.pallas_call(kernel, out_shape=out_shape, in_specs=[VMEM] * len(args),...  12.2 us
    all_to_all x1, waiting for transfers between devices, on_device(): recv = lax.all_to_all(send, 'blk', 0, 0, tiled=True)  9.68 us
    ppermute x2, waiting for transfers between devices, swap(): return lax.ppermute(x, axis, pairs)  7 us
  transfers between devices with their start and end apart: 3, of which 3 were waited for; matrix products, arithmetic and copies ran while one was open for 0% of the time, Pallas kernels for 4%

profile of v1, /device:TPU:7, one launch (start us, length us, event | category | flops | bytes accessed | tf_op | source)
XLA Modules:
  0.0 69.0 jit_solution(10420029764279032781)
XLA Ops:
  0.6 0.0 copy-start
  0.6 1.1 %copy-done = f32[9,8,16,128]{3,2,1,0:T(8,128)S(1)} copy-done((f32[9,8,16,128]{3,2,1,0:T(8,128)S(1)}, f32[9,8,16,128]{3,2,1,0:T(8,128)}, u32[]{:S(2)}) %copy-start) | copy-done | bytes 589848
  1.7 0.0 copy-start.7
  1.7 0.9 %copy-done.7 = f32[3,16,512]{2,1,0:T(8,128)S(1)} copy-done((f32[3,16,512]{2,1,0:T(8,128)S(1)}, f32[3,16,512]{2,1,0:T(8,128)}, u32[]{:S(2)}) %copy-start.7) | copy-done | bytes 98328
  2.6 0.0 copy-start.9
  2.6 0.8 %copy-done.9 = f32[8,16,128]{2,1,0:T(8,128)S(1)} copy-done((f32[8,16,128]{2,1,0:T(8,128)S(1)}, f32[8,16,128]{2,1,0:T(8,128)}, u32[]{:S(2)}) %copy-start.9) | copy-done | bytes 65560
  3.4 0.0 copy-start.11
  3.4 0.8 %copy-done.11 = f32[8,16,128]{2,1,0:T(8,128)S(1)} copy-done((f32[8,16,128]{2,1,0:T(8,128)S(1)}, f32[8,16,128]{2,1,0:T(8,128)}, u32[]{:S(2)}) %copy-start.11) | copy-done | bytes 65560
  4.3 0.0 copy-start.13
  4.3 0.8 %copy-done.13 = f32[8,16,128]{2,1,0:T(8,128)S(1)} copy-done((f32[8,16,128]{2,1,0:T(8,128)S(1)}, f32[8,16,128]{2,1,0:T(8,128)}, u32[]{:S(2)}) %copy-start.13) | copy-done | bytes 65560
  5.1 0.0 copy-start.17
  5.1 0.8 %copy-done.17 = f32[16,512]{1,0:T(8,128)S(1)} copy-done((f32[16,512]{1,0:T(8,128)S(1)}, f32[16,512]{1,0:T(8,128)}, u32[]{:S(2)}) %copy-start.17) | copy-done | bytes 32792
  5.9 0.0 copy-start.19
  5.9 0.7 copy-done.19
  6.5 0.0 copy-start.21
  6.5 0.0 copy-start.1
  6.5 0.0 copy-start.8
  6.5 0.0 copy-start.10
  6.5 0.0 copy-start.12
  6.5 0.0 copy-start.18
  6.6 0.1 shard_map.95
  6.7 10.9 %collective-permute-start = (f32[66,8,128]{2,1,0:T(8,128)S(1)}, f32[66,8,128]{2,1,0:T(8,128)S(1)}, u32[]{:S(2)}, u32[]{:S(2)}) collective-permute-start(f32[66,8,128]{2,1,0:T(8,128)S(1)} %get-tuple-element.8), channel_id=1, source_target_pairs={{6,12},{12,6},{18,24},{24,18},{30,36},{36,30},{42,48},{48,42},{54,... | collective-permute-start | bytes 811016 | tf_op jit(solution)/shard_map/ppermute | solution.py:440
  17.6 1.9 %collective-permute-start.1 = (f32[66,8,128]{2,1,0:T(8,128)S(1)}, f32[66,8,128]{2,1,0:T(8,128)S(1)}, u32[]{:S(2)}, u32[]{:S(2)}) collective-permute-start(f32[66,8,128]{2,1,0:T(8,128)S(1)} %get-tuple-element.9), channel_id=1, source_target_pairs={{0,6},{6,0},{12,18},{18,12},{24,30},{30,24},{36,42},{42,36},{48,54... | collective-permute-start | bytes 811016 | tf_op jit(solution)/shard_map/ppermute | solution.py:440
  19.5 4.3 %collective-permute-done.first = f32[66,8,128]{2,1,0:T(8,128)S(1)} collective-permute-done((f32[66,8,128]{2,1,0:T(8,128)S(1)}, f32[66,8,128]{2,1,0:T(8,128)S(1)}, u32[]{:S(2)}, u32[]{:S(2)}) %collective-permute-start) | collective-permute-done | bytes 270368 | tf_op jit(solution)/shard_map/ppermute | solution.py:440
  23.8 2.7 %collective-permute-done.1.second = f32[66,8,128]{2,1,0:T(8,128)S(1)} collective-permute-done((f32[66,8,128]{2,1,0:T(8,128)S(1)}, f32[66,8,128]{2,1,0:T(8,128)S(1)}, u32[]{:S(2)}, u32[]{:S(2)}) %collective-permute-start.1) | collective-permute-done | bytes 270368 | tf_op jit(solution)/shard_map/ppermute | solution.py:440
  26.5 1.5 %shard_map.96 = (f32[6,13,8,128]{3,2,1,0:T(8,128)}, f32[96,8,128]{2,1,0:T(8,128)S(1)}) custom-call(f32[9,8,16,128]{3,2,1,0:T(8,128)S(1)} %copy-done, f32[8,16,128]{2,1,0:T(8,128)S(1)} %copy-done.9, f32[8,16,128]{2,1,0:T(8,128)S(1)} %copy-done.11, f32[8,16,128]{2,1,0:T(8,128)S(1)} %copy-done.13, f32[3,16,512]{2,1,0:T(8,128)S(1)} %copy-done.7, ...), custom_call_target="tpu_custom_call" | custom-call | flops 10000000 | bytes 2170880 | tf_op jit(solution)/shard_map/pallas_call | solution.py:425
  28.0 0.0 copy-done.4
  28.1 13.1 %all-to-all-start = ((f32[6,13,8,128]{3,2,1,0:T(8,128)}), f32[6,13,8,128]{3,2,1,0:T(8,128)}, u32[]{:S(2)}, u32[]{:S(2)}) async-start(f32[6,13,8,128]{3,2,1,0:T(8,128)} %get-tuple-element.11), calls=%async_computation | async-start | bytes 638976 | tf_op jit(solution)/shard_map/all_to_all | solution.py:460
  41.1 0.0 copy-done.15
  41.1 0.0 copy-done.21
  41.1 0.0 copy-start.5
  41.2 0.9 %copy-done.5 = f32[66,8,128]{2,1,0:T(8,128)S(1)} copy-done((f32[66,8,128]{2,1,0:T(8,128)S(1)}, f32[66,8,128]{2,1,0:T(8,128)}, u32[]{:S(2)}) %copy-start.5) | copy-done | bytes 270360
  42.1 0.7 copy-done.20
  42.8 2.6 %shard_map.97 = (bf16[3,528,768]{2,1,0:T(8,128)(2,1)S(1)}, bf16[3,528,768]{2,1,0:T(8,128)(2,1)S(1)}) custom-call(s32[1,768]{1,0:T(1,128)S(1)} %reshape.7.face, s32[1,6]{1,0:T(1,128)S(1)} %copy-done.20, f32[66,8,128]{2,1,0:T(8,128)S(1)} %collective-permute-done.first, f32[66,8,128]{2,1,0:T(8,128)S(1)} %copy-done.5), custom_call_target="tpu_custom_call" | custom-call | flops 100000000 | bytes 5409816 | tf_op jit(solution)/shard_map/pallas_call | solution.py:425
  45.4 0.0 copy-start.2
  45.4 1.4 %copy-done.2 = bf16[3,528,768]{2,1,0:T(8,128)(2,1)} copy-done((bf16[3,528,768]{2,1,0:T(8,128)(2,1)}, bf16[3,528,768]{2,1,0:T(8,128)(2,1)S(1)}, u32[]{:S(2)}) %copy-start.2) | copy-done | bytes 2433048
  46.8 9.7 %all-to-all-done.recv = f32[6,13,8,128]{3,2,1,0:T(8,128)} async-done(((f32[6,13,8,128]{3,2,1,0:T(8,128)}), f32[6,13,8,128]{3,2,1,0:T(8,128)}, u32[]{:S(2)}, u32[]{:S(2)}) %all-to-all-start) | async-done | bytes 319520 | tf_op jit(solution)/shard_map/all_to_all | solution.py:460
  56.5 0.0 copy-done.1
  56.5 0.0 copy-done.8
  56.5 0.0 copy-done.10
  56.5 0.0 copy-done.12
  56.5 0.0 copy-done.18
  56.5 0.0 copy-start.3
  56.5 1.7 %copy-done.3 = bf16[3,528,768]{2,1,0:T(8,128)(2,1)S(1)} copy-done((bf16[3,528,768]{2,1,0:T(8,128)(2,1)S(1)}, bf16[3,528,768]{2,1,0:T(8,128)(2,1)}, u32[]{:S(2)}) %copy-start.3) | copy-done | bytes 2433048
  58.2 1.0 %copy-done.6 = f32[66,8,128]{2,1,0:T(8,128)S(1)} copy-done((f32[66,8,128]{2,1,0:T(8,128)S(1)}, f32[66,8,128]{2,1,0:T(8,128)}, u32[]{:S(2)}) %copy-start.6) | copy-done | bytes 270360
  59.1 0.8 %copy-done.14 = f32[8,16,128]{2,1,0:T(8,128)S(1)} copy-done((f32[8,16,128]{2,1,0:T(8,128)S(1)}, f32[8,16,128]{2,1,0:T(8,128)}, u32[]{:S(2)}) %copy-start.14) | copy-done | bytes 65560
  60.0 1.0 %copy-done.16 = f32[96,8,128]{2,1,0:T(8,128)S(1)} copy-done((f32[96,8,128]{2,1,0:T(8,128)S(1)}, f32[96,8,128]{2,1,0:T(8,128)}, u32[]{:S(2)}) %copy-start.16) | copy-done | bytes 393240
  61.0 8.0 %shard_map.98 = (f32[9,8,16,128]{3,2,1,0:T(8,128)}, f32[3,16,512]{2,1,0:T(8,128)}) custom-call(f32[9,8,16,128]{3,2,1,0:T(8,128)S(1)} %copy-done.1, f32[8,16,128]{2,1,0:T(8,128)S(1)} %copy-done.10, f32[8,16,128]{2,1,0:T(8,128)S(1)} %copy-done.12, f32[8,16,128]{2,1,0:T(8,128)S(1)} %copy-done.14, f32[3,16,512]{2,1,0:T(8,128)S(1)} %copy-done.8, ...), custom_call_target="tpu_custom_call" | custom-call | flops 100000000 | bytes 7725056 | tf_op jit(solution)/shard_map/pallas_call | solution.py:425
  (7 shorter events, 0.0 us)
Async XLA Ops:
  0.6 1.1 %copy-start = (f32[9,8,16,128]{3,2,1,0:T(8,128)S(1)}, f32[9,8,16,128]{3,2,1,0:T(8,128)}, u32[]{:S(2)}) copy-start(f32[9,8,16,128]{3,2,1,0:T(8,128)} %slab.5) | copy-start | bytes 1769476
  1.7 0.9 %copy-start.7 = (f32[3,16,512]{2,1,0:T(8,128)S(1)}, f32[3,16,512]{2,1,0:T(8,128)}, u32[]{:S(2)}) copy-start(f32[3,16,512]{2,1,0:T(8,128)} %ocean.5) | copy-start | bytes 294916
  2.6 0.8 %copy-start.9 = (f32[8,16,128]{2,1,0:T(8,128)S(1)}, f32[8,16,128]{2,1,0:T(8,128)}, u32[]{:S(2)}) copy-start(f32[8,16,128]{2,1,0:T(8,128)} %buo.5) | copy-start | bytes 196612
  3.4 0.8 %copy-start.11 = (f32[8,16,128]{2,1,0:T(8,128)S(1)}, f32[8,16,128]{2,1,0:T(8,128)}, u32[]{:S(2)}) copy-start(f32[8,16,128]{2,1,0:T(8,128)} %lam.5) | copy-start | bytes 196612
  4.3 0.8 %copy-start.13 = (f32[8,16,128]{2,1,0:T(8,128)S(1)}, f32[8,16,128]{2,1,0:T(8,128)}, u32[]{:S(2)}) copy-start(f32[8,16,128]{2,1,0:T(8,128)} %mu.5) | copy-start | bytes 196612
  5.1 0.8 %copy-start.17 = (f32[16,512]{1,0:T(8,128)S(1)}, f32[16,512]{1,0:T(8,128)}, u32[]{:S(2)}) copy-start(f32[16,512]{1,0:T(8,128)} %depth.5) | copy-start | bytes 98308
  5.9 0.7 copy-start.19
  6.5 34.6 %copy-start.21 = (s32[768]{0:T(1024)S(1)}, s32[768]{0:T(1024)}, u32[]{:S(2)}) copy-start(s32[768]{0:T(1024)} %param.12) | copy-start | bytes 9220
  6.5 49.9 %copy-start.1 = (f32[9,8,16,128]{3,2,1,0:T(8,128)S(1)}, f32[9,8,16,128]{3,2,1,0:T(8,128)}, u32[]{:S(2)}) copy-start(f32[9,8,16,128]{3,2,1,0:T(8,128)} %slab.5) | copy-start | bytes 1769476
  6.5 49.9 %copy-start.8 = (f32[3,16,512]{2,1,0:T(8,128)S(1)}, f32[3,16,512]{2,1,0:T(8,128)}, u32[]{:S(2)}) copy-start(f32[3,16,512]{2,1,0:T(8,128)} %ocean.5) | copy-start | bytes 294916
  6.5 49.9 %copy-start.10 = (f32[8,16,128]{2,1,0:T(8,128)S(1)}, f32[8,16,128]{2,1,0:T(8,128)}, u32[]{:S(2)}) copy-start(f32[8,16,128]{2,1,0:T(8,128)} %buo.5) | copy-start | bytes 196612
  6.5 49.9 %copy-start.12 = (f32[8,16,128]{2,1,0:T(8,128)S(1)}, f32[8,16,128]{2,1,0:T(8,128)}, u32[]{:S(2)}) copy-start(f32[8,16,128]{2,1,0:T(8,128)} %lam.5) | copy-start | bytes 196612
  6.5 49.9 %copy-start.18 = (f32[16,512]{1,0:T(8,128)S(1)}, f32[16,512]{1,0:T(8,128)}, u32[]{:S(2)}) copy-start(f32[16,512]{1,0:T(8,128)} %depth.5) | copy-start | bytes 98308
  6.7 17.1 %collective-permute-start = (f32[66,8,128]{2,1,0:T(8,128)S(1)}, f32[66,8,128]{2,1,0:T(8,128)S(1)}, u32[]{:S(2)}, u32[]{:S(2)}) collective-permute-start(f32[66,8,128]{2,1,0:T(8,128)S(1)} %get-tuple-element.8), channel_id=1, source_target_pairs={{6,12},{12,6},{18,24},{24,18},{30,36},{36,30},{42,48},{48,42},{54,... | collective-permute-start | bytes 811016 | tf_op jit(solution)/shard_map/ppermute | solution.py:440
  17.6 8.9 %collective-permute-start.1 = (f32[66,8,128]{2,1,0:T(8,128)S(1)}, f32[66,8,128]{2,1,0:T(8,128)S(1)}, u32[]{:S(2)}, u32[]{:S(2)}) collective-permute-start(f32[66,8,128]{2,1,0:T(8,128)S(1)} %get-tuple-element.9), channel_id=1, source_target_pairs={{0,6},{6,0},{12,18},{18,12},{24,30},{30,24},{36,42},{42,36},{48,54... | collective-permute-start | bytes 811016 | tf_op jit(solution)/shard_map/ppermute | solution.py:440
  26.5 1.5 %copy-start.4 = (f32[66,8,128]{2,1,0:T(8,128)}, f32[66,8,128]{2,1,0:T(8,128)S(1)}, u32[]{:S(2)}) copy-start(f32[66,8,128]{2,1,0:T(8,128)S(1)} %collective-permute-done.1.second) | copy-start | bytes 811012
  28.0 13.1 %copy-start.15 = (f32[96,8,128]{2,1,0:T(8,128)}, f32[96,8,128]{2,1,0:T(8,128)S(1)}, u32[]{:S(2)}) copy-start(f32[96,8,128]{2,1,0:T(8,128)S(1)} %get-tuple-element.10.strips) | copy-start | bytes 1179652
  28.1 28.4 %all-to-all-start = ((f32[6,13,8,128]{3,2,1,0:T(8,128)}), f32[6,13,8,128]{3,2,1,0:T(8,128)}, u32[]{:S(2)}, u32[]{:S(2)}) async-start(f32[6,13,8,128]{3,2,1,0:T(8,128)} %get-tuple-element.11), calls=%async_computation | async-start | bytes 638976 | tf_op jit(solution)/shard_map/all_to_all | solution.py:460
  41.1 1.0 %copy-start.5 = (f32[66,8,128]{2,1,0:T(8,128)S(1)}, f32[66,8,128]{2,1,0:T(8,128)}, u32[]{:S(2)}) copy-start(f32[66,8,128]{2,1,0:T(8,128)} %copy-done.4) | copy-start | bytes 811012
  42.1 0.7 copy-start.20
  45.4 1.4 %copy-start.2 = (bf16[3,528,768]{2,1,0:T(8,128)(2,1)}, bf16[3,528,768]{2,1,0:T(8,128)(2,1)S(1)}, u32[]{:S(2)}) copy-start(bf16[3,528,768]{2,1,0:T(8,128)(2,1)S(1)} %get-tuple-element.13.lo) | copy-start | bytes 7299076
  56.5 1.7 %copy-start.3 = (bf16[3,528,768]{2,1,0:T(8,128)(2,1)S(1)}, bf16[3,528,768]{2,1,0:T(8,128)(2,1)}, u32[]{:S(2)}) copy-start(bf16[3,528,768]{2,1,0:T(8,128)(2,1)} %copy-done.2) | copy-start | bytes 7299076
  58.2 1.0 %copy-start.6 = (f32[66,8,128]{2,1,0:T(8,128)S(1)}, f32[66,8,128]{2,1,0:T(8,128)}, u32[]{:S(2)}) copy-start(f32[66,8,128]{2,1,0:T(8,128)} %copy-done.4) | copy-start | bytes 811012
  59.1 0.8 %copy-start.14 = (f32[8,16,128]{2,1,0:T(8,128)S(1)}, f32[8,16,128]{2,1,0:T(8,128)}, u32[]{:S(2)}) copy-start(f32[8,16,128]{2,1,0:T(8,128)} %mu.5) | copy-start | bytes 196612
  60.0 1.0 %copy-start.16 = (f32[96,8,128]{2,1,0:T(8,128)S(1)}, f32[96,8,128]{2,1,0:T(8,128)}, u32[]{:S(2)}) copy-start(f32[96,8,128]{2,1,0:T(8,128)} %copy-done.15) | copy-start | bytes 1179652

commit v2 on v1

--- a/solution.py
+++ b/solution.py
@@ -18,12 +18,13 @@
 ]
 N_UP = len(UP_PLANES)
 UP_INDEX = {ft: i for i, ft in enumerate(UP_PLANES)}
+REST = [(f, t) for f in range(12) for t in range(DEPTH) if (f, t) not in UP_INDEX]
 STRIP = N_UP
-N_STRIP = 24
-MISC = STRIP + N_STRIP
+MISC = STRIP + (len(REST) + 3) // 4
 OCEAN = MISC + 1
 SEC_TILES = OCEAN + 16
-B_UP, B_FACTOR, B_SLAB, B_OCEAN, BLK_TILES = 0, 4, 6, 12, 13
+B_UP, B_FACTOR, B_SLAB, B_OCEAN, BLK_TILES = 0, 4, 6, 11, 12
+SPAN = 16
 F32 = jnp.float32
 BF16 = jnp.bfloat16
 VMEM = pl.BlockSpec(memory_space=pltpu.VMEM)
@@ -44,7 +45,15 @@
     return read
 
 
-def pack_kernel(slab, buo, lam, mu, ocean, depth, widths, first, second):
+def pack_kernel(*refs):
+    sources, widths, first, second = refs[:6], refs[6], refs[7], refs[8]
+    copies, sem = refs[9:15], refs[15]
+    moves = [pltpu.make_async_copy(a, c, sem.at[i]) for i, (a, c) in enumerate(zip(sources, copies))]
+    for move in moves:
+        move.start()
+    for move in moves:
+        move.wait()
+    slab, buo, lam, mu, ocean, depth = copies
     odd = lax.rem(lax.axis_index("sec"), 2)
     read = reader(slab, (buo, lam, mu))
     for out, lower in ((first, odd), (second, 1 - odd)):
@@ -52,8 +61,8 @@
         rows = pl.ds(start, 8)
         for i, (f, t) in enumerate(UP_PLANES):
             out[i] = read(f, t, rows)
-        for p in range(96):
-            f, t = p // 8, p % 8
+        out[MISC - 1] = jnp.zeros((8, LANES), F32)
+        for p, (f, t) in enumerate(REST):
             strip = jnp.where(lower == 1, read(f, t, slice(14, 16)), read(f, t, slice(0, 2)))
             out[STRIP + p // 4, 2 * (p % 4) : 2 * (p % 4) + 2, :] = strip
         out[MISC] = jnp.zeros((8, LANES), F32)
@@ -78,7 +87,7 @@
     return top, bottom
 
 
-def uplift_kernel(slab, buo, lam, mu, ocean, depth, first, second, send, strips):
+def uplift_kernel(slab, buo, lam, mu, ocean, depth, first, second, send, strips, windows):
     me = lax.axis_index("blk")
     read = reader(slab, (buo, lam, mu))
     top, bottom = sides(first, second)
@@ -182,27 +191,35 @@
     packed = jnp.where(lane[:16] < 64, factors[:16], pltpu.roll(factors[16:], 64, 1))
 
     tile = (8, LANES)
-    tlane = lane_iota(tile)
-    strips[...] = jnp.zeros((96, 8, LANES), F32)
+    tlane, trow = lane_iota(tile), row_iota(tile)
     odd = lax.rem(lax.axis_index("sec"), 2)
-    for p in range(96):
+    for i, (f, t) in enumerate(UP_PLANES):
+        strips[f, t] = jnp.where(trow < 2, bottom(i), jnp.where(trow >= 6, top(i), 0.0))
+    for p, (f, t) in enumerate(REST):
         i, at = STRIP + p // 4, slice(2 * (p % 4), 2 * (p % 4) + 2)
         a, c = first[i, at, :], second[i, at, :]
-        strips[p, 0:2, :] = jnp.where(odd == 0, c, a)
-        strips[p, 6:8, :] = jnp.where(odd == 0, a, c)
-    heads, tails = [], []
-    for r in range(3):
-        for half in range(2):
-            head, tail = jnp.zeros(tile, F32), jnp.zeros(tile, F32)
-            for t in range(4 * half, 4 * half + 4):
-                for f in range(12):
-                    at = 24 * (t % 4) + 2 * f
-                    x = read(f, t, slice(8 * r, 8 * r + 8)) if r < 2 else strips[f * 8 + t]
-                    x = pltpu.roll(x, at + 2, 1)
-                    tail = jnp.where((tlane >= at) & (tlane < at + 2), x, tail)
-                    head = jnp.where((tlane >= at + 2) & (tlane < at + 4), x, head)
-            heads.append(head)
-            tails.append(tail)
+        strips[f, t] = jnp.zeros(tile, F32)
+        strips[f, t, 0:2, :] = jnp.where(odd == 0, c, a)
+        strips[f, t, 6:8, :] = jnp.where(odd == 0, a, c)
+    heads = [jnp.zeros(tile, F32) for _ in range(5)]
+    tails = [jnp.zeros(tile, F32) for _ in range(5)]
+    spot = tlane % SPAN
+    for f in range(12):
+        for r in range(3):
+            near, far = jnp.zeros(tile, F32), jnp.zeros(tile, F32)
+            for t in range(DEPTH):
+                at = SPAN * t
+                x = read(f, t, slice(8 * r, 8 * r + 8)) if r < 2 else strips[f, t]
+                x = pltpu.roll(x, (at + 8) % LANES, 1)
+                near = jnp.where((tlane >= at + 8) & (tlane < at + 12), x, near)
+                far = jnp.where((tlane >= at + 4) & (tlane < at + 8), x, far)
+            windows[0, f, 8 * r : 8 * r + 8, :] = near
+            windows[1, f, 8 * r : 8 * r + 8, :] = far
+            i = f * 3 + r
+            k, at = i // 8, 2 * (i % 8)
+            here = (spot >= at) & (spot < at + 2)
+            heads[k] = jnp.where(here, pltpu.roll(near, (at - 8) % LANES, 1), heads[k])
+            tails[k] = jnp.where(here, pltpu.roll(far, (at - 6) % LANES, 1), tails[k])
     head, tail = jnp.zeros(tile, F32), jnp.zeros(tile, F32)
     for f in range(4):
         for r in range(4):
@@ -228,13 +245,16 @@
             send[d, B_UP + r] = rise[8 * r : 8 * r + 8]
         for r in range(2):
             send[d, B_FACTOR + r] = packed[8 * r : 8 * r + 8]
-        for i in range(7):
+        for i in range(6):
             send[d, B_SLAB + i] = jnp.where(d < me, heads[i], tails[i])
 
 
-def filter_kernel(face, widths, first, second, hi, lo):
+def middle_kernel(
+    slab, buo, lam, mu, ocean, depth, first, second, strips, face, widths, plain, seas, filters, cells, mats
+):
     me = lax.axis_index("blk")
     top, bottom = sides(first, second)
+    read = reader(slab, (buo, lam, mu))
     lane = lane_iota((1, LANES))
     face_at = (face[...] - me * COLS).astype(F32)
     width = face.shape[1]
@@ -253,8 +273,8 @@
         decay = jnp.exp2(distance * rate)
         value = decay / (1.0 + decay * decay) * gain
         upper = value.astype(BF16)
-        hi[k, rows, :] = upper
-        lo[k, rows, :] = (value - upper.astype(F32)).astype(BF16)
+        filters[rows, k * width : (k + 1) * width] = upper
+        filters[rows, (3 + k) * width : (4 + k) * width] = (value - upper.astype(F32)).astype(BF16)
 
     @pl.loop(0, COLS // 16)
     def _(c):
@@ -272,17 +292,84 @@
         gain = jnp.where(row < 8, groups[k][1][1], groups[k][2][1])
         put(k, slice(COLS, COLS + 16), distance, rate, gain)
 
-
-def final_kernel(
-    slab, buo, lam, mu, ocean, depth, first, second, strips, recv, hi, lo, slab_out, ocean_out, cells, mats, flat
-):
+    for f in range(4):
+        for k in range(4):
+            cols = slice(k * LANES, (k + 1) * LANES)
+            i = OCEAN + 4 * f + k
+            seas[f, 0:8, cols] = top(i)
+            seas[f, 8:24, cols] = ocean[f, :, cols] if f < 3 else depth[:, cols]
+            seas[f, 24:32, cols] = bottom(i)
+
+    for f in range(9):
+        for t in (0, DEPTH + 1):
+            cells[f, t] = jnp.zeros((24, LANES), F32)
+    for f in range(12):
+        for t in range(DEPTH):
+            if f < 9:
+                cells[f, t + 1, 0:R, :] = slab[f, t]
+                cells[f, t + 1, R:, :] = strips[f, t]
+            else:
+                mats[f - 9, t, 0:R, :] = (buo, lam, mu)[f - 9][t]
+                mats[f - 9, t, R:, :] = strips[f, t]
+    north = lambda v: pltpu.roll(v, 1, 0)
+    south = lambda v: pltpu.roll(v, 23, 0)
+    west = lambda v: pltpu.roll(v, 1, 1)
+    east = lambda v: pltpu.roll(v, LANES - 1, 1)
+    for step in range(2):
+
+        @pl.loop(1, DEPTH + 1)
+        def _(t):
+            s = [cells[3 + f, t] for f in range(6)]
+            below, above = cells[S11, t + 1], (cells[S12, t - 1], cells[S13, t - 1])
+            new = velocities([cells[a, t] for a in range(3)], s, Q * mats[0, t - 1], below, above, north, south, west, east)
+            for a in range(3):
+                cells[a, t] = new[a]
+
+        @pl.loop(1, DEPTH + 1)
+        def _(t):
+            v = [cells[a, t] for a in range(3)]
+            s = [cells[3 + f, t] for f in range(6)]
+            below, above = (cells[1, t + 1], cells[2, t + 1]), cells[0, t - 1]
+            new = stresses(s, v, Q * mats[1, t - 1], Q * mats[2, t - 1], below, above, north, south, west, east)
+            if step == 0:
+                for f in range(6):
+                    cells[3 + f, t] = new[f]
+            else:
+                for f, x in enumerate(v + new):
+                    plain[f, t - 1] = x[0:R]
+
+
+def velocities(v, s, qb, s11_below, above, north, south, west, east):
+    s11, s22, s33, s23, s13, s12 = s
+    return [
+        v[0] + qb * (s11_below - s11 + (s12 - north(s12)) + (s13 - west(s13))),
+        v[1] + qb * (south(s22) - s22 + (s12 - above[0]) + (s23 - west(s23))),
+        v[2] + qb * (east(s33) - s33 + (s13 - above[1]) + (s23 - north(s23))),
+    ]
+
+
+def stresses(s, v, la, m, below, v1_above, north, south, west, east):
+    v1, v2, v3 = v
+    d1, d2, d3 = v1 - v1_above, v2 - north(v2), v3 - west(v3)
+    dil = la * (d1 + d2 + d3)
+    m2 = 2.0 * m
+    return [
+        s[0] + (dil + m2 * d1),
+        s[1] + (dil + m2 * d2),
+        s[2] + (dil + m2 * d3),
+        s[3] + m * (east(v2) - v2 + (south(v3) - v3)),
+        s[4] + m * (east(v1) - v1 + (below[1] - v3)),
+        s[5] + m * (south(v1) - v1 + (below[0] - v2)),
+    ]
+
+
+def final_kernel(plain, seas, filters, windows, recv, slab_out, ocean_out, flat):
     sec, me = lax.axis_index("sec"), lax.axis_index("blk")
     n_sec, n_blk = lax.axis_size("sec"), lax.axis_size("blk")
-    read = reader(slab, (buo, lam, mu))
-    top, bottom = sides(first, second)
     shape = (32, LANES)
-    lane = lane_iota(shape)
+    lane, row = lane_iota(shape), row_iota(shape)
     before, after = jnp.maximum(me - 1, 0), jnp.minimum(me + 1, n_blk - 1)
+    west_on, east_on = me > 0, me < n_blk - 1
     tile = (8, LANES)
     tlane = lane_iota(tile)
 
@@ -297,44 +384,35 @@
         rises[j] = rises[j] + jnp.where(lane == LANES - 1, pick(0, 4), 0.0)
         rises[j + 1] = rises[j + 1] + jnp.where(lane == 0, pick(4, 21), 0.0) + jnp.where(lane == 1, pick(21, 22), 0.0)
     rise = jnp.concatenate(rises, axis=1)
-    rise_hi = rise.astype(BF16)
-    rise_lo = (rise - rise_hi.astype(F32)).astype(BF16)
-
-    def dot(a, c):
-        return lax.dot_general(a, c, (((1,), (1,)), ((), ())), preferred_element_type=F32)
-
-    source = None
-    col = lane_iota((COLS + 16, 32))
+    rise_hi = rise.astype(BF16).astype(F32)
+    rise_lo = rise - rise_hi
+    wide = row_iota(rise.shape)
+    upper, lower = [], []
     for k in range(3):
-        a = hi[k]
-        part = dot(a, rise_hi) + dot(a, rise_lo) + dot(lo[k], rise_hi)
-        source = part if k == 0 else jnp.where(col >= (0, 8, 24)[k], part, source)
+        mine = (wide >= (0, 8, 24)[k]) & (wide < (8, 24, 32)[k])
+        part = jnp.where(mine, rise_hi, 0.0)
+        upper.append(jnp.concatenate([part, jnp.where(mine, rise_lo, 0.0)], axis=0))
+        lower.append(jnp.concatenate([part, jnp.zeros_like(part)], axis=0))
+    both = jnp.concatenate(upper + lower, axis=1).astype(BF16)
+    source = lax.dot_general(filters[...], both, (((1,), (1,)), ((), ())), preferred_element_type=F32)
     flat[...] = jnp.zeros((5 * LANES, LANES), F32)
-    flat[0 : COLS + 8, 0:32] = source[0 : COLS + 8]
-    flat[5 * LANES - 8 : 5 * LANES, 0:32] = source[COLS + 8 : COLS + 16]
-    source = jnp.concatenate(
-        [flat[k * LANES : (k + 1) * LANES, :].T[0:32] for k in range(5)], axis=1
-    )
+    flat[0 : COLS + 8, 0:64] = source[0 : COLS + 8]
+    flat[5 * LANES - 8 : 5 * LANES, 0:64] = source[COLS + 8 : COLS + 16]
+    turned = [flat[k * LANES : (k + 1) * LANES, :].T for k in range(5)]
+    source = jnp.concatenate([x[0:32] + x[32:64] for x in turned], axis=1)
 
     ring = (32, 5 * LANES)
-    seas = []
+    fields = []
     for f in range(4):
-        tiles = []
-        for k in range(4):
-            cols = slice(k * LANES, (k + 1) * LANES)
-            own = ocean[f, :, cols] if f < 3 else depth[:, cols]
-            i = OCEAN + 4 * f + k
-            tiles.append(jnp.concatenate([top(i), own, bottom(i)], axis=0))
         halo = []
         for r in range(4):
             at = 32 * f + 8 * r
             east_in = pltpu.roll(recv[after, B_OCEAN], (LANES - at) % LANES, 1)
             west_in = pltpu.roll(recv[before, B_OCEAN], (2 * LANES - 8 - at) % LANES, 1)
-            x = jnp.where((tlane < 8) & (me < n_blk - 1), east_in, 0.0)
-            halo.append(jnp.where((tlane >= LANES - 8) & (me > 0), west_in, x))
-        tiles.append(jnp.concatenate(halo, axis=0))
-        seas.append(jnp.concatenate(tiles, axis=1))
-    surface, strike, dip, water = seas
+            x = jnp.where((tlane < 8) & east_on, east_in, 0.0)
+            halo.append(jnp.where((tlane >= LANES - 8) & west_on, west_in, x))
+        fields.append(jnp.concatenate([seas[f], jnp.concatenate(halo, axis=0)], axis=1))
+    surface, strike, dip, water = fields
     at = lane_iota(ring)
     at = jnp.where(at >= 5 * LANES - 8, at - 5 * LANES, at)
     x, y = row_iota(ring) - 8 + sec * R, at + me * COLS
@@ -351,84 +429,54 @@
     ocean_out[1] = strike[8:24, 0:COLS]
     ocean_out[2] = dip[8:24, 0:COLS]
 
-    for f in range(9):
-        for t in (0, DEPTH + 1):
-            cells[f, t] = jnp.zeros((24, 2 * LANES), F32)
-    west_on, east_on = me > 0, me < n_blk - 1
-    for r in range(3):
-        rows = slice(8 * r, 8 * r + 8)
-        for half in range(2):
-            i = B_SLAB + 2 * r + half
-            east_in = jnp.where(east_on, recv[after, i], 0.0)
-            west_in = jnp.where(west_on, recv[before, i], 0.0)
-            for t in range(4 * half, 4 * half + 4):
-                for f in range(12):
-                    at = 24 * (t % 4) + 2 * f
-                    edge = jnp.where(tlane < at + 2, west_in, east_in)
-                    edge = pltpu.roll(edge, LANES - at - 2, 1)
-                    own = read(f, t, rows) if r < 2 else strips[f * 8 + t]
-                    if f < 9:
-                        cells[f, t + 1, rows, 0:LANES] = own
-                        cells[f, t + 1, rows, LANES:] = edge
-                    else:
-                        mats[f - 9, t, rows, 0:LANES] = own
-                        mats[f - 9, t, rows, LANES:] = edge
-
+    spot = tlane % SPAN
     north = lambda v: pltpu.roll(v, 1, 0)
     south = lambda v: pltpu.roll(v, 23, 0)
     west = lambda v: pltpu.roll(v, 1, 1)
-    east = lambda v: pltpu.roll(v, 2 * LANES - 1, 1)
-    for step in range(2):
-
-        @pl.loop(1, DEPTH + 1)
-        def _(t):
-            qb = Q * mats[0, t - 1]
-            s12, s13, s23 = cells[S12, t], cells[S13, t], cells[S23, t]
-            s11, s22, s33 = cells[S11, t], cells[S22, t], cells[S33, t]
-            cells[0, t] = cells[0, t] + qb * (
-                cells[S11, t + 1] - s11 + (s12 - north(s12)) + (s13 - west(s13))
-            )
-            cells[1, t] = cells[1, t] + qb * (
-                south(s22) - s22 + (s12 - cells[S12, t - 1]) + (s23 - west(s23))
-            )
-            cells[2, t] = cells[2, t] + qb * (
-                east(s33) - s33 + (s13 - cells[S13, t - 1]) + (s23 - north(s23))
-            )
-
-        @pl.loop(1, DEPTH + 1)
-        def _(t):
-            la, m = Q * mats[1, t - 1], Q * mats[2, t - 1]
-            v1, v2, v3 = cells[0, t], cells[1, t], cells[2, t]
-            d1, d2, d3 = v1 - cells[0, t - 1], v2 - north(v2), v3 - west(v3)
-            dil = la * (d1 + d2 + d3)
-            m2 = 2.0 * m
-            new = [
-                cells[S11, t] + (dil + m2 * d1),
-                cells[S22, t] + (dil + m2 * d2),
-                cells[S33, t] + (dil + m2 * d3),
-                cells[S23, t] + m * (east(v2) - v2 + (south(v3) - v3)),
-                cells[S13, t] + m * (east(v1) - v1 + (cells[2, t + 1] - v3)),
-                cells[S12, t] + m * (south(v1) - v1 + (cells[1, t + 1] - v2)),
-            ]
-            if step == 0:
-                for f, x in enumerate(new):
-                    cells[3 + f, t] = x
-            else:
-                for f, x in enumerate([v1, v2, v3] + new):
-                    slab_out[f, t - 1] = x[0:R, 0:LANES]
-
-
-def call(kernel, out_shape, flops, *args, scratch=()):
+    east = lambda v: pltpu.roll(v, LANES - 1, 1)
+    wlane = lane_iota((24, LANES))
+    above = lambda v: jnp.where(wlane < SPAN, 0.0, pltpu.roll(v, SPAN, 1))
+    below = lambda v: jnp.where(wlane >= LANES - SPAN, 0.0, pltpu.roll(v, LANES - SPAN, 1))
+    results = []
+    for side in range(2):
+        other, on, home = ((before, west_on, 6), (after, east_on, 8))[side]
+        here = (spot >= home) & (spot < home + 2)
+        state = []
+        for f in range(12):
+            parts = []
+            for r in range(3):
+                i = f * 3 + r
+                x = pltpu.roll(recv[other, B_SLAB + i // 8], (home - 2 * (i % 8)) % LANES, 1)
+                own = windows[side, f, 8 * r : 8 * r + 8, :]
+                parts.append(jnp.where(here & on, x, own))
+            state.append(jnp.concatenate(parts, axis=0))
+        v, s = state[0:3], state[3:9]
+        qb, la, m = Q * state[BUO], Q * state[LAM], Q * state[MU]
+        for step in range(2):
+            v = velocities(v, s, qb, below(s[0]), (above(s[5]), above(s[4])), north, south, west, east)
+            s = stresses(s, v, la, m, (below(v[1]), below(v[2])), above(v[0]), north, south, west, east)
+        results.append(v + s)
+    edge = (tlane < 2) | (tlane >= LANES - 2)
+    for f in range(9):
+        for r in range(2):
+            rows = slice(8 * r, 8 * r + 8)
+            both = jnp.where(spot >= 8, results[0][f][rows], results[1][f][rows])
+            for t in range(DEPTH):
+                moved = pltpu.roll(both, (2 * LANES - SPAN * t - 8) % LANES, 1)
+                slab_out[f, t, rows, :] = jnp.where(edge, moved, plain[f, t, rows, :])
+
+
+def call(kernel, out_shape, flops, *args, far=0, scratch=()):
     many = isinstance(out_shape, (list, tuple))
     outs = list(out_shape) if many else [out_shape]
     n_bytes = sum(a.size * a.dtype.itemsize for a in args) + sum(math.prod(o.shape) * o.dtype.itemsize for o in outs)
     return pl.pallas_call(
         kernel,
         out_shape=out_shape,
-        in_specs=[VMEM] * len(args),
+        in_specs=[pl.BlockSpec(memory_space=pltpu.HBM)] * far + [VMEM] * (len(args) - far),
         out_specs=[VMEM] * len(outs) if many else VMEM,
         scratch_shapes=scratch,
-        compiler_params=pltpu.CompilerParams(vmem_limit_bytes=40 * 1024 * 1024),
+        compiler_params=pltpu.CompilerParams(vmem_limit_bytes=12 * 1024 * 1024),
         cost_estimate=pl.CostEstimate(flops=flops, bytes_accessed=n_bytes, transcendentals=0),
     )(*args)
 
@@ -446,38 +494,59 @@
     arr = jax.ShapeDtypeStruct
     own = (slab_state, buoyancy, lame_lambda, lame_mu, ocean_state, water_depth)
     message = arr((SEC_TILES, 8, LANES), F32)
-    first, second = call(pack_kernel, (message, message), 10**6, *own, band_widths)
+    first, second = call(
+        pack_kernel,
+        (message, message),
+        10**6,
+        *own,
+        band_widths,
+        far=6,
+        scratch=[pltpu.VMEM(a.shape, F32) for a in own] + [pltpu.SemaphoreType.DMA((6,))],
+    )
     first = swap(first, "sec", 1)
     second = swap(second, "sec", 0)
-    send, strips = call(
+    send, strips, windows = call(
         uplift_kernel,
-        (arr((n_blk, BLK_TILES, 8, LANES), F32), arr((96, 8, LANES), F32)),
+        (
+            arr((n_blk, BLK_TILES, 8, LANES), F32),
+            arr((12, DEPTH, 8, LANES), F32),
+            arr((2, 12, 24, LANES), F32),
+        ),
         10**7,
         *own,
         first,
         second,
     )
     recv = lax.all_to_all(send, "blk", 0, 0, tiled=True)
-    kernels = arr((3, COLS + 16, n_face), BF16)
-    hi, lo = call(
-        filter_kernel, (kernels, kernels), 10**8, face_map.reshape(1, n_face), band_widths, first, second
+    plain, seas, filters = call(
+        middle_kernel,
+        (
+            arr(slab_state.shape, F32),
+            arr((4, 32, COLS), F32),
+            arr((COLS + 16, 6 * n_face), BF16),
+        ),
+        10**8,
+        *own,
+        first,
+        second,
+        strips,
+        face_map.reshape(1, n_face),
+        band_widths,
+        scratch=[
+            pltpu.VMEM((9, DEPTH + 2, 24, LANES), F32),
+            pltpu.VMEM((3, DEPTH, 24, LANES), F32),
+        ],
     )
     return call(
         final_kernel,
         (arr(slab_state.shape, F32), arr(ocean_state.shape, F32)),
         10**8,
-        *own,
-        first,
-        second,
-        strips,
+        plain,
+        seas,
+        filters,
+        windows,
         recv,
-        hi,
-        lo,
-        scratch=[
-            pltpu.VMEM((9, DEPTH + 2, 24, 2 * LANES), F32),
-            pltpu.VMEM((3, DEPTH, 24, 2 * LANES), F32),
-            pltpu.VMEM((5 * LANES, LANES), F32),
-        ],
+        scratch=[pltpu.VMEM((5 * LANES, LANES), F32)],
     )
 
 

time: 69.8 us -> 63.9 us (0.915)
  waiting for transfers between devices: 16.7 us -> 6.47 us
  local copies, waits for them, and re-layouts: 13.4 us -> 17 us
  Pallas kernels: 12.2 us -> 13.1 us
    all_to_all x1, waiting for transfers between devices: 9.68 us -> 0.01 us  [on_device(): recv = lax.all_to_all(send, 'blk', 0, 0, tiled=True)]
    unnamed x44 -> x32, local copies, waits for them, and re-layouts: 13.4 us -> 16.3 us
    pallas_call x4, Pallas kernels: 12.2 us -> 13.1 us  [call(): pl.pallas_call(kernel, out_shape=out_shape, in_specs=[pl.BlockSpec(memory...]
  transfers between devices with their start and end apart: 3 -> 3, of which waited for: 3 -> 2; matrix products, arithmetic and copies ran while one was open for 0% -> 1% of each run, Pallas kernels for 4% -> 8%
where the time goes in v2:
time: 63.9 us; the launch traced here: 63 us
  starting transfers between devices  25.8 us (40%)
  local copies, waits for them, and re-layouts  17 us (27%)
  Pallas kernels  13.1 us (21%)
  waiting for transfers between devices  6.47 us (10%)
  between operations  0.69 us (1%)
    unnamed x32, local copies, waits for them, and re-layouts  16.3 us
    all_to_all x1, starting transfers between devices, on_device(): recv = lax.all_to_all(send, 'blk', 0, 0, tiled=True)  13.1 us
    pallas_call x4, Pallas kernels, call(): pl.pallas_call(kernel, out_shape=out_shape, in_specs=[pl.BlockSpec(memory...  13.1 us
    ppermute x2, starting transfers between devices, swap(): return lax.ppermute(x, axis, pairs)  12.7 us
    ppermute x2, waiting for transfers between devices, swap(): return lax.ppermute(x, axis, pairs)  6.47 us
  transfers between devices with their start and end apart: 3, of which 2 were waited for; matrix products, arithmetic and copies ran while one was open for 1% of the time, Pallas kernels for 8%

profile of v2, /device:TPU:7, one launch (start us, length us, event | category | flops | bytes accessed | tf_op | source)
XLA Modules:
  0.0 63.0 jit_solution(6474046362211228133)
XLA Ops:
  0.6 0.0 copy-start
  0.6 1.1 %copy-done = f32[9,8,16,128]{3,2,1,0:T(8,128)S(1)} copy-done((f32[9,8,16,128]{3,2,1,0:T(8,128)S(1)}, f32[9,8,16,128]{3,2,1,0:T(8,128)}, u32[]{:S(2)}) %copy-start) | copy-done | bytes 589848
  1.7 0.0 copy-start.4
  1.7 0.9 %copy-done.4 = f32[3,16,512]{2,1,0:T(8,128)S(1)} copy-done((f32[3,16,512]{2,1,0:T(8,128)S(1)}, f32[3,16,512]{2,1,0:T(8,128)}, u32[]{:S(2)}) %copy-start.4) | copy-done | bytes 98328
  2.6 0.0 copy-start.6
  2.6 0.8 %copy-done.6 = f32[8,16,128]{2,1,0:T(8,128)S(1)} copy-done((f32[8,16,128]{2,1,0:T(8,128)S(1)}, f32[8,16,128]{2,1,0:T(8,128)}, u32[]{:S(2)}) %copy-start.6) | copy-done | bytes 65560
  3.4 0.0 copy-start.8
  3.4 0.8 %copy-done.8 = f32[8,16,128]{2,1,0:T(8,128)S(1)} copy-done((f32[8,16,128]{2,1,0:T(8,128)S(1)}, f32[8,16,128]{2,1,0:T(8,128)}, u32[]{:S(2)}) %copy-start.8) | copy-done | bytes 65560
  4.3 0.0 copy-start.10
  4.3 0.8 %copy-done.10 = f32[8,16,128]{2,1,0:T(8,128)S(1)} copy-done((f32[8,16,128]{2,1,0:T(8,128)S(1)}, f32[8,16,128]{2,1,0:T(8,128)}, u32[]{:S(2)}) %copy-start.10) | copy-done | bytes 65560
  5.1 0.0 copy-start.12
  5.1 0.8 %copy-done.12 = f32[16,512]{1,0:T(8,128)S(1)} copy-done((f32[16,512]{1,0:T(8,128)S(1)}, f32[16,512]{1,0:T(8,128)}, u32[]{:S(2)}) %copy-start.12) | copy-done | bytes 32792
  5.9 0.0 copy-start.14
  5.9 0.7 %copy-done.14 = s32[1,6]{1,0:T(1,128)S(1)} copy-done((s32[1,6]{1,0:T(1,128)S(1)}, s32[1,6]{1,0:T(1,128)}, u32[]{:S(2)}) %copy-start.14) | copy-done | bytes 48
  6.5 0.7 %shard_map.95 = (f32[60,8,128]{2,1,0:T(8,128)S(1)}, f32[60,8,128]{2,1,0:T(8,128)S(1)}) custom-call(f32[9,8,16,128]{3,2,1,0:T(8,128)S(1)} %copy-done, f32[8,16,128]{2,1,0:T(8,128)S(1)} %copy-done.6, f32[8,16,128]{2,1,0:T(8,128)S(1)} %copy-done.8, f32[8,16,128]{2,1,0:T(8,128)S(1)} %copy-done.10, f32[3,16,512]{2,1,0:T(8,128)S(1)} %copy-done.4, ...), custom_call_target="tpu_custom_call" | custom-call | flops 1000000 | bytes 1409048 | tf_op jit(solution)/shard_map/pallas_call | solution.py:473
  7.2 10.8 %collective-permute-start = (f32[60,8,128]{2,1,0:T(8,128)S(1)}, f32[60,8,128]{2,1,0:T(8,128)S(1)}, u32[]{:S(2)}, u32[]{:S(2)}) collective-permute-start(f32[60,8,128]{2,1,0:T(8,128)S(1)} %get-tuple-element.10), channel_id=1, source_target_pairs={{6,12},{12,6},{18,24},{24,18},{30,36},{36,30},{42,48},{48,42},{54,... | collective-permute-start | bytes 737288 | tf_op jit(solution)/shard_map/ppermute | solution.py:488
  18.0 1.9 %collective-permute-start.1 = (f32[60,8,128]{2,1,0:T(8,128)S(1)}, f32[60,8,128]{2,1,0:T(8,128)S(1)}, u32[]{:S(2)}, u32[]{:S(2)}) collective-permute-start(f32[60,8,128]{2,1,0:T(8,128)S(1)} %get-tuple-element.11), channel_id=1, source_target_pairs={{0,6},{6,0},{12,18},{18,12},{24,30},{30,24},{36,42},{42,36},{48,54... | collective-permute-start | bytes 737288 | tf_op jit(solution)/shard_map/ppermute | solution.py:488
  19.9 3.7 %collective-permute-done.first = f32[60,8,128]{2,1,0:T(8,128)S(1)} collective-permute-done((f32[60,8,128]{2,1,0:T(8,128)S(1)}, f32[60,8,128]{2,1,0:T(8,128)S(1)}, u32[]{:S(2)}, u32[]{:S(2)}) %collective-permute-start) | collective-permute-done | bytes 245792 | tf_op jit(solution)/shard_map/ppermute | solution.py:488
  23.7 2.7 %collective-permute-done.1.second = f32[60,8,128]{2,1,0:T(8,128)S(1)} collective-permute-done((f32[60,8,128]{2,1,0:T(8,128)S(1)}, f32[60,8,128]{2,1,0:T(8,128)S(1)}, u32[]{:S(2)}, u32[]{:S(2)}) %collective-permute-start.1) | collective-permute-done | bytes 245792 | tf_op jit(solution)/shard_map/ppermute | solution.py:488
  26.4 3.6 %shard_map.96 = (f32[6,12,8,128]{3,2,1,0:T(8,128)}, f32[12,8,8,128]{3,2,1,0:T(8,128)S(1)}, f32[2,12,24,128]{3,2,1,0:T(8,128)S(1)}) custom-call(f32[9,8,16,128]{3,2,1,0:T(8,128)S(1)} %copy-done, f32[8,16,128]{2,1,0:T(8,128)S(1)} %copy-done.6, f32[8,16,128]{2,1,0:T(8,128)S(1)} %copy-done.8, f32[8,16,128]{2,1,0:T(8,128)S(1)} %copy-done.10, ...), custom_call_target="tpu_custom_call" | custom-call | flops 10000000 | bytes 2392064 | tf_op jit(solution)/shard_map/pallas_call | solution.py:473
  30.0 13.1 %all-to-all-start = ((f32[6,12,8,128]{3,2,1,0:T(8,128)}), f32[6,12,8,128]{3,2,1,0:T(8,128)S(1)}, u32[]{:S(2)}, u32[]{:S(2)}) async-start(f32[6,12,8,128]{3,2,1,0:T(8,128)} %get-tuple-element.17), calls=%async_computation | async-start | bytes 589824 | tf_op jit(solution)/shard_map/all_to_all | solution.py:520
  43.1 0.7 %reshape.7.face = s32[1,768]{1,0:T(1,128)S(1)} reshape(s32[768]{0:T(1024)} %param.12) | data formatting | bytes 6144 | tf_op jit(solution)/shard_map/reshape | solution.py:533
  43.8 0.0 copy-start.1
  43.8 1.1 %copy-done.1 = f32[9,8,16,128]{3,2,1,0:T(8,128)S(1)} copy-done((f32[9,8,16,128]{3,2,1,0:T(8,128)S(1)}, f32[9,8,16,128]{3,2,1,0:T(8,128)}, u32[]{:S(2)}) %copy-start.1) | copy-done | bytes 589848
  44.9 0.0 copy-start.5
  44.9 0.9 %copy-done.5 = f32[3,16,512]{2,1,0:T(8,128)S(1)} copy-done((f32[3,16,512]{2,1,0:T(8,128)S(1)}, f32[3,16,512]{2,1,0:T(8,128)}, u32[]{:S(2)}) %copy-start.5) | copy-done | bytes 98328
  45.8 0.0 copy-start.7
  45.8 0.8 %copy-done.7 = f32[8,16,128]{2,1,0:T(8,128)S(1)} copy-done((f32[8,16,128]{2,1,0:T(8,128)S(1)}, f32[8,16,128]{2,1,0:T(8,128)}, u32[]{:S(2)}) %copy-start.7) | copy-done | bytes 65560
  46.6 0.0 copy-start.9
  46.6 0.8 %copy-done.9 = f32[8,16,128]{2,1,0:T(8,128)S(1)} copy-done((f32[8,16,128]{2,1,0:T(8,128)S(1)}, f32[8,16,128]{2,1,0:T(8,128)}, u32[]{:S(2)}) %copy-start.9) | copy-done | bytes 65560
  47.4 0.0 copy-start.11
  47.4 0.8 %copy-done.11 = f32[8,16,128]{2,1,0:T(8,128)S(1)} copy-done((f32[8,16,128]{2,1,0:T(8,128)S(1)}, f32[8,16,128]{2,1,0:T(8,128)}, u32[]{:S(2)}) %copy-start.11) | copy-done | bytes 65560
  48.3 0.0 copy-start.13
  48.3 0.8 %copy-done.13 = f32[16,512]{1,0:T(8,128)S(1)} copy-done((f32[16,512]{1,0:T(8,128)S(1)}, f32[16,512]{1,0:T(8,128)}, u32[]{:S(2)}) %copy-start.13) | copy-done | bytes 32792
  49.0 0.0 copy-start.15
  49.0 0.7 %copy-done.15 = s32[1,6]{1,0:T(1,128)S(1)} copy-done((s32[1,6]{1,0:T(1,128)S(1)}, s32[1,6]{1,0:T(1,128)}, u32[]{:S(2)}) %copy-start.15) | copy-done | bytes 48
  49.7 5.2 %shard_map.97 = (f32[9,8,16,128]{3,2,1,0:T(8,128)S(1)}, f32[4,32,512]{2,1,0:T(8,128)S(1)}, bf16[528,4608]{1,0:T(8,128)(2,1)S(1)}) custom-call(f32[9,8,16,128]{3,2,1,0:T(8,128)S(1)} %copy-done.1, f32[8,16,128]{2,1,0:T(8,128)S(1)} %copy-done.7, f32[8,16,128]{2,1,0:T(8,128)S(1)} %copy-done.9, f32[8,16,128]{2,1,0:T(8,128)S(1)} %copy-done.11, ...), custom_call_target="tpu_custom_call" | custom-call | flops 100000000 | bytes 7523352 | tf_op jit(solution)/shard_map/pallas_call | solution.py:473
  54.9 0.0 copy-start.2
  55.0 2.2 %copy-done.2 = bf16[528,4608]{1,0:T(8,128)(2,1)} copy-done((bf16[528,4608]{1,0:T(8,128)(2,1)}, bf16[528,4608]{1,0:T(8,128)(2,1)S(1)}, u32[]{:S(2)}) %copy-start.2) | copy-done | bytes 4866072
  57.1 0.0 all-to-all-done.recv
  57.1 0.0 copy-start.3
  57.2 2.4 %copy-done.3 = bf16[528,4608]{1,0:T(8,128)(2,1)S(1)} copy-done((bf16[528,4608]{1,0:T(8,128)(2,1)S(1)}, bf16[528,4608]{1,0:T(8,128)(2,1)}, u32[]{:S(2)}) %copy-start.3) | copy-done | bytes 4866072
  59.5 3.5 %shard_map.98 = (f32[9,8,16,128]{3,2,1,0:T(8,128)}, f32[3,16,512]{2,1,0:T(8,128)}) custom-call(f32[9,8,16,128]{3,2,1,0:T(8,128)S(1)} %get-tuple-element.13.plain, f32[4,32,512]{2,1,0:T(8,128)S(1)} %get-tuple-element.14.seas, bf16[528,4608]{1,0:T(8,128)(2,1)S(1)} %copy-done.3, f32[2,12,24,128]{3,2,1,0:T(8,128)S(1)} %get-tuple-element.16.windows, ...), custom_call_target="tpu_custom_call" | custom-call | flops 100000000 | bytes 6995968 | tf_op jit(solution)/shard_map/pallas_call | solution.py:473
Async XLA Ops:
  0.6 1.1 %copy-start = (f32[9,8,16,128]{3,2,1,0:T(8,128)S(1)}, f32[9,8,16,128]{3,2,1,0:T(8,128)}, u32[]{:S(2)}) copy-start(f32[9,8,16,128]{3,2,1,0:T(8,128)} %slab.3) | copy-start | bytes 1769476
  1.7 0.9 %copy-start.4 = (f32[3,16,512]{2,1,0:T(8,128)S(1)}, f32[3,16,512]{2,1,0:T(8,128)}, u32[]{:S(2)}) copy-start(f32[3,16,512]{2,1,0:T(8,128)} %ocean.3) | copy-start | bytes 294916
  2.6 0.8 %copy-start.6 = (f32[8,16,128]{2,1,0:T(8,128)S(1)}, f32[8,16,128]{2,1,0:T(8,128)}, u32[]{:S(2)}) copy-start(f32[8,16,128]{2,1,0:T(8,128)} %buo.3) | copy-start | bytes 196612
  3.4 0.8 %copy-start.8 = (f32[8,16,128]{2,1,0:T(8,128)S(1)}, f32[8,16,128]{2,1,0:T(8,128)}, u32[]{:S(2)}) copy-start(f32[8,16,128]{2,1,0:T(8,128)} %lam.3) | copy-start | bytes 196612
  4.3 0.8 %copy-start.10 = (f32[8,16,128]{2,1,0:T(8,128)S(1)}, f32[8,16,128]{2,1,0:T(8,128)}, u32[]{:S(2)}) copy-start(f32[8,16,128]{2,1,0:T(8,128)} %mu.3) | copy-start | bytes 196612
  5.1 0.8 %copy-start.12 = (f32[16,512]{1,0:T(8,128)S(1)}, f32[16,512]{1,0:T(8,128)}, u32[]{:S(2)}) copy-start(f32[16,512]{1,0:T(8,128)} %depth.3) | copy-start | bytes 98308
  5.9 0.7 %copy-start.14 = (s32[1,6]{1,0:T(1,128)S(1)}, s32[1,6]{1,0:T(1,128)}, u32[]{:S(2)}) copy-start(s32[1,6]{1,0:T(1,128)} %widths.1) | copy-start | bytes 76
  7.2 16.5 %collective-permute-start = (f32[60,8,128]{2,1,0:T(8,128)S(1)}, f32[60,8,128]{2,1,0:T(8,128)S(1)}, u32[]{:S(2)}, u32[]{:S(2)}) collective-permute-start(f32[60,8,128]{2,1,0:T(8,128)S(1)} %get-tuple-element.10), channel_id=1, source_target_pairs={{6,12},{12,6},{18,24},{24,18},{30,36},{36,30},{42,48},{48,42},{54,... | collective-permute-start | bytes 737288 | tf_op jit(solution)/shard_map/ppermute | solution.py:488
  18.0 8.4 %collective-permute-start.1 = (f32[60,8,128]{2,1,0:T(8,128)S(1)}, f32[60,8,128]{2,1,0:T(8,128)S(1)}, u32[]{:S(2)}, u32[]{:S(2)}) collective-permute-start(f32[60,8,128]{2,1,0:T(8,128)S(1)} %get-tuple-element.11), channel_id=1, source_target_pairs={{0,6},{6,0},{12,18},{18,12},{24,30},{30,24},{36,42},{42,36},{48,54... | collective-permute-start | bytes 737288 | tf_op jit(solution)/shard_map/ppermute | solution.py:488
  30.0 27.1 %all-to-all-start = ((f32[6,12,8,128]{3,2,1,0:T(8,128)}), f32[6,12,8,128]{3,2,1,0:T(8,128)S(1)}, u32[]{:S(2)}, u32[]{:S(2)}) async-start(f32[6,12,8,128]{3,2,1,0:T(8,128)} %get-tuple-element.17), calls=%async_computation | async-start | bytes 589824 | tf_op jit(solution)/shard_map/all_to_all | solution.py:520
  43.8 1.1 %copy-start.1 = (f32[9,8,16,128]{3,2,1,0:T(8,128)S(1)}, f32[9,8,16,128]{3,2,1,0:T(8,128)}, u32[]{:S(2)}) copy-start(f32[9,8,16,128]{3,2,1,0:T(8,128)} %slab.3) | copy-start | bytes 1769476
  44.9 0.9 %copy-start.5 = (f32[3,16,512]{2,1,0:T(8,128)S(1)}, f32[3,16,512]{2,1,0:T(8,128)}, u32[]{:S(2)}) copy-start(f32[3,16,512]{2,1,0:T(8,128)} %ocean.3) | copy-start | bytes 294916
  45.8 0.8 %copy-start.7 = (f32[8,16,128]{2,1,0:T(8,128)S(1)}, f32[8,16,128]{2,1,0:T(8,128)}, u32[]{:S(2)}) copy-start(f32[8,16,128]{2,1,0:T(8,128)} %buo.3) | copy-start | bytes 196612
  46.6 0.8 %copy-start.9 = (f32[8,16,128]{2,1,0:T(8,128)S(1)}, f32[8,16,128]{2,1,0:T(8,128)}, u32[]{:S(2)}) copy-start(f32[8,16,128]{2,1,0:T(8,128)} %lam.3) | copy-start | bytes 196612
  47.4 0.8 %copy-start.11 = (f32[8,16,128]{2,1,0:T(8,128)S(1)}, f32[8,16,128]{2,1,0:T(8,128)}, u32[]{:S(2)}) copy-start(f32[8,16,128]{2,1,0:T(8,128)} %mu.3) | copy-start | bytes 196612
  48.3 0.8 %copy-start.13 = (f32[16,512]{1,0:T(8,128)S(1)}, f32[16,512]{1,0:T(8,128)}, u32[]{:S(2)}) copy-start(f32[16,512]{1,0:T(8,128)} %depth.3) | copy-start | bytes 98308
  49.0 0.7 %copy-start.15 = (s32[1,6]{1,0:T(1,128)S(1)}, s32[1,6]{1,0:T(1,128)}, u32[]{:S(2)}) copy-start(s32[1,6]{1,0:T(1,128)} %widths.1) | copy-start | bytes 76
  54.9 2.2 %copy-start.2 = (bf16[528,4608]{1,0:T(8,128)(2,1)}, bf16[528,4608]{1,0:T(8,128)(2,1)S(1)}, u32[]{:S(2)}) copy-start(bf16[528,4608]{1,0:T(8,128)(2,1)S(1)} %get-tuple-element.15.filters) | copy-start | bytes 14598148
  57.1 2.4 %copy-start.3 = (bf16[528,4608]{1,0:T(8,128)(2,1)S(1)}, bf16[528,4608]{1,0:T(8,128)(2,1)}, u32[]{:S(2)}) copy-start(bf16[528,4608]{1,0:T(8,128)(2,1)} %copy-done.2) | copy-start | bytes 14598148

commit v3 on v2

--- a/solution.py
+++ b/solution.py
@@ -26,6 +26,7 @@
 B_UP, B_FACTOR, B_SLAB, B_OCEAN, BLK_TILES = 0, 4, 6, 11, 12
 SPAN = 16
 F32 = jnp.float32
+MIB = 1 << 20
 BF16 = jnp.bfloat16
 VMEM = pl.BlockSpec(memory_space=pltpu.VMEM)
 
@@ -38,24 +39,24 @@
     return lax.broadcasted_iota(jnp.int32, shape, 0)
 
 
-def reader(slab, mats):
-    def read(f, t, rows):
-        return slab[f, t, rows, :] if f < 9 else mats[f - 9][t, rows, :]
-
-    return read
-
-
-def pack_kernel(*refs):
-    sources, widths, first, second = refs[:6], refs[6], refs[7], refs[8]
-    copies, sem = refs[9:15], refs[15]
-    moves = [pltpu.make_async_copy(a, c, sem.at[i]) for i, (a, c) in enumerate(zip(sources, copies))]
+def fetch(sources, targets, sem):
+    moves = [pltpu.make_async_copy(a, b, sem.at[i]) for i, (a, b) in enumerate(zip(sources, targets))]
     for move in moves:
         move.start()
     for move in moves:
         move.wait()
-    slab, buo, lam, mu, ocean, depth = copies
+
+
+def pack_kernel(*refs):
+    sources, (first, second), copies, sem = refs[:7], refs[7:9], refs[9:16], refs[16]
+    fetch(sources, copies, sem)
+    widths = copies[6]
+    slab, buo, lam, mu, ocean, depth = copies[:6]
     odd = lax.rem(lax.axis_index("sec"), 2)
-    read = reader(slab, (buo, lam, mu))
+
+    def read(f, t, rows):
+        return slab[f, t, rows, :] if f < 9 else (buo, lam, mu)[f - 9][t, rows, :]
+
     for out, lower in ((first, odd), (second, 1 - odd)):
         start = pl.multiple_of(lower * 8, 8)
         rows = pl.ds(start, 8)
@@ -87,16 +88,51 @@
     return top, bottom
 
 
-def uplift_kernel(slab, buo, lam, mu, ocean, depth, first, second, send, strips, windows):
+def edges(x, r, tlane):
+    out = None
+    for t in range(DEPTH):
+        moved = pltpu.roll(x[t, 8 * r : 8 * r + 8], (SPAN * t + 8) % LANES, 1)
+        out = moved if t == 0 else jnp.where(tlane >= SPAN * t, moved, out)
+    return out
+
+
+def halo_spot(f, r, tlane):
+    i = f * 3 + r
+    at = 2 * (i % 8)
+    spot = tlane % SPAN
+    return i // 8, at, (spot >= at) & (spot < at + 2)
+
+
+def carry_kernel(slab, buo, lam, mu, ocean, depth, state, sea, windows, halos):
+    state[0:9] = slab[...]
+    for i, x in enumerate((buo, lam, mu)):
+        state[9 + i] = x[...]
+    sea[0:3] = ocean[...]
+    sea[3] = depth[...]
+    tlane = lane_iota((8, LANES))
+    heads = [jnp.zeros((8, LANES), F32) for _ in range(5)]
+    tails = [jnp.zeros((8, LANES), F32) for _ in range(5)]
+    for f in range(12):
+        for r in range(2):
+            x = edges(slab.at[f] if f < 9 else (buo, lam, mu)[f - 9], r, tlane)
+            windows[f, 8 * r : 8 * r + 8, :] = x
+            k, at, here = halo_spot(f, r, tlane)
+            heads[k] = jnp.where(here, pltpu.roll(x, (at - 8) % LANES, 1), heads[k])
+            tails[k] = jnp.where(here, pltpu.roll(x, (at - 6) % LANES, 1), tails[k])
+    for k in range(5):
+        halos[0, k] = heads[k]
+        halos[1, k] = tails[k]
+
+
+def uplift_kernel(state, sea, halos, first, second, send, strips, last):
     me = lax.axis_index("blk")
-    read = reader(slab, (buo, lam, mu))
     top, bottom = sides(first, second)
     shape = (32, LANES)
     lane, row = lane_iota(shape), row_iota(shape)
 
     def plane(f, t):
         i = UP_INDEX[(f, t)]
-        return jnp.concatenate([top(i), read(f, t, slice(0, 16)), bottom(i)], axis=0)
+        return jnp.concatenate([top(i), state[f, t], bottom(i)], axis=0)
 
     def north(x):
         return pltpu.roll(x, 1, 0)
@@ -201,25 +237,14 @@
         strips[f, t] = jnp.zeros(tile, F32)
         strips[f, t, 0:2, :] = jnp.where(odd == 0, c, a)
         strips[f, t, 6:8, :] = jnp.where(odd == 0, a, c)
-    heads = [jnp.zeros(tile, F32) for _ in range(5)]
-    tails = [jnp.zeros(tile, F32) for _ in range(5)]
-    spot = tlane % SPAN
+    heads = [halos[0, k] for k in range(5)]
+    tails = [halos[1, k] for k in range(5)]
     for f in range(12):
-        for r in range(3):
-            near, far = jnp.zeros(tile, F32), jnp.zeros(tile, F32)
-            for t in range(DEPTH):
-                at = SPAN * t
-                x = read(f, t, slice(8 * r, 8 * r + 8)) if r < 2 else strips[f, t]
-                x = pltpu.roll(x, (at + 8) % LANES, 1)
-                near = jnp.where((tlane >= at + 8) & (tlane < at + 12), x, near)
-                far = jnp.where((tlane >= at + 4) & (tlane < at + 8), x, far)
-            windows[0, f, 8 * r : 8 * r + 8, :] = near
-            windows[1, f, 8 * r : 8 * r + 8, :] = far
-            i = f * 3 + r
-            k, at = i // 8, 2 * (i % 8)
-            here = (spot >= at) & (spot < at + 2)
-            heads[k] = jnp.where(here, pltpu.roll(near, (at - 8) % LANES, 1), heads[k])
-            tails[k] = jnp.where(here, pltpu.roll(far, (at - 6) % LANES, 1), tails[k])
+        x = edges(strips.at[f], 0, tlane)
+        last[f] = x
+        k, at, here = halo_spot(f, 2, tlane)
+        heads[k] = jnp.where(here, pltpu.roll(x, (at - 8) % LANES, 1), heads[k])
+        tails[k] = jnp.where(here, pltpu.roll(x, (at - 6) % LANES, 1), tails[k])
     head, tail = jnp.zeros(tile, F32), jnp.zeros(tile, F32)
     for f in range(4):
         for r in range(4):
@@ -233,7 +258,7 @@
                 elif r == 3:
                     x = bottom(OCEAN + 4 * f + k)
                 else:
-                    x = ocean[f, rows, cols] if f < 3 else depth[rows, cols]
+                    x = sea[f, rows, cols]
                 ends.append(x)
             here = (tlane >= at) & (tlane < at + 8)
             head = jnp.where(here, pltpu.roll(ends[0], at, 1), head)
@@ -249,12 +274,14 @@
             send[d, B_SLAB + i] = jnp.where(d < me, heads[i], tails[i])
 
 
-def middle_kernel(
-    slab, buo, lam, mu, ocean, depth, first, second, strips, face, widths, plain, seas, filters, cells, mats
-):
+def filter_moves(source, target, sem):
+    rows = [slice(k * LANES, (k + 1) * LANES + (16 if k == 3 else 0)) for k in range(4)]
+    return [pltpu.make_async_copy(source.at[at, :], target.at[at, :], sem.at[k]) for k, at in enumerate(rows)]
+
+
+def middle_kernel(state, sea, first, second, strips, face, widths, plain, seas, filters, cells, mats, held, sem):
     me = lax.axis_index("blk")
     top, bottom = sides(first, second)
-    read = reader(slab, (buo, lam, mu))
     lane = lane_iota((1, LANES))
     face_at = (face[...] - me * COLS).astype(F32)
     width = face.shape[1]
@@ -273,16 +300,8 @@
         decay = jnp.exp2(distance * rate)
         value = decay / (1.0 + decay * decay) * gain
         upper = value.astype(BF16)
-        filters[rows, k * width : (k + 1) * width] = upper
-        filters[rows, (3 + k) * width : (4 + k) * width] = (value - upper.astype(F32)).astype(BF16)
-
-    @pl.loop(0, COLS // 16)
-    def _(c):
-        start = pl.multiple_of(c * 16, 16)
-        at = (lax.broadcasted_iota(jnp.int32, (16, width), 0) + start).astype(F32)
-        distance = jnp.abs(at - face_at)
-        for k in range(3):
-            put(k, pl.ds(start, 16), distance, *groups[k][0])
+        held[rows, k * width : (k + 1) * width] = upper
+        held[rows, (3 + k) * width : (4 + k) * width] = (value - upper.astype(F32)).astype(BF16)
 
     row = row_iota((16, width))
     at = jnp.where(row < 8, row + COLS, row - 16).astype(F32)
@@ -291,13 +310,25 @@
         rate = jnp.where(row < 8, groups[k][1][0], groups[k][2][0])
         gain = jnp.where(row < 8, groups[k][1][1], groups[k][2][1])
         put(k, slice(COLS, COLS + 16), distance, rate, gain)
+    moves = filter_moves(held, filters, sem)
+    for piece in range(4):
+
+        @pl.loop(piece * LANES // 16, (piece + 1) * LANES // 16)
+        def _(c):
+            start = pl.multiple_of(c * 16, 16)
+            at = (lax.broadcasted_iota(jnp.int32, (16, width), 0) + start).astype(F32)
+            distance = jnp.abs(at - face_at)
+            for k in range(3):
+                put(k, pl.ds(start, 16), distance, *groups[k][0])
+
+        moves[piece].start()
 
     for f in range(4):
         for k in range(4):
             cols = slice(k * LANES, (k + 1) * LANES)
             i = OCEAN + 4 * f + k
             seas[f, 0:8, cols] = top(i)
-            seas[f, 8:24, cols] = ocean[f, :, cols] if f < 3 else depth[:, cols]
+            seas[f, 8:24, cols] = sea[f, :, cols]
             seas[f, 24:32, cols] = bottom(i)
 
     for f in range(9):
@@ -306,10 +337,10 @@
     for f in range(12):
         for t in range(DEPTH):
             if f < 9:
-                cells[f, t + 1, 0:R, :] = slab[f, t]
+                cells[f, t + 1, 0:R, :] = state[f, t]
                 cells[f, t + 1, R:, :] = strips[f, t]
             else:
-                mats[f - 9, t, 0:R, :] = (buo, lam, mu)[f - 9][t]
+                mats[f - 9, t, 0:R, :] = state[f, t]
                 mats[f - 9, t, R:, :] = strips[f, t]
     north = lambda v: pltpu.roll(v, 1, 0)
     south = lambda v: pltpu.roll(v, 23, 0)
@@ -337,6 +368,9 @@
             else:
                 for f, x in enumerate(v + new):
                     plain[f, t - 1] = x[0:R]
+
+    for move in moves:
+        move.wait()
 
 
 def velocities(v, s, qb, s11_below, above, north, south, west, east):
@@ -363,7 +397,7 @@
     ]
 
 
-def final_kernel(plain, seas, filters, windows, recv, slab_out, ocean_out, flat):
+def final_kernel(filters, plain, seas, windows, last, recv, slab_out, ocean_out, flat, held, slab, sem):
     sec, me = lax.axis_index("sec"), lax.axis_index("blk")
     n_sec, n_blk = lax.axis_size("sec"), lax.axis_size("blk")
     shape = (32, LANES)
@@ -372,6 +406,48 @@
     west_on, east_on = me > 0, me < n_blk - 1
     tile = (8, LANES)
     tlane = lane_iota(tile)
+
+    moves = filter_moves(filters, held, sem)
+    for move in moves:
+        move.start()
+
+    spot = tlane % SPAN
+    north = lambda v: pltpu.roll(v, 1, 0)
+    south = lambda v: pltpu.roll(v, 23, 0)
+    west = lambda v: pltpu.roll(v, 1, 1)
+    east = lambda v: pltpu.roll(v, LANES - 1, 1)
+    wlane = lane_iota((24, LANES))
+    above = lambda v: jnp.where(wlane < SPAN, 0.0, pltpu.roll(v, SPAN, 1))
+    below = lambda v: jnp.where(wlane >= LANES - SPAN, 0.0, pltpu.roll(v, LANES - SPAN, 1))
+    results = []
+    for side in range(2):
+        other, on, home = ((before, west_on, 6), (after, east_on, 8))[side]
+        here = (spot >= home) & (spot < home + 2)
+        state = []
+        for f in range(12):
+            parts = []
+            for r in range(3):
+                i = f * 3 + r
+                x = pltpu.roll(recv[other, B_SLAB + i // 8], (home - 2 * (i % 8)) % LANES, 1)
+                own = windows[f, 8 * r : 8 * r + 8, :] if r < 2 else last[f]
+                parts.append(jnp.where(here, jnp.where(on, x, 0.0), own))
+            state.append(jnp.concatenate(parts, axis=0))
+        v, s = state[0:3], state[3:9]
+        qb, la, m = Q * state[BUO], Q * state[LAM], Q * state[MU]
+        for step in range(2):
+            v = velocities(v, s, qb, below(s[0]), (above(s[5]), above(s[4])), north, south, west, east)
+            s = stresses(s, v, la, m, (below(v[1]), below(v[2])), above(v[0]), north, south, west, east)
+        results.append(v + s)
+    edge = (tlane < 2) | (tlane >= LANES - 2)
+    for f in range(9):
+        for r in range(2):
+            rows = slice(8 * r, 8 * r + 8)
+            both = jnp.where(spot >= 8, results[0][f][rows], results[1][f][rows])
+            for t in range(DEPTH):
+                moved = pltpu.roll(both, (2 * LANES - SPAN * t - 8) % LANES, 1)
+                slab[f, t, rows, :] = jnp.where(edge, moved, plain[f, t, rows, :])
+    leave = pltpu.make_async_copy(slab, slab_out, sem.at[4])
+    leave.start()
 
     rises = [jnp.concatenate([recv[j, B_UP + r] for r in range(4)], axis=0) for j in range(n_blk)]
     factors = []
@@ -394,10 +470,14 @@
         upper.append(jnp.concatenate([part, jnp.where(mine, rise_lo, 0.0)], axis=0))
         lower.append(jnp.concatenate([part, jnp.zeros_like(part)], axis=0))
     both = jnp.concatenate(upper + lower, axis=1).astype(BF16)
-    source = lax.dot_general(filters[...], both, (((1,), (1,)), ((), ())), preferred_element_type=F32)
-    flat[...] = jnp.zeros((5 * LANES, LANES), F32)
-    flat[0 : COLS + 8, 0:64] = source[0 : COLS + 8]
-    flat[5 * LANES - 8 : 5 * LANES, 0:64] = source[COLS + 8 : COLS + 16]
+    flat[4 * LANES :, :] = jnp.zeros((LANES, LANES), F32)
+    for k in range(4):
+        moves[k].wait()
+        rows = slice(k * LANES, (k + 1) * LANES + (16 if k == 3 else 0))
+        part = lax.dot_general(held[rows, :], both, (((1,), (1,)), ((), ())), preferred_element_type=F32)
+        flat[k * LANES : (k + 1) * LANES, 0:64] = part[0:LANES]
+    flat[COLS : COLS + 8, 0:64] = part[LANES : LANES + 8]
+    flat[5 * LANES - 8 : 5 * LANES, 0:64] = part[LANES + 8 : LANES + 16]
     turned = [flat[k * LANES : (k + 1) * LANES, :].T for k in range(5)]
     source = jnp.concatenate([x[0:32] + x[32:64] for x in turned], axis=1)
 
@@ -428,55 +508,20 @@
     ocean_out[0] = surface[8:24, 0:COLS]
     ocean_out[1] = strike[8:24, 0:COLS]
     ocean_out[2] = dip[8:24, 0:COLS]
-
-    spot = tlane % SPAN
-    north = lambda v: pltpu.roll(v, 1, 0)
-    south = lambda v: pltpu.roll(v, 23, 0)
-    west = lambda v: pltpu.roll(v, 1, 1)
-    east = lambda v: pltpu.roll(v, LANES - 1, 1)
-    wlane = lane_iota((24, LANES))
-    above = lambda v: jnp.where(wlane < SPAN, 0.0, pltpu.roll(v, SPAN, 1))
-    below = lambda v: jnp.where(wlane >= LANES - SPAN, 0.0, pltpu.roll(v, LANES - SPAN, 1))
-    results = []
-    for side in range(2):
-        other, on, home = ((before, west_on, 6), (after, east_on, 8))[side]
-        here = (spot >= home) & (spot < home + 2)
-        state = []
-        for f in range(12):
-            parts = []
-            for r in range(3):
-                i = f * 3 + r
-                x = pltpu.roll(recv[other, B_SLAB + i // 8], (home - 2 * (i % 8)) % LANES, 1)
-                own = windows[side, f, 8 * r : 8 * r + 8, :]
-                parts.append(jnp.where(here & on, x, own))
-            state.append(jnp.concatenate(parts, axis=0))
-        v, s = state[0:3], state[3:9]
-        qb, la, m = Q * state[BUO], Q * state[LAM], Q * state[MU]
-        for step in range(2):
-            v = velocities(v, s, qb, below(s[0]), (above(s[5]), above(s[4])), north, south, west, east)
-            s = stresses(s, v, la, m, (below(v[1]), below(v[2])), above(v[0]), north, south, west, east)
-        results.append(v + s)
-    edge = (tlane < 2) | (tlane >= LANES - 2)
-    for f in range(9):
-        for r in range(2):
-            rows = slice(8 * r, 8 * r + 8)
-            both = jnp.where(spot >= 8, results[0][f][rows], results[1][f][rows])
-            for t in range(DEPTH):
-                moved = pltpu.roll(both, (2 * LANES - SPAN * t - 8) % LANES, 1)
-                slab_out[f, t, rows, :] = jnp.where(edge, moved, plain[f, t, rows, :])
-
-
-def call(kernel, out_shape, flops, *args, far=0, scratch=()):
-    many = isinstance(out_shape, (list, tuple))
-    outs = list(out_shape) if many else [out_shape]
+    leave.wait()
+
+
+def call(kernel, out_shape, flops, *args, far=0, out_far=(), limit=None, scratch=()):
+    outs = list(out_shape)
     n_bytes = sum(a.size * a.dtype.itemsize for a in args) + sum(math.prod(o.shape) * o.dtype.itemsize for o in outs)
+    anywhere = pl.BlockSpec(memory_space=pl.ANY)
     return pl.pallas_call(
         kernel,
         out_shape=out_shape,
-        in_specs=[pl.BlockSpec(memory_space=pltpu.HBM)] * far + [VMEM] * (len(args) - far),
-        out_specs=[VMEM] * len(outs) if many else VMEM,
+        in_specs=[anywhere] * far + [VMEM] * (len(args) - far),
+        out_specs=[anywhere if i in out_far else VMEM for i in range(len(outs))],
         scratch_shapes=scratch,
-        compiler_params=pltpu.CompilerParams(vmem_limit_bytes=12 * 1024 * 1024),
+        compiler_params=pltpu.CompilerParams(vmem_limit_bytes=limit) if limit else None,
         cost_estimate=pl.CostEstimate(flops=flops, bytes_accessed=n_bytes, transcendentals=0),
     )(*args)
 
@@ -494,59 +539,85 @@
     arr = jax.ShapeDtypeStruct
     own = (slab_state, buoyancy, lame_lambda, lame_mu, ocean_state, water_depth)
     message = arr((SEC_TILES, 8, LANES), F32)
+    sources = (*own, band_widths)
     first, second = call(
         pack_kernel,
-        (message, message),
+        [message, message],
         10**6,
-        *own,
-        band_widths,
-        far=6,
-        scratch=[pltpu.VMEM(a.shape, F32) for a in own] + [pltpu.SemaphoreType.DMA((6,))],
+        *sources,
+        far=7,
+        scratch=[pltpu.VMEM(a.shape, a.dtype) for a in sources] + [pltpu.SemaphoreType.DMA((7,))],
     )
     first = swap(first, "sec", 1)
     second = swap(second, "sec", 0)
-    send, strips, windows = call(
+    state, sea, windows, halos = call(
+        carry_kernel,
+        [
+            arr((12, DEPTH, R, LANES), F32),
+            arr((4, R, COLS), F32),
+            arr((12, R, LANES), F32),
+            arr((2, 5, 8, LANES), F32),
+        ],
+        10**7,
+        *own,
+        limit=MIB * 12,
+    )
+    send, strips, last = call(
         uplift_kernel,
-        (
+        [
             arr((n_blk, BLK_TILES, 8, LANES), F32),
             arr((12, DEPTH, 8, LANES), F32),
-            arr((2, 12, 24, LANES), F32),
-        ),
+            arr((12, 8, LANES), F32),
+        ],
         10**7,
-        *own,
+        state,
+        sea,
+        halos,
         first,
         second,
+        limit=MIB * 12,
     )
     recv = lax.all_to_all(send, "blk", 0, 0, tiled=True)
+    filters = arr((4 * (COLS + 16), 6 * n_face), BF16)
     plain, seas, filters = call(
         middle_kernel,
-        (
-            arr(slab_state.shape, F32),
-            arr((4, 32, COLS), F32),
-            arr((COLS + 16, 6 * n_face), BF16),
-        ),
+        [arr(slab_state.shape, F32), arr((4, 32, COLS), F32), filters],
         10**8,
-        *own,
+        state,
+        sea,
         first,
         second,
         strips,
         face_map.reshape(1, n_face),
         band_widths,
+        out_far=(2,),
+        limit=MIB * 46,
         scratch=[
             pltpu.VMEM((9, DEPTH + 2, 24, LANES), F32),
             pltpu.VMEM((3, DEPTH, 24, LANES), F32),
+            pltpu.VMEM((COLS + 16, 6 * n_face), BF16),
+            pltpu.SemaphoreType.DMA((4,)),
         ],
     )
     return call(
         final_kernel,
-        (arr(slab_state.shape, F32), arr(ocean_state.shape, F32)),
+        [arr(slab_state.shape, F32), arr(ocean_state.shape, F32)],
         10**8,
+        filters,
         plain,
         seas,
-        filters,
         windows,
+        last,
         recv,
-        scratch=[pltpu.VMEM((5 * LANES, LANES), F32)],
+        far=1,
+        out_far=(0,),
+        limit=MIB * 46,
+        scratch=[
+            pltpu.VMEM((5 * LANES, LANES), F32),
+            pltpu.VMEM((COLS + 16, 6 * n_face), BF16),
+            pltpu.VMEM(slab_state.shape, F32),
+            pltpu.SemaphoreType.DMA((5,)),
+        ],
     )
 
 

time: 63.9 us -> 56.4 us (0.88)
  local copies, waits for them, and re-layouts: 17 us -> 6.57 us
  Pallas kernels: 13.1 us -> 16 us
    unnamed x32 -> x14, local copies, waits for them, and re-layouts: 16.3 us -> 5.88 us
    all_to_all x1, waiting for transfers between devices: 0.01 us -> 6.36 us  [on_device(): recv = lax.all_to_all(send, 'blk', 0, 0, tiled=True)]
    ppermute x2, waiting for transfers between devices: 6.47 us -> 0.42 us  [swap(): return lax.ppermute(x, axis, pairs)]
    pallas_call x4 -> x5, Pallas kernels: 13.1 us -> 16 us  [call(): pl.pallas_call(kernel, out_shape=out_shape, in_specs=[anywhere] * far + [...]
  transfers between devices with their start and end apart: 3 -> 3, of which waited for: 2 -> 2; matrix products, arithmetic and copies ran while one was open for 1% -> 1% of each run, Pallas kernels for 8% -> 11%
where the time goes in v3:
time: 56.4 us; the launch traced here: 55.8 us
  starting transfers between devices  25.8 us (46%)
  Pallas kernels  16 us (28%)
  waiting for transfers between devices  6.79 us (12%)
  local copies, waits for them, and re-layouts  6.57 us (12%)
  between operations  0.68 us (1%)
    pallas_call x5, Pallas kernels, call(): pl.pallas_call(kernel, out_shape=out_shape, in_specs=[anywhere] * far + [...  16 us
    all_to_all x1, starting transfers between devices, on_device(): recv = lax.all_to_all(send, 'blk', 0, 0, tiled=True)  13.1 us
    ppermute x2, starting transfers between devices, swap(): return lax.ppermute(x, axis, pairs)  12.7 us
    all_to_all x1, waiting for transfers between devices, on_device(): recv = lax.all_to_all(send, 'blk', 0, 0, tiled=True)  6.36 us
    unnamed x14, local copies, waits for them, and re-layouts  5.88 us
  transfers between devices with their start and end apart: 3, of which 2 were waited for; matrix products, arithmetic and copies ran while one was open for 1% of the time, Pallas kernels for 11%

profile of v3, /device:TPU:7, one launch (start us, length us, event | category | flops | bytes accessed | tf_op | source)
XLA Modules:
  0.0 55.8 jit_solution(9894272512414211744)
XLA Ops:
  0.6 2.1 %shard_map.96 = (f32[60,8,128]{2,1,0:T(8,128)}, f32[60,8,128]{2,1,0:T(8,128)}) custom-call(f32[9,8,16,128]{3,2,1,0:T(8,128)} %refs_0_.1, f32[8,16,128]{2,1,0:T(8,128)} %refs_1_.1, f32[8,16,128]{2,1,0:T(8,128)} %refs_2_.1, f32[8,16,128]{2,1,0:T(8,128)} %refs_3_.1, f32[3,16,512]{2,1,0:T(8,128)} %refs_4_.1, f32[16,512]{1,0:T(8,128)} %refs_5_.1, s32[1,6]{1,0:T(1,128)} %widths.1), custom_call_target="tpu_custom_call" | custom-call | flops 1000000 | bytes 1409048 | tf_op jit(solution)/shard_map/pallas_call | solution.py:518
  2.7 10.8 %collective-permute-start = (f32[60,8,128]{2,1,0:T(8,128)}, f32[60,8,128]{2,1,0:T(8,128)S(1)}, u32[]{:S(2)}, u32[]{:S(2)}) collective-permute-start(f32[60,8,128]{2,1,0:T(8,128)} %get-tuple-element.16), channel_id=1, source_target_pairs={{6,12},{12,6},{18,24},{24,18},{30,36},{36,30},{42,48},{48,42},{54,... | collective-permute-start | bytes 737288 | tf_op jit(solution)/shard_map/ppermute | solution.py:533
  13.5 1.9 %collective-permute-start.1 = (f32[60,8,128]{2,1,0:T(8,128)}, f32[60,8,128]{2,1,0:T(8,128)S(1)}, u32[]{:S(2)}, u32[]{:S(2)}) collective-permute-start(f32[60,8,128]{2,1,0:T(8,128)} %get-tuple-element.17), channel_id=1, source_target_pairs={{0,6},{6,0},{12,18},{18,12},{24,30},{30,24},{36,42},{42,36},{48,54... | collective-permute-start | bytes 737288 | tf_op jit(solution)/shard_map/ppermute | solution.py:533
  15.4 0.0 copy-start
  15.4 1.1 %copy-done = f32[9,8,16,128]{3,2,1,0:T(8,128)S(1)} copy-done((f32[9,8,16,128]{3,2,1,0:T(8,128)S(1)}, f32[9,8,16,128]{3,2,1,0:T(8,128)}, u32[]{:S(2)}) %copy-start) | copy-done | bytes 589848
  16.5 0.0 copy-start.1
  16.5 0.9 %copy-done.1 = f32[3,16,512]{2,1,0:T(8,128)S(1)} copy-done((f32[3,16,512]{2,1,0:T(8,128)S(1)}, f32[3,16,512]{2,1,0:T(8,128)}, u32[]{:S(2)}) %copy-start.1) | copy-done | bytes 98328
  17.4 0.0 copy-start.2
  17.4 0.8 %copy-done.2 = f32[8,16,128]{2,1,0:T(8,128)S(1)} copy-done((f32[8,16,128]{2,1,0:T(8,128)S(1)}, f32[8,16,128]{2,1,0:T(8,128)}, u32[]{:S(2)}) %copy-start.2) | copy-done | bytes 65560
  18.2 0.0 copy-start.3
  18.2 0.8 %copy-done.3 = f32[8,16,128]{2,1,0:T(8,128)S(1)} copy-done((f32[8,16,128]{2,1,0:T(8,128)S(1)}, f32[8,16,128]{2,1,0:T(8,128)}, u32[]{:S(2)}) %copy-start.3) | copy-done | bytes 65560
  19.1 0.0 copy-start.4
  19.1 0.8 %copy-done.4 = f32[8,16,128]{2,1,0:T(8,128)S(1)} copy-done((f32[8,16,128]{2,1,0:T(8,128)S(1)}, f32[8,16,128]{2,1,0:T(8,128)}, u32[]{:S(2)}) %copy-start.4) | copy-done | bytes 65560
  19.9 0.0 copy-start.5
  19.9 0.8 %copy-done.5 = f32[16,512]{1,0:T(8,128)S(1)} copy-done((f32[16,512]{1,0:T(8,128)S(1)}, f32[16,512]{1,0:T(8,128)}, u32[]{:S(2)}) %copy-start.5) | copy-done | bytes 32792
  20.7 1.0 %shard_map.95 = (f32[12,8,16,128]{3,2,1,0:T(8,128)S(1)}, f32[4,16,512]{2,1,0:T(8,128)S(1)}, f32[12,16,128]{2,1,0:T(8,128)S(1)}, f32[2,5,8,128]{3,2,1,0:T(8,128)S(1)}) custom-call(f32[9,8,16,128]{3,2,1,0:T(8,128)S(1)} %copy-done, f32[8,16,128]{2,1,0:T(8,128)S(1)} %copy-done.2, f32[8,16,128]{2,1,0:T(8,128)S(1)} %copy-done.3, f32[8,16,128]{2,1,0:T(8,128)S(1)} %copy-done.4, ...), custom_call_target="tpu_custom_call" | custom-call | flops 10000000 | bytes 1974272 | tf_op jit(solution)/shard_map/pallas_call | solution.py:518
  21.7 0.0 collective-permute-done.first
  21.7 0.4 collective-permute-done.1.second
  22.1 1.8 %shard_map.97 = (f32[6,12,8,128]{3,2,1,0:T(8,128)}, f32[12,8,8,128]{3,2,1,0:T(8,128)S(1)}, f32[12,8,128]{2,1,0:T(8,128)S(1)}) custom-call(f32[12,8,16,128]{3,2,1,0:T(8,128)S(1)} %get-tuple-element.14.state, f32[4,16,512]{2,1,0:T(8,128)S(1)} %get-tuple-element.15.sea, f32[2,5,8,128]{3,2,1,0:T(8,128)S(1)} %get-tuple-element.18.halos, ...), custom_call_target="tpu_custom_call" | custom-call | flops 10000000 | bytes 2187264 | tf_op jit(solution)/shard_map/pallas_call | solution.py:518
  23.9 13.1 %all-to-all-start = ((f32[6,12,8,128]{3,2,1,0:T(8,128)}), f32[6,12,8,128]{3,2,1,0:T(8,128)S(1)}, u32[]{:S(2)}, u32[]{:S(2)}) async-start(f32[6,12,8,128]{3,2,1,0:T(8,128)} %get-tuple-element.25), calls=%async_computation | async-start | bytes 589824 | tf_op jit(solution)/shard_map/all_to_all | solution.py:580
  37.0 0.7 %reshape.7.face = s32[1,768]{1,0:T(1,128)S(1)} reshape(s32[768]{0:T(1024)} %param.12) | data formatting | bytes 6144 | tf_op jit(solution)/shard_map/reshape | solution.py:591
  37.7 0.0 copy-start.6
  37.7 0.7 %copy-done.6 = s32[1,6]{1,0:T(1,128)S(1)} copy-done((s32[1,6]{1,0:T(1,128)S(1)}, s32[1,6]{1,0:T(1,128)}, u32[]{:S(2)}) %copy-start.6) | copy-done | bytes 48
  38.4 5.3 %shard_map.98 = (f32[9,8,16,128]{3,2,1,0:T(8,128)S(1)}, f32[4,32,512]{2,1,0:T(8,128)S(1)}, bf16[2112,4608]{1,0:T(8,128)(2,1)}) custom-call(f32[12,8,16,128]{3,2,1,0:T(8,128)S(1)} %get-tuple-element.14.state, f32[4,16,512]{2,1,0:T(8,128)S(1)} %get-tuple-element.15.sea, f32[60,8,128]{2,1,0:T(8,128)S(1)} %collective-permute-done.first, ...), custom_call_target="tpu_custom_call" | custom-call | flops 100000000 | bytes 22121496 | tf_op jit(solution)/shard_map/pallas_call | solution.py:518
  43.7 6.4 %all-to-all-done.recv = f32[6,12,8,128]{3,2,1,0:T(8,128)S(1)} async-done(((f32[6,12,8,128]{3,2,1,0:T(8,128)}), f32[6,12,8,128]{3,2,1,0:T(8,128)S(1)}, u32[]{:S(2)}, u32[]{:S(2)}) %all-to-all-start) | async-done | bytes 294944 | tf_op jit(solution)/shard_map/all_to_all | solution.py:580
  50.0 5.7 %shard_map.99 = (f32[9,8,16,128]{3,2,1,0:T(8,128)}, f32[3,16,512]{2,1,0:T(8,128)}) custom-call(bf16[2112,4608]{1,0:T(8,128)(2,1)} %get-tuple-element.20.filters, f32[9,8,16,128]{3,2,1,0:T(8,128)S(1)} %get-tuple-element.21.plain, f32[4,32,512]{2,1,0:T(8,128)S(1)} %get-tuple-element.22.seas, f32[12,16,128]{2,1,0:T(8,128)S(1)} %get-tuple-element.23.windows, ...), custom_call_target="tpu_custom_call" | custom-call | flops 100000000 | bytes 21446656 | tf_op jit(solution)/shard_map/pallas_call | solution.py:518
Async XLA Ops:
  2.7 19.0 %collective-permute-start = (f32[60,8,128]{2,1,0:T(8,128)}, f32[60,8,128]{2,1,0:T(8,128)S(1)}, u32[]{:S(2)}, u32[]{:S(2)}) collective-permute-start(f32[60,8,128]{2,1,0:T(8,128)} %get-tuple-element.16), channel_id=1, source_target_pairs={{6,12},{12,6},{18,24},{24,18},{30,36},{36,30},{42,48},{48,42},{54,... | collective-permute-start | bytes 737288 | tf_op jit(solution)/shard_map/ppermute | solution.py:533
  13.5 8.6 %collective-permute-start.1 = (f32[60,8,128]{2,1,0:T(8,128)}, f32[60,8,128]{2,1,0:T(8,128)S(1)}, u32[]{:S(2)}, u32[]{:S(2)}) collective-permute-start(f32[60,8,128]{2,1,0:T(8,128)} %get-tuple-element.17), channel_id=1, source_target_pairs={{0,6},{6,0},{12,18},{18,12},{24,30},{30,24},{36,42},{42,36},{48,54... | collective-permute-start | bytes 737288 | tf_op jit(solution)/shard_map/ppermute | solution.py:533
  15.4 1.1 %copy-start = (f32[9,8,16,128]{3,2,1,0:T(8,128)S(1)}, f32[9,8,16,128]{3,2,1,0:T(8,128)}, u32[]{:S(2)}) copy-start(f32[9,8,16,128]{3,2,1,0:T(8,128)} %refs_0_.1) | copy-start | bytes 1769476
  16.5 0.9 %copy-start.1 = (f32[3,16,512]{2,1,0:T(8,128)S(1)}, f32[3,16,512]{2,1,0:T(8,128)}, u32[]{:S(2)}) copy-start(f32[3,16,512]{2,1,0:T(8,128)} %refs_4_.1) | copy-start | bytes 294916
  17.4 0.8 %copy-start.2 = (f32[8,16,128]{2,1,0:T(8,128)S(1)}, f32[8,16,128]{2,1,0:T(8,128)}, u32[]{:S(2)}) copy-start(f32[8,16,128]{2,1,0:T(8,128)} %refs_1_.1) | copy-start | bytes 196612
  18.2 0.8 %copy-start.3 = (f32[8,16,128]{2,1,0:T(8,128)S(1)}, f32[8,16,128]{2,1,0:T(8,128)}, u32[]{:S(2)}) copy-start(f32[8,16,128]{2,1,0:T(8,128)} %refs_2_.1) | copy-start | bytes 196612
  19.1 0.8 %copy-start.4 = (f32[8,16,128]{2,1,0:T(8,128)S(1)}, f32[8,16,128]{2,1,0:T(8,128)}, u32[]{:S(2)}) copy-start(f32[8,16,128]{2,1,0:T(8,128)} %refs_3_.1) | copy-start | bytes 196612
  19.9 0.8 %copy-start.5 = (f32[16,512]{1,0:T(8,128)S(1)}, f32[16,512]{1,0:T(8,128)}, u32[]{:S(2)}) copy-start(f32[16,512]{1,0:T(8,128)} %refs_5_.1) | copy-start | bytes 98308
  23.9 26.1 %all-to-all-start = ((f32[6,12,8,128]{3,2,1,0:T(8,128)}), f32[6,12,8,128]{3,2,1,0:T(8,128)S(1)}, u32[]{:S(2)}, u32[]{:S(2)}) async-start(f32[6,12,8,128]{3,2,1,0:T(8,128)} %get-tuple-element.25), calls=%async_computation | async-start | bytes 589824 | tf_op jit(solution)/shard_map/all_to_all | solution.py:580
  37.7 0.7 %copy-start.6 = (s32[1,6]{1,0:T(1,128)S(1)}, s32[1,6]{1,0:T(1,128)}, u32[]{:S(2)}) copy-start(s32[1,6]{1,0:T(1,128)} %widths.1) | copy-start | bytes 76

commit v4 on v3

--- a/solution.py
+++ b/solution.py
@@ -27,6 +27,7 @@
 SPAN = 16
 F32 = jnp.float32
 MIB = 1 << 20
+PAD = 36
 BF16 = jnp.bfloat16
 VMEM = pl.BlockSpec(memory_space=pltpu.VMEM)
 
@@ -39,17 +40,19 @@
     return lax.broadcasted_iota(jnp.int32, shape, 0)
 
 
-def fetch(sources, targets, sem):
+def fetch(sources, targets, sem, others):
     moves = [pltpu.make_async_copy(a, b, sem.at[i]) for i, (a, b) in enumerate(zip(sources, targets))]
-    for move in moves:
+    for move in moves + others:
         move.start()
     for move in moves:
         move.wait()
 
 
 def pack_kernel(*refs):
-    sources, (first, second), copies, sem = refs[:7], refs[7:9], refs[9:16], refs[16]
-    fetch(sources, copies, sem)
+    sources, (first, second, state, sea), copies, sem, join_sem = refs[:7], refs[7:11], refs[11:18], refs[18], refs[19]
+    parts = [state.at[0:9], state.at[9], state.at[10], state.at[11], sea.at[0:3], sea.at[3]]
+    joins = [pltpu.make_async_copy(a, b, join_sem.at[i]) for i, (a, b) in enumerate(zip(sources, parts))]
+    fetch(sources, copies, sem, joins)
     widths = copies[6]
     slab, buo, lam, mu, ocean, depth = copies[:6]
     odd = lax.rem(lax.axis_index("sec"), 2)
@@ -74,6 +77,8 @@
             for k in range(4):
                 cols = slice(k * LANES, (k + 1) * LANES)
                 out[OCEAN + 4 * f + k] = ocean[f, rows, cols] if f < 3 else depth[rows, cols]
+    for join in joins:
+        join.wait()
 
 
 def sides(first, second):
@@ -96,6 +101,20 @@
     return out
 
 
+def fill_strips(strips, first, second):
+    top, bottom = sides(first, second)
+    odd = lax.rem(lax.axis_index("sec"), 2)
+    row = row_iota((8, LANES))
+    for i, (f, t) in enumerate(UP_PLANES):
+        strips[f, t] = jnp.where(row < 2, bottom(i), jnp.where(row >= 6, top(i), 0.0))
+    for p, (f, t) in enumerate(REST):
+        i, at = STRIP + p // 4, slice(2 * (p % 4), 2 * (p % 4) + 2)
+        a, c = first[i, at, :], second[i, at, :]
+        strips[f, t] = jnp.zeros((8, LANES), F32)
+        strips[f, t, 0:2, :] = jnp.where(odd == 0, c, a)
+        strips[f, t, 6:8, :] = jnp.where(odd == 0, a, c)
+
+
 def halo_spot(f, r, tlane):
     i = f * 3 + r
     at = 2 * (i % 8)
@@ -103,18 +122,15 @@
     return i // 8, at, (spot >= at) & (spot < at + 2)
 
 
-def carry_kernel(slab, buo, lam, mu, ocean, depth, state, sea, windows, halos):
-    state[0:9] = slab[...]
-    for i, x in enumerate((buo, lam, mu)):
-        state[9 + i] = x[...]
-    sea[0:3] = ocean[...]
-    sea[3] = depth[...]
+def carry_kernel(state_in, sea_in, state, sea, windows, halos):
+    state[...] = state_in[...]
+    sea[...] = sea_in[...]
     tlane = lane_iota((8, LANES))
     heads = [jnp.zeros((8, LANES), F32) for _ in range(5)]
     tails = [jnp.zeros((8, LANES), F32) for _ in range(5)]
     for f in range(12):
         for r in range(2):
-            x = edges(slab.at[f] if f < 9 else (buo, lam, mu)[f - 9], r, tlane)
+            x = edges(state_in.at[f], r, tlane)
             windows[f, 8 * r : 8 * r + 8, :] = x
             k, at, here = halo_spot(f, r, tlane)
             heads[k] = jnp.where(here, pltpu.roll(x, (at - 8) % LANES, 1), heads[k])
@@ -124,7 +140,7 @@
         halos[1, k] = tails[k]
 
 
-def uplift_kernel(state, sea, halos, first, second, send, strips, last):
+def uplift_kernel(state, sea, halos, first, second, send, last, strips):
     me = lax.axis_index("blk")
     top, bottom = sides(first, second)
     shape = (32, LANES)
@@ -227,16 +243,8 @@
     packed = jnp.where(lane[:16] < 64, factors[:16], pltpu.roll(factors[16:], 64, 1))
 
     tile = (8, LANES)
-    tlane, trow = lane_iota(tile), row_iota(tile)
-    odd = lax.rem(lax.axis_index("sec"), 2)
-    for i, (f, t) in enumerate(UP_PLANES):
-        strips[f, t] = jnp.where(trow < 2, bottom(i), jnp.where(trow >= 6, top(i), 0.0))
-    for p, (f, t) in enumerate(REST):
-        i, at = STRIP + p // 4, slice(2 * (p % 4), 2 * (p % 4) + 2)
-        a, c = first[i, at, :], second[i, at, :]
-        strips[f, t] = jnp.zeros(tile, F32)
-        strips[f, t, 0:2, :] = jnp.where(odd == 0, c, a)
-        strips[f, t, 6:8, :] = jnp.where(odd == 0, a, c)
+    tlane = lane_iota(tile)
+    fill_strips(strips, first, second)
     heads = [halos[0, k] for k in range(5)]
     tails = [halos[1, k] for k in range(5)]
     for f in range(12):
@@ -279,7 +287,9 @@
     return [pltpu.make_async_copy(source.at[at, :], target.at[at, :], sem.at[k]) for k, at in enumerate(rows)]
 
 
-def middle_kernel(state, sea, first, second, strips, face, widths, plain, seas, filters, cells, mats, held, sem):
+def middle_kernel(
+    state, sea, first, second, face, widths, plain_out, near, far, cells, mats, held, strips, plain, sem
+):
     me = lax.axis_index("blk")
     top, bottom = sides(first, second)
     lane = lane_iota((1, LANES))
@@ -300,8 +310,9 @@
         decay = jnp.exp2(distance * rate)
         value = decay / (1.0 + decay * decay) * gain
         upper = value.astype(BF16)
-        held[rows, k * width : (k + 1) * width] = upper
-        held[rows, (3 + k) * width : (4 + k) * width] = (value - upper.astype(F32)).astype(BF16)
+        out, at = (near, 0) if k == 1 else (held, k * width)
+        out[rows, at : at + width] = upper
+        out[rows, at + width : at + 2 * width] = (value - upper.astype(F32)).astype(BF16)
 
     row = row_iota((16, width))
     at = jnp.where(row < 8, row + COLS, row - 16).astype(F32)
@@ -310,7 +321,7 @@
         rate = jnp.where(row < 8, groups[k][1][0], groups[k][2][0])
         gain = jnp.where(row < 8, groups[k][1][1], groups[k][2][1])
         put(k, slice(COLS, COLS + 16), distance, rate, gain)
-    moves = filter_moves(held, filters, sem)
+    moves = filter_moves(held, far, sem)
     for piece in range(4):
 
         @pl.loop(piece * LANES // 16, (piece + 1) * LANES // 16)
@@ -327,10 +338,12 @@
         for k in range(4):
             cols = slice(k * LANES, (k + 1) * LANES)
             i = OCEAN + 4 * f + k
-            seas[f, 0:8, cols] = top(i)
-            seas[f, 8:24, cols] = sea[f, :, cols]
-            seas[f, 24:32, cols] = bottom(i)
-
+            plain[9 + f, 2 * k, 0:8, :] = top(i)
+            plain[9 + f, 2 * k, 8:16, :] = sea[f, 0:8, cols]
+            plain[9 + f, 2 * k + 1, 0:8, :] = sea[f, 8:16, cols]
+            plain[9 + f, 2 * k + 1, 8:16, :] = bottom(i)
+
+    fill_strips(strips, first, second)
     for f in range(9):
         for t in (0, DEPTH + 1):
             cells[f, t] = jnp.zeros((24, LANES), F32)
@@ -369,7 +382,9 @@
                 for f, x in enumerate(v + new):
                     plain[f, t - 1] = x[0:R]
 
-    for move in moves:
+    leave = pltpu.make_async_copy(plain, plain_out.at[0:13], sem.at[4])
+    leave.start()
+    for move in moves + [leave]:
         move.wait()
 
 
@@ -397,7 +412,7 @@
     ]
 
 
-def final_kernel(filters, plain, seas, windows, last, recv, slab_out, ocean_out, flat, held, slab, sem):
+def final_kernel(far, plain_in, near, windows, last, recv, slab_out, ocean_out, flat, held, plain, slab, sem):
     sec, me = lax.axis_index("sec"), lax.axis_index("blk")
     n_sec, n_blk = lax.axis_size("sec"), lax.axis_size("blk")
     shape = (32, LANES)
@@ -407,8 +422,9 @@
     tile = (8, LANES)
     tlane = lane_iota(tile)
 
-    moves = filter_moves(filters, held, sem)
-    for move in moves:
+    enter = pltpu.make_async_copy(plain_in.at[0:13], plain, sem.at[5])
+    moves = filter_moves(far, held, sem)
+    for move in [enter] + moves:
         move.start()
 
     spot = tlane % SPAN
@@ -438,6 +454,7 @@
             v = velocities(v, s, qb, below(s[0]), (above(s[5]), above(s[4])), north, south, west, east)
             s = stresses(s, v, la, m, (below(v[1]), below(v[2])), above(v[0]), north, south, west, east)
         results.append(v + s)
+    enter.wait()
     edge = (tlane < 2) | (tlane >= LANES - 2)
     for f in range(9):
         for r in range(2):
@@ -463,21 +480,23 @@
     rise_hi = rise.astype(BF16).astype(F32)
     rise_lo = rise - rise_hi
     wide = row_iota(rise.shape)
-    upper, lower = [], []
-    for k in range(3):
+    upper = {}
+    for k in (1, 0, 2):
         mine = (wide >= (0, 8, 24)[k]) & (wide < (8, 24, 32)[k])
         part = jnp.where(mine, rise_hi, 0.0)
-        upper.append(jnp.concatenate([part, jnp.where(mine, rise_lo, 0.0)], axis=0))
-        lower.append(jnp.concatenate([part, jnp.zeros_like(part)], axis=0))
-    both = jnp.concatenate(upper + lower, axis=1).astype(BF16)
+        upper[k] = jnp.concatenate([part, jnp.where(mine, rise_lo, 0.0)], axis=0).astype(BF16)
+        upper[k] = [upper[k], jnp.concatenate([part, jnp.zeros_like(part)], axis=0).astype(BF16)]
+
+    def dot(a, c):
+        return lax.dot_general(a, c, (((1,), (1,)), ((), ())), preferred_element_type=F32)
+
+    for move in moves:
+        move.wait()
+    source = dot(near[...], jnp.concatenate(upper[1], axis=1))
+    source = source + dot(held[...], jnp.concatenate(upper[0] + upper[2], axis=1))
     flat[4 * LANES :, :] = jnp.zeros((LANES, LANES), F32)
-    for k in range(4):
-        moves[k].wait()
-        rows = slice(k * LANES, (k + 1) * LANES + (16 if k == 3 else 0))
-        part = lax.dot_general(held[rows, :], both, (((1,), (1,)), ((), ())), preferred_element_type=F32)
-        flat[k * LANES : (k + 1) * LANES, 0:64] = part[0:LANES]
-    flat[COLS : COLS + 8, 0:64] = part[LANES : LANES + 8]
-    flat[5 * LANES - 8 : 5 * LANES, 0:64] = part[LANES + 8 : LANES + 16]
+    flat[0 : COLS + 8, 0:64] = source[0 : COLS + 8]
+    flat[5 * LANES - 8 : 5 * LANES, 0:64] = source[COLS + 8 : COLS + 16]
     turned = [flat[k * LANES : (k + 1) * LANES, :].T for k in range(5)]
     source = jnp.concatenate([x[0:32] + x[32:64] for x in turned], axis=1)
 
@@ -491,7 +510,8 @@
             west_in = pltpu.roll(recv[before, B_OCEAN], (2 * LANES - 8 - at) % LANES, 1)
             x = jnp.where((tlane < 8) & east_on, east_in, 0.0)
             halo.append(jnp.where((tlane >= LANES - 8) & west_on, west_in, x))
-        fields.append(jnp.concatenate([seas[f], jnp.concatenate(halo, axis=0)], axis=1))
+        tiles = [jnp.concatenate([plain[9 + f, 2 * k], plain[9 + f, 2 * k + 1]], axis=0) for k in range(4)]
+        fields.append(jnp.concatenate(tiles + [jnp.concatenate(halo, axis=0)], axis=1))
     surface, strike, dip, water = fields
     at = lane_iota(ring)
     at = jnp.where(at >= 5 * LANES - 8, at - 5 * LANES, at)
@@ -540,35 +560,36 @@
     own = (slab_state, buoyancy, lame_lambda, lame_mu, ocean_state, water_depth)
     message = arr((SEC_TILES, 8, LANES), F32)
     sources = (*own, band_widths)
-    first, second = call(
+    state, sea = arr((12, DEPTH, R, LANES), F32), arr((4, R, COLS), F32)
+    first, second, state, sea = call(
         pack_kernel,
-        [message, message],
+        [message, message, state, sea],
         10**6,
         *sources,
         far=7,
-        scratch=[pltpu.VMEM(a.shape, a.dtype) for a in sources] + [pltpu.SemaphoreType.DMA((7,))],
+        out_far=(2, 3),
+        scratch=[pltpu.VMEM(a.shape, a.dtype) for a in sources]
+        + [pltpu.SemaphoreType.DMA((7,)), pltpu.SemaphoreType.DMA((6,))],
     )
     first = swap(first, "sec", 1)
     second = swap(second, "sec", 0)
     state, sea, windows, halos = call(
         carry_kernel,
         [
-            arr((12, DEPTH, R, LANES), F32),
-            arr((4, R, COLS), F32),
+            arr(state.shape, F32),
+            arr(sea.shape, F32),
             arr((12, R, LANES), F32),
             arr((2, 5, 8, LANES), F32),
         ],
         10**7,
-        *own,
+        state,
+        sea,
         limit=MIB * 12,
     )
-    send, strips, last = call(
+    strips = pltpu.VMEM((12, DEPTH, 8, LANES), F32)
+    send, last = call(
         uplift_kernel,
-        [
-            arr((n_blk, BLK_TILES, 8, LANES), F32),
-            arr((12, DEPTH, 8, LANES), F32),
-            arr((12, 8, LANES), F32),
-        ],
+        [arr((n_blk, BLK_TILES, 8, LANES), F32), arr((12, 8, LANES), F32)],
         10**7,
         state,
         sea,
@@ -576,47 +597,53 @@
         first,
         second,
         limit=MIB * 12,
+        scratch=[strips],
     )
     recv = lax.all_to_all(send, "blk", 0, 0, tiled=True)
-    filters = arr((4 * (COLS + 16), 6 * n_face), BF16)
-    plain, seas, filters = call(
+    near = arr((COLS + 16, 2 * n_face), BF16)
+    far = arr((6 * (COLS + 16), 4 * n_face), BF16)
+    held = pltpu.VMEM((COLS + 16, 4 * n_face), BF16)
+    plain = arr((PAD * 9, *slab_state.shape[1:]), F32)
+    plain, near, far = call(
         middle_kernel,
-        [arr(slab_state.shape, F32), arr((4, 32, COLS), F32), filters],
+        [plain, near, far],
         10**8,
         state,
         sea,
         first,
         second,
-        strips,
         face_map.reshape(1, n_face),
         band_widths,
-        out_far=(2,),
+        out_far=(0, 2),
         limit=MIB * 46,
         scratch=[
             pltpu.VMEM((9, DEPTH + 2, 24, LANES), F32),
             pltpu.VMEM((3, DEPTH, 24, LANES), F32),
-            pltpu.VMEM((COLS + 16, 6 * n_face), BF16),
-            pltpu.SemaphoreType.DMA((4,)),
+            held,
+            strips,
+            pltpu.VMEM((13, DEPTH, R, LANES), F32),
+            pltpu.SemaphoreType.DMA((5,)),
         ],
     )
     return call(
         final_kernel,
         [arr(slab_state.shape, F32), arr(ocean_state.shape, F32)],
         10**8,
-        filters,
+        far,
         plain,
-        seas,
+        near,
         windows,
         last,
         recv,
-        far=1,
+        far=2,
         out_far=(0,),
         limit=MIB * 46,
         scratch=[
             pltpu.VMEM((5 * LANES, LANES), F32),
-            pltpu.VMEM((COLS + 16, 6 * n_face), BF16),
+            held,
+            pltpu.VMEM((13, DEPTH, R, LANES), F32),
             pltpu.VMEM(slab_state.shape, F32),
-            pltpu.SemaphoreType.DMA((5,)),
+            pltpu.SemaphoreType.DMA((6,)),
         ],
     )
 

time: 56.4 us -> 83.5 us (1.48)
  Pallas kernels: 16 us -> 44.4 us
  local copies, waits for them, and re-layouts: 6.57 us -> 3.37 us
  waiting for transfers between devices: 6.79 us -> 8.96 us
    pallas_call x5, Pallas kernels: 16 us -> 44.4 us  [call(): pl.pallas_call(kernel, out_shape=out_shape, in_specs=[anywhere] * far + [...]
    unnamed x14 -> x6, local copies, waits for them, and re-layouts: 5.88 us -> 2.68 us
    ppermute x2, waiting for transfers between devices: 0.42 us -> 3.61 us  [swap(): return lax.ppermute(x, axis, pairs)]
    all_to_all x1, waiting for transfers between devices: 6.36 us -> 5.35 us  [on_device(): recv = lax.all_to_all(send, 'blk', 0, 0, tiled=True)]
  transfers between devices with their start and end apart: 3 -> 3, of which waited for: 2 -> 3; matrix products, arithmetic and copies ran while one was open for 1% -> 1% of each run, Pallas kernels for 11% -> 9%
where the time goes in v4:
time: 83.5 us; the launch traced here: 83.2 us
  Pallas kernels  44.4 us (53%)
  starting transfers between devices  25.8 us (31%)
  waiting for transfers between devices  8.96 us (11%)
  local copies, waits for them, and re-layouts  3.37 us (4%)
    pallas_call x5, Pallas kernels, call(): pl.pallas_call(kernel, out_shape=out_shape, in_specs=[anywhere] * far + [...  44.4 us
    all_to_all x1, starting transfers between devices, on_device(): recv = lax.all_to_all(send, 'blk', 0, 0, tiled=True)  13.1 us
    ppermute x2, starting transfers between devices, swap(): return lax.ppermute(x, axis, pairs)  12.7 us
    all_to_all x1, waiting for transfers between devices, on_device(): recv = lax.all_to_all(send, 'blk', 0, 0, tiled=True)  5.35 us
    ppermute x2, waiting for transfers between devices, swap(): return lax.ppermute(x, axis, pairs)  3.61 us
    unnamed x6, local copies, waits for them, and re-layouts  2.68 us
  transfers between devices with their start and end apart: 3, of which 3 were waited for; matrix products, arithmetic and copies ran while one was open for 1% of the time, Pallas kernels for 9%

profile of v4, /device:TPU:7, one launch (start us, length us, event | category | flops | bytes accessed | tf_op | source)
XLA Modules:
  0.0 83.2 jit_solution(12303086262356931481)
XLA Ops:
  0.6 29.8 %shard_map.95 = (f32[60,8,128]{2,1,0:T(8,128)}, f32[60,8,128]{2,1,0:T(8,128)}, f32[12,8,16,128]{3,2,1,0:T(8,128)}, f32[4,16,512]{2,1,0:T(8,128)}) custom-call(f32[9,8,16,128]{3,2,1,0:T(8,128)} %refs_0_.1, f32[8,16,128]{2,1,0:T(8,128)} %refs_1_.1, f32[8,16,128]{2,1,0:T(8,128)} %refs_2_.1, f32[8,16,128]{2,1,0:T(8,128)} %refs_3_.1, f32[3,16,512]{2,1,0:T(8,128)} %refs_4_.1, ...), custom_call_target="tpu_custom_call" | custom-call | flops 1000000 | bytes 2326552 | tf_op jit(solution)/shard_map/pallas_call | solution.py:538
  30.4 10.8 %collective-permute-start = (f32[60,8,128]{2,1,0:T(8,128)}, f32[60,8,128]{2,1,0:T(8,128)S(1)}, u32[]{:S(2)}, u32[]{:S(2)}) collective-permute-start(f32[60,8,128]{2,1,0:T(8,128)} %get-tuple-element.19), channel_id=1, source_target_pairs={{6,12},{12,6},{18,24},{24,18},{30,36},{36,30},{42,48},{48,42},{54,... | collective-permute-start | bytes 737288 | tf_op jit(solution)/shard_map/ppermute | solution.py:553
  41.2 1.9 %collective-permute-start.1 = (f32[60,8,128]{2,1,0:T(8,128)}, f32[60,8,128]{2,1,0:T(8,128)S(1)}, u32[]{:S(2)}, u32[]{:S(2)}) collective-permute-start(f32[60,8,128]{2,1,0:T(8,128)} %get-tuple-element.20), channel_id=1, source_target_pairs={{0,6},{6,0},{12,18},{18,12},{24,30},{30,24},{36,42},{42,36},{48,54... | collective-permute-start | bytes 737288 | tf_op jit(solution)/shard_map/ppermute | solution.py:553
  43.1 0.0 copy-start
  43.2 1.1 %copy-done = f32[12,8,16,128]{3,2,1,0:T(8,128)S(1)} copy-done((f32[12,8,16,128]{3,2,1,0:T(8,128)S(1)}, f32[12,8,16,128]{3,2,1,0:T(8,128)}, u32[]{:S(2)}) %copy-start) | copy-done | bytes 786456
  44.3 0.0 copy-start.1
  44.3 0.9 %copy-done.1 = f32[4,16,512]{2,1,0:T(8,128)S(1)} copy-done((f32[4,16,512]{2,1,0:T(8,128)S(1)}, f32[4,16,512]{2,1,0:T(8,128)}, u32[]{:S(2)}) %copy-start.1) | copy-done | bytes 131096
  45.2 1.0 %shard_map.96 = (f32[12,8,16,128]{3,2,1,0:T(8,128)S(1)}, f32[4,16,512]{2,1,0:T(8,128)S(1)}, f32[12,16,128]{2,1,0:T(8,128)S(1)}, f32[2,5,8,128]{3,2,1,0:T(8,128)S(1)}) custom-call(f32[12,8,16,128]{3,2,1,0:T(8,128)S(1)} %copy-done, f32[4,16,512]{2,1,0:T(8,128)S(1)} %copy-done.1), custom_call_target="tpu_custom_call" | custom-call | flops 10000000 | bytes 1974272 | tf_op jit(solution)/shard_map/pallas_call | solution.py:538
  46.2 0.9 %collective-permute-done.first = f32[60,8,128]{2,1,0:T(8,128)S(1)} collective-permute-done((f32[60,8,128]{2,1,0:T(8,128)}, f32[60,8,128]{2,1,0:T(8,128)S(1)}, u32[]{:S(2)}, u32[]{:S(2)}) %collective-permute-start) | collective-permute-done | bytes 245792 | tf_op jit(solution)/shard_map/ppermute | solution.py:553
  47.1 2.7 %collective-permute-done.1.second = f32[60,8,128]{2,1,0:T(8,128)S(1)} collective-permute-done((f32[60,8,128]{2,1,0:T(8,128)}, f32[60,8,128]{2,1,0:T(8,128)S(1)}, u32[]{:S(2)}, u32[]{:S(2)}) %collective-permute-start.1) | collective-permute-done | bytes 245792 | tf_op jit(solution)/shard_map/ppermute | solution.py:553
  49.8 1.8 %shard_map.98 = (f32[6,12,8,128]{3,2,1,0:T(8,128)}, f32[12,8,128]{2,1,0:T(8,128)S(1)}) custom-call(f32[12,8,16,128]{3,2,1,0:T(8,128)S(1)} %get-tuple-element.17.state, f32[4,16,512]{2,1,0:T(8,128)S(1)} %get-tuple-element.18.sea, f32[2,5,8,128]{3,2,1,0:T(8,128)S(1)} %get-tuple-element.25.halos, f32[60,8,128]{2,1,0:T(8,128)S(1)} %collective-permute-done.first, ...), custom_call_target="tpu_custom_call" | custom-call | flops 10000000 | bytes 1794048 | tf_op jit(solution)/shard_map/pallas_call | solution.py:538
  51.7 13.1 %all-to-all-start = ((f32[6,12,8,128]{3,2,1,0:T(8,128)}), f32[6,12,8,128]{3,2,1,0:T(8,128)S(1)}, u32[]{:S(2)}, u32[]{:S(2)}) async-start(f32[6,12,8,128]{3,2,1,0:T(8,128)} %get-tuple-element.27), calls=%async_computation | async-start | bytes 589824 | tf_op jit(solution)/shard_map/all_to_all | solution.py:602
  64.8 0.7 reshape.7.face
  65.4 0.0 copy-start.2
  65.4 0.7 copy-done.2
  66.1 6.3 %shard_map.97 = (f32[324,8,16,128]{3,2,1,0:T(8,128)}, bf16[528,1536]{1,0:T(8,128)(2,1)S(1)}, bf16[3168,3072]{1,0:T(8,128)(2,1)}) custom-call(f32[12,8,16,128]{3,2,1,0:T(8,128)S(1)} %get-tuple-element.17.state, f32[4,16,512]{2,1,0:T(8,128)S(1)} %get-tuple-element.18.sea, f32[60,8,128]{2,1,0:T(8,128)S(1)} %collective-permute-done.first, ...), custom_call_target="tpu_custom_call" | custom-call | flops 100000000 | bytes 43731992 | tf_op jit(solution)/shard_map/pallas_call | solution.py:538
  72.4 5.4 %all-to-all-done.recv = f32[6,12,8,128]{3,2,1,0:T(8,128)S(1)} async-done(((f32[6,12,8,128]{3,2,1,0:T(8,128)}), f32[6,12,8,128]{3,2,1,0:T(8,128)S(1)}, u32[]{:S(2)}, u32[]{:S(2)}) %all-to-all-start) | async-done | bytes 294944 | tf_op jit(solution)/shard_map/all_to_all | solution.py:602
  77.8 5.4 %shard_map.99 = (f32[9,8,16,128]{3,2,1,0:T(8,128)}, f32[3,16,512]{2,1,0:T(8,128)}) custom-call(bf16[3168,3072]{1,0:T(8,128)(2,1)} %get-tuple-element.21.far, f32[324,8,16,128]{3,2,1,0:T(8,128)} %get-tuple-element.22.plain_in, bf16[528,1536]{1,0:T(8,128)(2,1)S(1)} %get-tuple-element.23.near, f32[12,16,128]{2,1,0:T(8,128)S(1)} %get-tuple-element.24.windows, ...), custom_call_target="tpu_custom_call" | custom-call | flops 100000000 | bytes 43450368 | tf_op jit(solution)/shard_map/pallas_call | solution.py:538
Async XLA Ops:
  30.4 16.7 %collective-permute-start = (f32[60,8,128]{2,1,0:T(8,128)}, f32[60,8,128]{2,1,0:T(8,128)S(1)}, u32[]{:S(2)}, u32[]{:S(2)}) collective-permute-start(f32[60,8,128]{2,1,0:T(8,128)} %get-tuple-element.19), channel_id=1, source_target_pairs={{6,12},{12,6},{18,24},{24,18},{30,36},{36,30},{42,48},{48,42},{54,... | collective-permute-start | bytes 737288 | tf_op jit(solution)/shard_map/ppermute | solution.py:553
  41.2 8.6 %collective-permute-start.1 = (f32[60,8,128]{2,1,0:T(8,128)}, f32[60,8,128]{2,1,0:T(8,128)S(1)}, u32[]{:S(2)}, u32[]{:S(2)}) collective-permute-start(f32[60,8,128]{2,1,0:T(8,128)} %get-tuple-element.20), channel_id=1, source_target_pairs={{0,6},{6,0},{12,18},{18,12},{24,30},{30,24},{36,42},{42,36},{48,54... | collective-permute-start | bytes 737288 | tf_op jit(solution)/shard_map/ppermute | solution.py:553
  43.1 1.1 %copy-start = (f32[12,8,16,128]{3,2,1,0:T(8,128)S(1)}, f32[12,8,16,128]{3,2,1,0:T(8,128)}, u32[]{:S(2)}) copy-start(f32[12,8,16,128]{3,2,1,0:T(8,128)} %get-tuple-element.15.state_in) | copy-start | bytes 2359300
  44.3 0.9 %copy-start.1 = (f32[4,16,512]{2,1,0:T(8,128)S(1)}, f32[4,16,512]{2,1,0:T(8,128)}, u32[]{:S(2)}) copy-start(f32[4,16,512]{2,1,0:T(8,128)} %get-tuple-element.16.sea_in) | copy-start | bytes 393220
  51.7 26.1 %all-to-all-start = ((f32[6,12,8,128]{3,2,1,0:T(8,128)}), f32[6,12,8,128]{3,2,1,0:T(8,128)S(1)}, u32[]{:S(2)}, u32[]{:S(2)}) async-start(f32[6,12,8,128]{3,2,1,0:T(8,128)} %get-tuple-element.27), calls=%async_computation | async-start | bytes 589824 | tf_op jit(solution)/shard_map/all_to_all | solution.py:602
  65.4 0.7 copy-start.2

commit v5 on v4

--- a/solution.py
+++ b/solution.py
@@ -23,7 +23,7 @@
 MISC = STRIP + (len(REST) + 3) // 4
 OCEAN = MISC + 1
 SEC_TILES = OCEAN + 16
-B_UP, B_FACTOR, B_SLAB, B_OCEAN, BLK_TILES = 0, 4, 6, 11, 12
+B_UP, B_FACTOR, B_SLAB, B_OCEAN, BLK_TILES = 0, 4, 6, 10, 11
 SPAN = 16
 F32 = jnp.float32
 MIB = 1 << 20
@@ -40,19 +40,17 @@
     return lax.broadcasted_iota(jnp.int32, shape, 0)
 
 
-def fetch(sources, targets, sem, others):
+def fetch(sources, targets, sem):
     moves = [pltpu.make_async_copy(a, b, sem.at[i]) for i, (a, b) in enumerate(zip(sources, targets))]
-    for move in moves + others:
+    for move in moves:
         move.start()
     for move in moves:
         move.wait()
 
 
 def pack_kernel(*refs):
-    sources, (first, second, state, sea), copies, sem, join_sem = refs[:7], refs[7:11], refs[11:18], refs[18], refs[19]
-    parts = [state.at[0:9], state.at[9], state.at[10], state.at[11], sea.at[0:3], sea.at[3]]
-    joins = [pltpu.make_async_copy(a, b, join_sem.at[i]) for i, (a, b) in enumerate(zip(sources, parts))]
-    fetch(sources, copies, sem, joins)
+    sources, (first, second), copies, sem = refs[:7], refs[7:9], refs[9:16], refs[16]
+    fetch(sources, copies, sem)
     widths = copies[6]
     slab, buo, lam, mu, ocean, depth = copies[:6]
     odd = lax.rem(lax.axis_index("sec"), 2)
@@ -77,8 +75,6 @@
             for k in range(4):
                 cols = slice(k * LANES, (k + 1) * LANES)
                 out[OCEAN + 4 * f + k] = ocean[f, rows, cols] if f < 3 else depth[rows, cols]
-    for join in joins:
-        join.wait()
 
 
 def sides(first, second):
@@ -115,27 +111,29 @@
         strips[f, t, 6:8, :] = jnp.where(odd == 0, a, c)
 
 
-def halo_spot(f, r, tlane):
-    i = f * 3 + r
+def halo_spot(i, tlane):
     at = 2 * (i % 8)
     spot = tlane % SPAN
     return i // 8, at, (spot >= at) & (spot < at + 2)
 
 
-def carry_kernel(state_in, sea_in, state, sea, windows, halos):
-    state[...] = state_in[...]
-    sea[...] = sea_in[...]
+def carry_kernel(slab, buo, lam, mu, ocean, depth, state, sea, windows, halos):
+    state[0:9] = slab[...]
+    for i, x in enumerate((buo, lam, mu)):
+        state[9 + i] = x[...]
+    sea[0:3] = ocean[...]
+    sea[3] = depth[...]
     tlane = lane_iota((8, LANES))
-    heads = [jnp.zeros((8, LANES), F32) for _ in range(5)]
-    tails = [jnp.zeros((8, LANES), F32) for _ in range(5)]
+    heads = [jnp.zeros((8, LANES), F32) for _ in range(3)]
+    tails = [jnp.zeros((8, LANES), F32) for _ in range(3)]
     for f in range(12):
         for r in range(2):
-            x = edges(state_in.at[f], r, tlane)
+            x = edges(slab.at[f] if f < 9 else (buo, lam, mu)[f - 9], r, tlane)
             windows[f, 8 * r : 8 * r + 8, :] = x
-            k, at, here = halo_spot(f, r, tlane)
+            k, at, here = halo_spot(2 * f + r, tlane)
             heads[k] = jnp.where(here, pltpu.roll(x, (at - 8) % LANES, 1), heads[k])
             tails[k] = jnp.where(here, pltpu.roll(x, (at - 6) % LANES, 1), tails[k])
-    for k in range(5):
+    for k in range(3):
         halos[0, k] = heads[k]
         halos[1, k] = tails[k]
 
@@ -245,12 +243,16 @@
     tile = (8, LANES)
     tlane = lane_iota(tile)
     fill_strips(strips, first, second)
-    heads = [halos[0, k] for k in range(5)]
-    tails = [halos[1, k] for k in range(5)]
-    for f in range(12):
-        x = edges(strips.at[f], 0, tlane)
-        last[f] = x
-        k, at, here = halo_spot(f, 2, tlane)
+    heads = [halos[0, k] for k in range(3)] + [jnp.zeros(tile, F32)]
+    tails = [halos[1, k] for k in range(3)] + [jnp.zeros(tile, F32)]
+    trow = row_iota(tile)
+    empty = (trow >= 2) & (trow < 6)
+    for p in range(6):
+        pair = [edges(strips.at[2 * p + i], 0, tlane) for i in range(2)]
+        for i in range(2):
+            last[2 * p + i] = pair[i]
+        x = jnp.where(empty, pltpu.roll(pair[1], 4, 0), pair[0])
+        k, at, here = halo_spot(24 + p, tlane)
         heads[k] = jnp.where(here, pltpu.roll(x, (at - 8) % LANES, 1), heads[k])
         tails[k] = jnp.where(here, pltpu.roll(x, (at - 6) % LANES, 1), tails[k])
     head, tail = jnp.zeros(tile, F32), jnp.zeros(tile, F32)
@@ -278,7 +280,7 @@
             send[d, B_UP + r] = rise[8 * r : 8 * r + 8]
         for r in range(2):
             send[d, B_FACTOR + r] = packed[8 * r : 8 * r + 8]
-        for i in range(6):
+        for i in range(5):
             send[d, B_SLAB + i] = jnp.where(d < me, heads[i], tails[i])
 
 
@@ -426,45 +428,6 @@
     moves = filter_moves(far, held, sem)
     for move in [enter] + moves:
         move.start()
-
-    spot = tlane % SPAN
-    north = lambda v: pltpu.roll(v, 1, 0)
-    south = lambda v: pltpu.roll(v, 23, 0)
-    west = lambda v: pltpu.roll(v, 1, 1)
-    east = lambda v: pltpu.roll(v, LANES - 1, 1)
-    wlane = lane_iota((24, LANES))
-    above = lambda v: jnp.where(wlane < SPAN, 0.0, pltpu.roll(v, SPAN, 1))
-    below = lambda v: jnp.where(wlane >= LANES - SPAN, 0.0, pltpu.roll(v, LANES - SPAN, 1))
-    results = []
-    for side in range(2):
-        other, on, home = ((before, west_on, 6), (after, east_on, 8))[side]
-        here = (spot >= home) & (spot < home + 2)
-        state = []
-        for f in range(12):
-            parts = []
-            for r in range(3):
-                i = f * 3 + r
-                x = pltpu.roll(recv[other, B_SLAB + i // 8], (home - 2 * (i % 8)) % LANES, 1)
-                own = windows[f, 8 * r : 8 * r + 8, :] if r < 2 else last[f]
-                parts.append(jnp.where(here, jnp.where(on, x, 0.0), own))
-            state.append(jnp.concatenate(parts, axis=0))
-        v, s = state[0:3], state[3:9]
-        qb, la, m = Q * state[BUO], Q * state[LAM], Q * state[MU]
-        for step in range(2):
-            v = velocities(v, s, qb, below(s[0]), (above(s[5]), above(s[4])), north, south, west, east)
-            s = stresses(s, v, la, m, (below(v[1]), below(v[2])), above(v[0]), north, south, west, east)
-        results.append(v + s)
-    enter.wait()
-    edge = (tlane < 2) | (tlane >= LANES - 2)
-    for f in range(9):
-        for r in range(2):
-            rows = slice(8 * r, 8 * r + 8)
-            both = jnp.where(spot >= 8, results[0][f][rows], results[1][f][rows])
-            for t in range(DEPTH):
-                moved = pltpu.roll(both, (2 * LANES - SPAN * t - 8) % LANES, 1)
-                slab[f, t, rows, :] = jnp.where(edge, moved, plain[f, t, rows, :])
-    leave = pltpu.make_async_copy(slab, slab_out, sem.at[4])
-    leave.start()
 
     rises = [jnp.concatenate([recv[j, B_UP + r] for r in range(4)], axis=0) for j in range(n_blk)]
     factors = []
@@ -490,7 +453,7 @@
     def dot(a, c):
         return lax.dot_general(a, c, (((1,), (1,)), ((), ())), preferred_element_type=F32)
 
-    for move in moves:
+    for move in moves + [enter]:
         move.wait()
     source = dot(near[...], jnp.concatenate(upper[1], axis=1))
     source = source + dot(held[...], jnp.concatenate(upper[0] + upper[2], axis=1))
@@ -499,6 +462,46 @@
     flat[5 * LANES - 8 : 5 * LANES, 0:64] = source[COLS + 8 : COLS + 16]
     turned = [flat[k * LANES : (k + 1) * LANES, :].T for k in range(5)]
     source = jnp.concatenate([x[0:32] + x[32:64] for x in turned], axis=1)
+
+    spot = tlane % SPAN
+    north = lambda v: pltpu.roll(v, 1, 0)
+    south = lambda v: pltpu.roll(v, 23, 0)
+    west = lambda v: pltpu.roll(v, 1, 1)
+    east = lambda v: pltpu.roll(v, LANES - 1, 1)
+    wlane = lane_iota((24, LANES))
+    above = lambda v: jnp.where(wlane < SPAN, 0.0, pltpu.roll(v, SPAN, 1))
+    below = lambda v: jnp.where(wlane >= LANES - SPAN, 0.0, pltpu.roll(v, LANES - SPAN, 1))
+    results = []
+    for side in range(2):
+        other, on, home = ((before, west_on, 6), (after, east_on, 8))[side]
+        here = (spot >= home) & (spot < home + 2)
+        state = []
+        for f in range(12):
+            parts = []
+            for r in range(3):
+                i = 2 * f + r if r < 2 else 24 + f // 2
+                x = pltpu.roll(recv[other, B_SLAB + i // 8], (home - 2 * (i % 8)) % LANES, 1)
+                if r == 2 and f % 2:
+                    x = pltpu.roll(x, 4, 0)
+                own = windows[f, 8 * r : 8 * r + 8, :] if r < 2 else last[f]
+                parts.append(jnp.where(here, jnp.where(on, x, 0.0), own))
+            state.append(jnp.concatenate(parts, axis=0))
+        v, s = state[0:3], state[3:9]
+        qb, la, m = Q * state[BUO], Q * state[LAM], Q * state[MU]
+        for step in range(2):
+            v = velocities(v, s, qb, below(s[0]), (above(s[5]), above(s[4])), north, south, west, east)
+            s = stresses(s, v, la, m, (below(v[1]), below(v[2])), above(v[0]), north, south, west, east)
+        results.append(v + s)
+    edge = (tlane < 2) | (tlane >= LANES - 2)
+    for f in range(9):
+        for r in range(2):
+            rows = slice(8 * r, 8 * r + 8)
+            both = jnp.where(spot >= 8, results[0][f][rows], results[1][f][rows])
+            for t in range(DEPTH):
+                moved = pltpu.roll(both, (2 * LANES - SPAN * t - 8) % LANES, 1)
+                slab[f, t, rows, :] = jnp.where(edge, moved, plain[f, t, rows, :])
+    leave = pltpu.make_async_copy(slab, slab_out, sem.at[4])
+    leave.start()
 
     ring = (32, 5 * LANES)
     fields = []
@@ -561,15 +564,13 @@
     message = arr((SEC_TILES, 8, LANES), F32)
     sources = (*own, band_widths)
     state, sea = arr((12, DEPTH, R, LANES), F32), arr((4, R, COLS), F32)
-    first, second, state, sea = call(
+    first, second = call(
         pack_kernel,
-        [message, message, state, sea],
+        [message, message],
         10**6,
         *sources,
         far=7,
-        out_far=(2, 3),
-        scratch=[pltpu.VMEM(a.shape, a.dtype) for a in sources]
-        + [pltpu.SemaphoreType.DMA((7,)), pltpu.SemaphoreType.DMA((6,))],
+        scratch=[pltpu.VMEM(a.shape, a.dtype) for a in sources] + [pltpu.SemaphoreType.DMA((7,))],
     )
     first = swap(first, "sec", 1)
     second = swap(second, "sec", 0)
@@ -579,11 +580,10 @@
             arr(state.shape, F32),
             arr(sea.shape, F32),
             arr((12, R, LANES), F32),
-            arr((2, 5, 8, LANES), F32),
+            arr((2, 3, 8, LANES), F32),
         ],
         10**7,
-        state,
-        sea,
+        *own,
         limit=MIB * 12,
     )
     strips = pltpu.VMEM((12, DEPTH, 8, LANES), F32)

time: 83.5 us -> 54.9 us (0.66)
  Pallas kernels: 44.4 us -> 16.2 us
  waiting for transfers between devices: 8.96 us -> 5.09 us
  local copies, waits for them, and re-layouts: 3.37 us -> 6.57 us
    pallas_call x5, Pallas kernels: 44.4 us -> 16.2 us  [call(): pl.pallas_call(kernel, out_shape=out_shape, in_specs=[anywhere] * far + [...]
    unnamed x6 -> x14, local copies, waits for them, and re-layouts: 2.68 us -> 5.88 us
    ppermute x2, waiting for transfers between devices: 3.61 us -> 0.43 us  [swap(): return lax.ppermute(x, axis, pairs)]
  transfers between devices with their start and end apart: 3 -> 3, of which waited for: 3 -> 2; matrix products, arithmetic and copies ran while one was open for 1% -> 1% of each run, Pallas kernels for 9% -> 13%
where the time goes in v5:
time: 54.9 us; the launch traced here: 54.3 us
  starting transfers between devices  25.8 us (47%)
  Pallas kernels  16.2 us (30%)
  local copies, waits for them, and re-layouts  6.57 us (12%)
  waiting for transfers between devices  5.09 us (9%)
  between operations  0.68 us (1%)
    pallas_call x5, Pallas kernels, call(): pl.pallas_call(kernel, out_shape=out_shape, in_specs=[anywhere] * far + [...  16.2 us
    all_to_all x1, starting transfers between devices, on_device(): recv = lax.all_to_all(send, 'blk', 0, 0, tiled=True)  13.1 us
    ppermute x2, starting transfers between devices, swap(): return lax.ppermute(x, axis, pairs)  12.7 us
    unnamed x14, local copies, waits for them, and re-layouts  5.88 us
    all_to_all x1, waiting for transfers between devices, on_device(): recv = lax.all_to_all(send, 'blk', 0, 0, tiled=True)  4.67 us
  transfers between devices with their start and end apart: 3, of which 2 were waited for; matrix products, arithmetic and copies ran while one was open for 1% of the time, Pallas kernels for 13%

profile of v5, /device:TPU:7, one launch (start us, length us, event | category | flops | bytes accessed | tf_op | source)
XLA Modules:
  0.0 54.3 jit_solution(8657070872686545545)
XLA Ops:
  0.6 2.1 %shard_map.96 = (f32[60,8,128]{2,1,0:T(8,128)}, f32[60,8,128]{2,1,0:T(8,128)}) custom-call(f32[9,8,16,128]{3,2,1,0:T(8,128)} %refs_0_.1, f32[8,16,128]{2,1,0:T(8,128)} %refs_1_.1, f32[8,16,128]{2,1,0:T(8,128)} %refs_2_.1, f32[8,16,128]{2,1,0:T(8,128)} %refs_3_.1, f32[3,16,512]{2,1,0:T(8,128)} %refs_4_.1, f32[16,512]{1,0:T(8,128)} %refs_5_.1, s32[1,6]{1,0:T(1,128)} %widths.1), custom_call_target="tpu_custom_call" | custom-call | flops 1000000 | bytes 1409048 | tf_op jit(solution)/shard_map/pallas_call | solution.py:541
  2.7 10.8 %collective-permute-start = (f32[60,8,128]{2,1,0:T(8,128)}, f32[60,8,128]{2,1,0:T(8,128)S(1)}, u32[]{:S(2)}, u32[]{:S(2)}) collective-permute-start(f32[60,8,128]{2,1,0:T(8,128)} %get-tuple-element.15), channel_id=1, source_target_pairs={{6,12},{12,6},{18,24},{24,18},{30,36},{36,30},{42,48},{48,42},{54,... | collective-permute-start | bytes 737288 | tf_op jit(solution)/shard_map/ppermute | solution.py:556
  13.5 1.9 %collective-permute-start.1 = (f32[60,8,128]{2,1,0:T(8,128)}, f32[60,8,128]{2,1,0:T(8,128)S(1)}, u32[]{:S(2)}, u32[]{:S(2)}) collective-permute-start(f32[60,8,128]{2,1,0:T(8,128)} %get-tuple-element.16), channel_id=1, source_target_pairs={{0,6},{6,0},{12,18},{18,12},{24,30},{30,24},{36,42},{42,36},{48,54... | collective-permute-start | bytes 737288 | tf_op jit(solution)/shard_map/ppermute | solution.py:556
  15.4 0.0 copy-start
  15.4 1.1 %copy-done = f32[9,8,16,128]{3,2,1,0:T(8,128)S(1)} copy-done((f32[9,8,16,128]{3,2,1,0:T(8,128)S(1)}, f32[9,8,16,128]{3,2,1,0:T(8,128)}, u32[]{:S(2)}) %copy-start) | copy-done | bytes 589848
  16.5 0.0 copy-start.1
  16.5 0.9 %copy-done.1 = f32[3,16,512]{2,1,0:T(8,128)S(1)} copy-done((f32[3,16,512]{2,1,0:T(8,128)S(1)}, f32[3,16,512]{2,1,0:T(8,128)}, u32[]{:S(2)}) %copy-start.1) | copy-done | bytes 98328
  17.4 0.0 copy-start.2
  17.4 0.8 %copy-done.2 = f32[8,16,128]{2,1,0:T(8,128)S(1)} copy-done((f32[8,16,128]{2,1,0:T(8,128)S(1)}, f32[8,16,128]{2,1,0:T(8,128)}, u32[]{:S(2)}) %copy-start.2) | copy-done | bytes 65560
  18.2 0.0 copy-start.3
  18.2 0.8 %copy-done.3 = f32[8,16,128]{2,1,0:T(8,128)S(1)} copy-done((f32[8,16,128]{2,1,0:T(8,128)S(1)}, f32[8,16,128]{2,1,0:T(8,128)}, u32[]{:S(2)}) %copy-start.3) | copy-done | bytes 65560
  19.1 0.0 copy-start.4
  19.1 0.8 %copy-done.4 = f32[8,16,128]{2,1,0:T(8,128)S(1)} copy-done((f32[8,16,128]{2,1,0:T(8,128)S(1)}, f32[8,16,128]{2,1,0:T(8,128)}, u32[]{:S(2)}) %copy-start.4) | copy-done | bytes 65560
  19.9 0.0 copy-start.5
  19.9 0.8 %copy-done.5 = f32[16,512]{1,0:T(8,128)S(1)} copy-done((f32[16,512]{1,0:T(8,128)S(1)}, f32[16,512]{1,0:T(8,128)}, u32[]{:S(2)}) %copy-start.5) | copy-done | bytes 32792
  20.7 1.0 %shard_map.95 = (f32[12,8,16,128]{3,2,1,0:T(8,128)S(1)}, f32[4,16,512]{2,1,0:T(8,128)S(1)}, f32[12,16,128]{2,1,0:T(8,128)S(1)}, f32[2,3,8,128]{3,2,1,0:T(8,128)S(1)}) custom-call(f32[9,8,16,128]{3,2,1,0:T(8,128)S(1)} %copy-done, f32[8,16,128]{2,1,0:T(8,128)S(1)} %copy-done.2, f32[8,16,128]{2,1,0:T(8,128)S(1)} %copy-done.3, f32[8,16,128]{2,1,0:T(8,128)S(1)} %copy-done.4, ...), custom_call_target="tpu_custom_call" | custom-call | flops 10000000 | bytes 1957888 | tf_op jit(solution)/shard_map/pallas_call | solution.py:541
  21.7 0.0 collective-permute-done.first
  21.7 0.4 collective-permute-done.1.second
  22.1 1.5 %shard_map.98 = (f32[6,11,8,128]{3,2,1,0:T(8,128)}, f32[12,8,128]{2,1,0:T(8,128)S(1)}) custom-call(f32[12,8,16,128]{3,2,1,0:T(8,128)S(1)} %get-tuple-element.13.state, f32[4,16,512]{2,1,0:T(8,128)S(1)} %get-tuple-element.14.sea, f32[2,3,8,128]{3,2,1,0:T(8,128)S(1)} %get-tuple-element.21.halos, f32[60,8,128]{2,1,0:T(8,128)S(1)} %collective-permute-done.first, ...), custom_call_target="tpu_custom_call" | custom-call | flops 10000000 | bytes 1753088 | tf_op jit(solution)/shard_map/pallas_call | solution.py:541
  23.6 13.1 %all-to-all-start = ((f32[6,11,8,128]{3,2,1,0:T(8,128)}), f32[6,11,8,128]{3,2,1,0:T(8,128)S(1)}, u32[]{:S(2)}, u32[]{:S(2)}) async-start(f32[6,11,8,128]{3,2,1,0:T(8,128)} %get-tuple-element.23), calls=%async_computation | async-start | bytes 540672 | tf_op jit(solution)/shard_map/all_to_all | solution.py:602
  36.7 0.7 %reshape.7.face = s32[1,768]{1,0:T(1,128)S(1)} reshape(s32[768]{0:T(1024)} %param.12) | data formatting | bytes 6144 | tf_op jit(solution)/shard_map/reshape | solution.py:615
  37.4 0.0 copy-start.6
  37.4 0.7 %copy-done.6 = s32[1,6]{1,0:T(1,128)S(1)} copy-done((s32[1,6]{1,0:T(1,128)S(1)}, s32[1,6]{1,0:T(1,128)}, u32[]{:S(2)}) %copy-start.6) | copy-done | bytes 48
  38.0 6.3 %shard_map.97 = (f32[324,8,16,128]{3,2,1,0:T(8,128)}, bf16[528,1536]{1,0:T(8,128)(2,1)S(1)}, bf16[3168,3072]{1,0:T(8,128)(2,1)}) custom-call(f32[12,8,16,128]{3,2,1,0:T(8,128)S(1)} %get-tuple-element.13.state, f32[4,16,512]{2,1,0:T(8,128)S(1)} %get-tuple-element.14.sea, f32[60,8,128]{2,1,0:T(8,128)S(1)} %collective-permute-done.first, ...), custom_call_target="tpu_custom_call" | custom-call | flops 100000000 | bytes 43731992 | tf_op jit(solution)/shard_map/pallas_call | solution.py:541
  44.3 4.7 %all-to-all-done.recv = f32[6,11,8,128]{3,2,1,0:T(8,128)S(1)} async-done(((f32[6,11,8,128]{3,2,1,0:T(8,128)}), f32[6,11,8,128]{3,2,1,0:T(8,128)S(1)}, u32[]{:S(2)}, u32[]{:S(2)}) %all-to-all-start) | async-done | bytes 270368 | tf_op jit(solution)/shard_map/all_to_all | solution.py:602
  49.0 5.3 %shard_map.99 = (f32[9,8,16,128]{3,2,1,0:T(8,128)}, f32[3,16,512]{2,1,0:T(8,128)}) custom-call(bf16[3168,3072]{1,0:T(8,128)(2,1)} %get-tuple-element.17.far, f32[324,8,16,128]{3,2,1,0:T(8,128)} %get-tuple-element.18.plain_in, bf16[528,1536]{1,0:T(8,128)(2,1)S(1)} %get-tuple-element.19.near, f32[12,16,128]{2,1,0:T(8,128)S(1)} %get-tuple-element.20.windows, ...), custom_call_target="tpu_custom_call" | custom-call | flops 100000000 | bytes 43425792 | tf_op jit(solution)/shard_map/pallas_call | solution.py:541
Async XLA Ops:
  2.7 19.0 %collective-permute-start = (f32[60,8,128]{2,1,0:T(8,128)}, f32[60,8,128]{2,1,0:T(8,128)S(1)}, u32[]{:S(2)}, u32[]{:S(2)}) collective-permute-start(f32[60,8,128]{2,1,0:T(8,128)} %get-tuple-element.15), channel_id=1, source_target_pairs={{6,12},{12,6},{18,24},{24,18},{30,36},{36,30},{42,48},{48,42},{54,... | collective-permute-start | bytes 737288 | tf_op jit(solution)/shard_map/ppermute | solution.py:556
  13.5 8.6 %collective-permute-start.1 = (f32[60,8,128]{2,1,0:T(8,128)}, f32[60,8,128]{2,1,0:T(8,128)S(1)}, u32[]{:S(2)}, u32[]{:S(2)}) collective-permute-start(f32[60,8,128]{2,1,0:T(8,128)} %get-tuple-element.16), channel_id=1, source_target_pairs={{0,6},{6,0},{12,18},{18,12},{24,30},{30,24},{36,42},{42,36},{48,54... | collective-permute-start | bytes 737288 | tf_op jit(solution)/shard_map/ppermute | solution.py:556
  15.4 1.1 %copy-start = (f32[9,8,16,128]{3,2,1,0:T(8,128)S(1)}, f32[9,8,16,128]{3,2,1,0:T(8,128)}, u32[]{:S(2)}) copy-start(f32[9,8,16,128]{3,2,1,0:T(8,128)} %refs_0_.1) | copy-start | bytes 1769476
  16.5 0.9 %copy-start.1 = (f32[3,16,512]{2,1,0:T(8,128)S(1)}, f32[3,16,512]{2,1,0:T(8,128)}, u32[]{:S(2)}) copy-start(f32[3,16,512]{2,1,0:T(8,128)} %refs_4_.1) | copy-start | bytes 294916
  17.4 0.8 %copy-start.2 = (f32[8,16,128]{2,1,0:T(8,128)S(1)}, f32[8,16,128]{2,1,0:T(8,128)}, u32[]{:S(2)}) copy-start(f32[8,16,128]{2,1,0:T(8,128)} %refs_1_.1) | copy-start | bytes 196612
  18.2 0.8 %copy-start.3 = (f32[8,16,128]{2,1,0:T(8,128)S(1)}, f32[8,16,128]{2,1,0:T(8,128)}, u32[]{:S(2)}) copy-start(f32[8,16,128]{2,1,0:T(8,128)} %refs_2_.1) | copy-start | bytes 196612
  19.1 0.8 %copy-start.4 = (f32[8,16,128]{2,1,0:T(8,128)S(1)}, f32[8,16,128]{2,1,0:T(8,128)}, u32[]{:S(2)}) copy-start(f32[8,16,128]{2,1,0:T(8,128)} %refs_3_.1) | copy-start | bytes 196612
  19.9 0.8 %copy-start.5 = (f32[16,512]{1,0:T(8,128)S(1)}, f32[16,512]{1,0:T(8,128)}, u32[]{:S(2)}) copy-start(f32[16,512]{1,0:T(8,128)} %refs_5_.1) | copy-start | bytes 98308
  23.6 25.4 %all-to-all-start = ((f32[6,11,8,128]{3,2,1,0:T(8,128)}), f32[6,11,8,128]{3,2,1,0:T(8,128)S(1)}, u32[]{:S(2)}, u32[]{:S(2)}) async-start(f32[6,11,8,128]{3,2,1,0:T(8,128)} %get-tuple-element.23), calls=%async_computation | async-start | bytes 540672 | tf_op jit(solution)/shard_map/all_to_all | solution.py:602
  37.4 0.7 %copy-start.6 = (s32[1,6]{1,0:T(1,128)S(1)}, s32[1,6]{1,0:T(1,128)}, u32[]{:S(2)}) copy-start(s32[1,6]{1,0:T(1,128)} %widths.1) | copy-start | bytes 76

commit v6 on v5

--- a/solution.py
+++ b/solution.py
@@ -425,7 +425,7 @@
     tlane = lane_iota(tile)
 
     enter = pltpu.make_async_copy(plain_in.at[0:13], plain, sem.at[5])
-    moves = filter_moves(far, held, sem)
+    moves = [pltpu.make_async_copy(far.at[0 : COLS + 16, :], held, sem.at[0])]
     for move in [enter] + moves:
         move.start()
 

time: 54.9 us -> 55 us (level)
  no operation moved by 1% of the time
where the time goes in v6:
time: 55 us; the launch traced here: 54.4 us
  starting transfers between devices  25.8 us (47%)
  Pallas kernels  16.2 us (29%)
  local copies, waits for them, and re-layouts  6.57 us (12%)
  waiting for transfers between devices  5.09 us (9%)
  between operations  0.68 us (1%)
    pallas_call x5, Pallas kernels, call(): pl.pallas_call(kernel, out_shape=out_shape, in_specs=[anywhere] * far + [...  16.2 us
    all_to_all x1, starting transfers between devices, on_device(): recv = lax.all_to_all(send, 'blk', 0, 0, tiled=True)  13.1 us
    ppermute x2, starting transfers between devices, swap(): return lax.ppermute(x, axis, pairs)  12.7 us
    unnamed x14, local copies, waits for them, and re-layouts  5.88 us
    all_to_all x1, waiting for transfers between devices, on_device(): recv = lax.all_to_all(send, 'blk', 0, 0, tiled=True)  4.67 us
  transfers between devices with their start and end apart: 3, of which 2 were waited for; matrix products, arithmetic and copies ran while one was open for 1% of the time, Pallas kernels for 13%

profile of v6, /device:TPU:7, one launch (start us, length us, event | category | flops | bytes accessed | tf_op | source)
XLA Modules:
  0.0 54.4 jit_solution(11833030490661358397)
XLA Ops:
  0.6 2.1 %shard_map.96 = (f32[60,8,128]{2,1,0:T(8,128)}, f32[60,8,128]{2,1,0:T(8,128)}) custom-call(f32[9,8,16,128]{3,2,1,0:T(8,128)} %refs_0_.1, f32[8,16,128]{2,1,0:T(8,128)} %refs_1_.1, f32[8,16,128]{2,1,0:T(8,128)} %refs_2_.1, f32[8,16,128]{2,1,0:T(8,128)} %refs_3_.1, f32[3,16,512]{2,1,0:T(8,128)} %refs_4_.1, f32[16,512]{1,0:T(8,128)} %refs_5_.1, s32[1,6]{1,0:T(1,128)} %widths.1), custom_call_target="tpu_custom_call" | custom-call | flops 1000000 | bytes 1409048 | tf_op jit(solution)/shard_map/pallas_call | solution.py:541
  2.7 10.8 %collective-permute-start = (f32[60,8,128]{2,1,0:T(8,128)}, f32[60,8,128]{2,1,0:T(8,128)S(1)}, u32[]{:S(2)}, u32[]{:S(2)}) collective-permute-start(f32[60,8,128]{2,1,0:T(8,128)} %get-tuple-element.15), channel_id=1, source_target_pairs={{6,12},{12,6},{18,24},{24,18},{30,36},{36,30},{42,48},{48,42},{54,... | collective-permute-start | bytes 737288 | tf_op jit(solution)/shard_map/ppermute | solution.py:556
  13.5 1.9 %collective-permute-start.1 = (f32[60,8,128]{2,1,0:T(8,128)}, f32[60,8,128]{2,1,0:T(8,128)S(1)}, u32[]{:S(2)}, u32[]{:S(2)}) collective-permute-start(f32[60,8,128]{2,1,0:T(8,128)} %get-tuple-element.16), channel_id=1, source_target_pairs={{0,6},{6,0},{12,18},{18,12},{24,30},{30,24},{36,42},{42,36},{48,54... | collective-permute-start | bytes 737288 | tf_op jit(solution)/shard_map/ppermute | solution.py:556
  15.4 0.0 copy-start
  15.4 1.1 %copy-done = f32[9,8,16,128]{3,2,1,0:T(8,128)S(1)} copy-done((f32[9,8,16,128]{3,2,1,0:T(8,128)S(1)}, f32[9,8,16,128]{3,2,1,0:T(8,128)}, u32[]{:S(2)}) %copy-start) | copy-done | bytes 589848
  16.5 0.0 copy-start.1
  16.5 0.9 %copy-done.1 = f32[3,16,512]{2,1,0:T(8,128)S(1)} copy-done((f32[3,16,512]{2,1,0:T(8,128)S(1)}, f32[3,16,512]{2,1,0:T(8,128)}, u32[]{:S(2)}) %copy-start.1) | copy-done | bytes 98328
  17.4 0.0 copy-start.2
  17.4 0.8 %copy-done.2 = f32[8,16,128]{2,1,0:T(8,128)S(1)} copy-done((f32[8,16,128]{2,1,0:T(8,128)S(1)}, f32[8,16,128]{2,1,0:T(8,128)}, u32[]{:S(2)}) %copy-start.2) | copy-done | bytes 65560
  18.2 0.0 copy-start.3
  18.2 0.8 %copy-done.3 = f32[8,16,128]{2,1,0:T(8,128)S(1)} copy-done((f32[8,16,128]{2,1,0:T(8,128)S(1)}, f32[8,16,128]{2,1,0:T(8,128)}, u32[]{:S(2)}) %copy-start.3) | copy-done | bytes 65560
  19.1 0.0 copy-start.4
  19.1 0.8 %copy-done.4 = f32[8,16,128]{2,1,0:T(8,128)S(1)} copy-done((f32[8,16,128]{2,1,0:T(8,128)S(1)}, f32[8,16,128]{2,1,0:T(8,128)}, u32[]{:S(2)}) %copy-start.4) | copy-done | bytes 65560
  19.9 0.0 copy-start.5
  19.9 0.8 %copy-done.5 = f32[16,512]{1,0:T(8,128)S(1)} copy-done((f32[16,512]{1,0:T(8,128)S(1)}, f32[16,512]{1,0:T(8,128)}, u32[]{:S(2)}) %copy-start.5) | copy-done | bytes 32792
  20.7 1.0 %shard_map.95 = (f32[12,8,16,128]{3,2,1,0:T(8,128)S(1)}, f32[4,16,512]{2,1,0:T(8,128)S(1)}, f32[12,16,128]{2,1,0:T(8,128)S(1)}, f32[2,3,8,128]{3,2,1,0:T(8,128)S(1)}) custom-call(f32[9,8,16,128]{3,2,1,0:T(8,128)S(1)} %copy-done, f32[8,16,128]{2,1,0:T(8,128)S(1)} %copy-done.2, f32[8,16,128]{2,1,0:T(8,128)S(1)} %copy-done.3, f32[8,16,128]{2,1,0:T(8,128)S(1)} %copy-done.4, ...), custom_call_target="tpu_custom_call" | custom-call | flops 10000000 | bytes 1957888 | tf_op jit(solution)/shard_map/pallas_call | solution.py:541
  21.7 0.0 collective-permute-done.first
  21.7 0.4 collective-permute-done.1.second
  22.1 1.5 %shard_map.98 = (f32[6,11,8,128]{3,2,1,0:T(8,128)}, f32[12,8,128]{2,1,0:T(8,128)S(1)}) custom-call(f32[12,8,16,128]{3,2,1,0:T(8,128)S(1)} %get-tuple-element.13.state, f32[4,16,512]{2,1,0:T(8,128)S(1)} %get-tuple-element.14.sea, f32[2,3,8,128]{3,2,1,0:T(8,128)S(1)} %get-tuple-element.21.halos, f32[60,8,128]{2,1,0:T(8,128)S(1)} %collective-permute-done.first, ...), custom_call_target="tpu_custom_call" | custom-call | flops 10000000 | bytes 1753088 | tf_op jit(solution)/shard_map/pallas_call | solution.py:541
  23.6 13.1 %all-to-all-start = ((f32[6,11,8,128]{3,2,1,0:T(8,128)}), f32[6,11,8,128]{3,2,1,0:T(8,128)S(1)}, u32[]{:S(2)}, u32[]{:S(2)}) async-start(f32[6,11,8,128]{3,2,1,0:T(8,128)} %get-tuple-element.23), calls=%async_computation | async-start | bytes 540672 | tf_op jit(solution)/shard_map/all_to_all | solution.py:602
  36.7 0.7 %reshape.7.face = s32[1,768]{1,0:T(1,128)S(1)} reshape(s32[768]{0:T(1024)} %param.12) | data formatting | bytes 6144 | tf_op jit(solution)/shard_map/reshape | solution.py:615
  37.4 0.0 copy-start.6
  37.4 0.7 %copy-done.6 = s32[1,6]{1,0:T(1,128)S(1)} copy-done((s32[1,6]{1,0:T(1,128)S(1)}, s32[1,6]{1,0:T(1,128)}, u32[]{:S(2)}) %copy-start.6) | copy-done | bytes 48
  38.0 6.3 %shard_map.97 = (f32[324,8,16,128]{3,2,1,0:T(8,128)}, bf16[528,1536]{1,0:T(8,128)(2,1)S(1)}, bf16[3168,3072]{1,0:T(8,128)(2,1)}) custom-call(f32[12,8,16,128]{3,2,1,0:T(8,128)S(1)} %get-tuple-element.13.state, f32[4,16,512]{2,1,0:T(8,128)S(1)} %get-tuple-element.14.sea, f32[60,8,128]{2,1,0:T(8,128)S(1)} %collective-permute-done.first, ...), custom_call_target="tpu_custom_call" | custom-call | flops 100000000 | bytes 43731992 | tf_op jit(solution)/shard_map/pallas_call | solution.py:541
  44.3 4.7 %all-to-all-done.recv = f32[6,11,8,128]{3,2,1,0:T(8,128)S(1)} async-done(((f32[6,11,8,128]{3,2,1,0:T(8,128)}), f32[6,11,8,128]{3,2,1,0:T(8,128)S(1)}, u32[]{:S(2)}, u32[]{:S(2)}) %all-to-all-start) | async-done | bytes 270368 | tf_op jit(solution)/shard_map/all_to_all | solution.py:602
  49.0 5.4 %shard_map.99 = (f32[9,8,16,128]{3,2,1,0:T(8,128)}, f32[3,16,512]{2,1,0:T(8,128)}) custom-call(bf16[3168,3072]{1,0:T(8,128)(2,1)} %get-tuple-element.17.far, f32[324,8,16,128]{3,2,1,0:T(8,128)} %get-tuple-element.18.plain_in, bf16[528,1536]{1,0:T(8,128)(2,1)S(1)} %get-tuple-element.19.near, f32[12,16,128]{2,1,0:T(8,128)S(1)} %get-tuple-element.20.windows, ...), custom_call_target="tpu_custom_call" | custom-call | flops 100000000 | bytes 43425792 | tf_op jit(solution)/shard_map/pallas_call | solution.py:541
Async XLA Ops:
  2.7 19.0 %collective-permute-start = (f32[60,8,128]{2,1,0:T(8,128)}, f32[60,8,128]{2,1,0:T(8,128)S(1)}, u32[]{:S(2)}, u32[]{:S(2)}) collective-permute-start(f32[60,8,128]{2,1,0:T(8,128)} %get-tuple-element.15), channel_id=1, source_target_pairs={{6,12},{12,6},{18,24},{24,18},{30,36},{36,30},{42,48},{48,42},{54,... | collective-permute-start | bytes 737288 | tf_op jit(solution)/shard_map/ppermute | solution.py:556
  13.5 8.6 %collective-permute-start.1 = (f32[60,8,128]{2,1,0:T(8,128)}, f32[60,8,128]{2,1,0:T(8,128)S(1)}, u32[]{:S(2)}, u32[]{:S(2)}) collective-permute-start(f32[60,8,128]{2,1,0:T(8,128)} %get-tuple-element.16), channel_id=1, source_target_pairs={{0,6},{6,0},{12,18},{18,12},{24,30},{30,24},{36,42},{42,36},{48,54... | collective-permute-start | bytes 737288 | tf_op jit(solution)/shard_map/ppermute | solution.py:556
  15.4 1.1 %copy-start = (f32[9,8,16,128]{3,2,1,0:T(8,128)S(1)}, f32[9,8,16,128]{3,2,1,0:T(8,128)}, u32[]{:S(2)}) copy-start(f32[9,8,16,128]{3,2,1,0:T(8,128)} %refs_0_.1) | copy-start | bytes 1769476
  16.5 0.9 %copy-start.1 = (f32[3,16,512]{2,1,0:T(8,128)S(1)}, f32[3,16,512]{2,1,0:T(8,128)}, u32[]{:S(2)}) copy-start(f32[3,16,512]{2,1,0:T(8,128)} %refs_4_.1) | copy-start | bytes 294916
  17.4 0.8 %copy-start.2 = (f32[8,16,128]{2,1,0:T(8,128)S(1)}, f32[8,16,128]{2,1,0:T(8,128)}, u32[]{:S(2)}) copy-start(f32[8,16,128]{2,1,0:T(8,128)} %refs_1_.1) | copy-start | bytes 196612
  18.2 0.8 %copy-start.3 = (f32[8,16,128]{2,1,0:T(8,128)S(1)}, f32[8,16,128]{2,1,0:T(8,128)}, u32[]{:S(2)}) copy-start(f32[8,16,128]{2,1,0:T(8,128)} %refs_2_.1) | copy-start | bytes 196612
  19.1 0.8 %copy-start.4 = (f32[8,16,128]{2,1,0:T(8,128)S(1)}, f32[8,16,128]{2,1,0:T(8,128)}, u32[]{:S(2)}) copy-start(f32[8,16,128]{2,1,0:T(8,128)} %refs_3_.1) | copy-start | bytes 196612
  19.9 0.8 %copy-start.5 = (f32[16,512]{1,0:T(8,128)S(1)}, f32[16,512]{1,0:T(8,128)}, u32[]{:S(2)}) copy-start(f32[16,512]{1,0:T(8,128)} %refs_5_.1) | copy-start | bytes 98308
  23.6 25.4 %all-to-all-start = ((f32[6,11,8,128]{3,2,1,0:T(8,128)}), f32[6,11,8,128]{3,2,1,0:T(8,128)S(1)}, u32[]{:S(2)}, u32[]{:S(2)}) async-start(f32[6,11,8,128]{3,2,1,0:T(8,128)} %get-tuple-element.23), calls=%async_computation | async-start | bytes 540672 | tf_op jit(solution)/shard_map/all_to_all | solution.py:602
  37.4 0.7 %copy-start.6 = (s32[1,6]{1,0:T(1,128)S(1)}, s32[1,6]{1,0:T(1,128)}, u32[]{:S(2)}) copy-start(s32[1,6]{1,0:T(1,128)} %widths.1) | copy-start | bytes 76
